TPU v7x, 32 devices: a whole 2x2x4 slice. The times are simulated.
32 devices in a mesh: pair: 16 (over z, y, x), dp: 2 (over core).
Axes of the slice: x: 2, y: 2, z: 4, core: 2. Of those that a mesh axis runs over, the one named last changes fastest.
Arguments:
- features: bfloat16 [16384, 2048], P(('pair', 'dp')), may hold values from -6 to 6
- proj_weight: bfloat16 [2048, 128], replicated, may hold values from -0.01171875 to 0.01171875
- row_lse: bfloat16 [16384], P(('pair', 'dp')), may hold values from 6 to 9
- positive: int32 [16384], P(('pair', 'dp')), may hold values from 0 to 16383, as said below
Outputs:
- grad_embed: float32 [16384, 128], P(('pair', 'dp'))
- grad_weight: float32 [2048, 128], P('dp')
Inputs may be any that keep to these rules, and one draw needn't show every extreme that they name: positive[i] names the row that holds the other view of row i's cutout: positive[positive[i]] = i and positive[i] != i.
All inputs are finite; a program needn't handle non-finite values.
Results may differ from a plain program's by a relative error of at most 0.0045.
Values may be sent and summed in bfloat16 or wider, within the bound.
No kernel may reach another device: no remote copies, remote signals or barrier semaphores. Data moves between devices by JAX's collectives and lax.ppermute only.
A program may use at most 64 MiB of HBM per device.

v0:
```python
import jax
import jax.numpy as jnp
from jax import lax
from jax.sharding import PartitionSpec as P

contrastive_divisor = 0.1
epsilon = 1e-06


def from_behind(value, axis, steps):
    count = lax.axis_size(axis)
    pairs = [(source, (source + steps) % count) for source in range(count)]
    return lax.ppermute(value, axis, pairs)


def coupling_tile(embedded, own_lse, own_positive, counterpart_feature_vectors, part_lse, first_id):
    cosine_affinity_matrix = (
        lax.dot_general(
            embedded,
            counterpart_feature_vectors,
            (((1,), (1,)), ((), ())),
            preferred_element_type=jnp.float32,
        )
        / contrastive_divisor
    )
    weights = jnp.exp(cosine_affinity_matrix - own_lse.astype(jnp.float32)[:, None]) + jnp.exp(
        cosine_affinity_matrix - part_lse.astype(jnp.float32)[None, :]
    )
    identity_rows = first_id + jnp.arange(counterpart_feature_vectors.shape[0], dtype=jnp.int32)
    matched = (own_positive[:, None] == identity_rows[None, :]).astype(jnp.float32)
    return (weights - 2.0 * matched).astype(jnp.bfloat16)


def body(features, proj_weight, row_lse, positive):
    row_count = features.shape[0]
    dp_count = lax.axis_size("dp")
    pair_count = lax.axis_size("pair")
    group_rows = row_count * dp_count
    far_offset = pair_count // 4
    my_block = lax.axis_index("pair")
    projected = jnp.dot(features, proj_weight, preferred_element_type=jnp.float32)
    magnitude = jnp.sqrt(jnp.sum(projected * projected, axis=-1, keepdims=True) + epsilon)
    unit_vectors = projected / magnitude
    embedded = unit_vectors.astype(jnp.bfloat16)
    whole_embed, whole_lse = (
        lax.all_gather(embedded, "dp", axis=0, tiled=True),
        lax.all_gather(row_lse, "dp", axis=0, tiled=True),
    )
    upstream_derivative = jnp.zeros((row_count, embedded.shape[1]), jnp.float32)
    for offset in (1, far_offset):
        counterpart_feature_vectors, part_lse = from_behind(
            (whole_embed, whole_lse), "pair", offset
        )
        part_block = jnp.remainder(my_block - offset, pair_count)
        tile_coupling = coupling_tile(
            embedded,
            row_lse,
            positive,
            counterpart_feature_vectors,
            part_lse,
            part_block * group_rows,
        )
        coupling, counterpart_feature_vectors = (tile_coupling, counterpart_feature_vectors)
        upstream_derivative = upstream_derivative + jnp.dot(
            coupling, counterpart_feature_vectors, preferred_element_type=jnp.float32
        )
        returned = lax.psum_scatter(
            lax.dot_general(
                coupling, embedded, (((0,), (0,)), ((), ())), preferred_element_type=jnp.float32
            ),
            "dp",
            scatter_dimension=0,
            tiled=True,
        )
        upstream_derivative = upstream_derivative + from_behind(returned, "pair", -offset)
    derivative_pair_affinity = upstream_derivative / contrastive_divisor
    grad_embed = (
        derivative_pair_affinity
        - unit_vectors * jnp.sum(unit_vectors * derivative_pair_affinity, axis=-1, keepdims=True)
    ) / magnitude
    grad_half = grad_embed.astype(jnp.bfloat16)
    local_term = lax.dot_general(
        features, grad_half, (((0,), (0,)), ((), ())), preferred_element_type=jnp.float32
    )
    summed = lax.psum(local_term, "pair")
    grad_weight = lax.psum_scatter(summed, "dp", scatter_dimension=0, tiled=True)
    return (grad_embed, grad_weight)


def solution(mesh):
    return jax.shard_map(
        body,
        mesh=mesh,
        in_specs=(P(("pair", "dp"), None), P(), P(("pair", "dp")), P(("pair", "dp"))),
        out_specs=(P(("pair", "dp"), None), P("dp", None)),
        check_vma=False,
    )
```

profile of v0, /device:TPU:0, one launch (start us, length us, event | category | flops | bytes accessed | tf_op | source)
XLA Modules:
  0.0 204.0 jit_solution(16239086399272684663)
XLA Ops:
  7.2 1.5 copy-done
  8.8 1.9 multiply_reduce_fusion.1
  10.7 2.1 %all_gather.6 = bf16[1024,128]{0,1:T(8,128)(2,1)S(1)} all-gather(bf16[512,128]{0,1:T(8,128)(2,1)S(1)} %fusion.4), channel_id=1, replica_groups=mesh['pair'=16,'dp'=2] {'dp'}, dimensions={0}, use_global_device_ids=true | all-gather | bytes 393216 | tf_op jit(solution)/shard_map/all_gather | solution.py:46
  12.8 2.9 %collective-permute-start.3 = (bf16[1024,128]{0,1:T(8,128)(2,1)S(1)}, bf16[1024,128]{0,1:T(8,128)(2,1)S(1)}, u32[]{:S(2)}, u32[]{:S(2)}) collective-permute-start(bf16[1024,128]{0,1:T(8,128)(2,1)S(1)} %all_gather.6), channel_id=1, source_target_pairs={{0,8},{2,10},{4,12},{6,14},{8,16},{10,18},{12,20},{14,22},{16,24},... | collective-permute-start | bytes 786440 | tf_op jit(solution)/shard_map/ppermute | solution.py:13
  15.7 1.8 all-gather
  17.5 1.6 collective-permute-start.4
  19.2 1.5 collective-permute-start.1
  20.7 1.5 collective-permute-start
  22.1 2.3 %collective-permute-done.4 = bf16[1024]{0:T(1024)(128)(2,1)S(1)} collective-permute-done((bf16[1024]{0:T(1024)(128)(2,1)S(1)}, bf16[1024]{0:T(1024)(128)(2,1)S(1)}, u32[]{:S(2)}, u32[]{:S(2)}) %collective-permute-start.4) | collective-permute-done | bytes 2080 | tf_op jit(solution)/shard_map/ppermute | solution.py:13
  24.4 1.9 collective-permute-done.1
  26.4 0.5 fusion.5
  26.8 5.3 %collective-permute-done = bf16[1024,128]{0,1:T(8,128)(2,1)S(1)} collective-permute-done((bf16[1024,128]{0,1:T(8,128)(2,1)S(1)}, bf16[1024,128]{0,1:T(8,128)(2,1)S(1)}, u32[]{:S(2)}, u32[]{:S(2)}) %collective-permute-start) | collective-permute-done | bytes 262176 | tf_op jit(solution)/shard_map/ppermute | solution.py:13
  32.1 0.7 copy-done.3
  32.8 3.0 %subtract_convert_fusion.1 = (bf16[512,1024]{1,0:T(8,128)(2,1)S(1)}, bf16[512,1024]{1,0:T(8,128)(2,1)S(1)}) fusion(s32[1024]{0:T(1024)S(1)} %get-tuple-element.15, f32[1024]{0:T(1024)S(1)} %convert_element_type.26, f32[512]{0:T(512)S(1)} %convert_element_type.25, s32[512]{0:T(512)S(1)} %copy-done.5, s32[1024]{0:T(1024)S(1)} %get-tuple-element.14, ...), kind=kOutput, calls=%fused_computation.2 | convolution fusion | flops 142606336 | bytes 4608000 | tf_op jit(solution)/shard_map/dot_general | solution.py:18
  35.8 1.0 copy-done.1
  36.7 1.1 fusion.8
  37.9 0.0 reduce-scatter.4.cloned.1.call-start
  37.9 1.1 fusion.7
  39.1 4.2 %reduce-scatter.6.cloned.1.call-done = f32[512,128]{0,1:T(8,128)} async-done(((f32[1024,128]{0,1:T(8,128)}), f32[512,128]{0,1:T(8,128)}) %reduce-scatter.6.cloned.1.call-update) | async-done | bytes 262160 | tf_op jit(solution)/shard_map/reduce_scatter | solution.py:67
  43.4 3.6 %collective-permute-start.5 = (f32[512,128]{0,1:T(8,128)}, f32[512,128]{0,1:T(8,128)}, u32[]{:S(2)}, u32[]{:S(2)}) collective-permute-start(f32[512,128]{0,1:T(8,128)} %reduce-scatter.6.cloned.1.call-done), channel_id=1, source_target_pairs={{0,24},{2,26},{4,28},{6,30},{8,0},{10,2},{12,4},{14,6},{16,8},{18,... | collective-permute-start | bytes 786440 | tf_op jit(solution)/shard_map/ppermute | solution.py:13
  46.9 7.9 %reduce-scatter.4.cloned.1.call-done = f32[512,128]{0,1:T(8,128)} async-done(((f32[1024,128]{0,1:T(8,128)}), f32[512,128]{0,1:T(8,128)}) %reduce-scatter.4.cloned.1.call-update) | async-done | bytes 262160 | tf_op jit(solution)/shard_map/reduce_scatter | solution.py:67
  54.8 5.4 %collective-permute-start.2 = (f32[512,128]{0,1:T(8,128)}, f32[512,128]{0,1:T(8,128)S(1)}, u32[]{:S(2)}, u32[]{:S(2)}) collective-permute-start(f32[512,128]{0,1:T(8,128)} %reduce-scatter.4.cloned.1.call-done), channel_id=1, source_target_pairs={{0,30},{2,0},{4,2},{6,4},{8,6},{10,8},{12,10},{14,12},{16,14},{18,... | collective-permute-start | bytes 786440 | tf_op jit(solution)/shard_map/ppermute | solution.py:13
  60.2 1.7 fusion.6
  62.0 4.6 %collective-permute-done.2 = f32[512,128]{0,1:T(8,128)S(1)} collective-permute-done((f32[512,128]{0,1:T(8,128)}, f32[512,128]{0,1:T(8,128)S(1)}, u32[]{:S(2)}, u32[]{:S(2)}) %collective-permute-start.2) | collective-permute-done | bytes 262176 | tf_op jit(solution)/shard_map/ppermute | solution.py:13
  66.6 1.6 multiply_reduce_fusion
  68.1 0.1 subtract_divide_fusion
  68.2 1.4 convolution_bitcast_fusion
  69.6 0.0 all-reduce.2.cloned.1.call-start
  69.7 10.4 %reduce-scatter.8.cloned.1.call-done = f32[1024,128]{0,1:T(8,128)} async-done(((f32[2048,128]{0,1:T(8,128)}), f32[1024,128]{0,1:T(8,128)}) %reduce-scatter.8.cloned.1.call-update) | async-done | bytes 524304 | tf_op jit(solution)/shard_map/reduce_scatter | solution.py:86
  80.1 0.8 copy.16
  80.9 114.5 %all-reduce.2.cloned.1.call-done = f32[1024,128]{0,1:T(8,128)} async-done(((f32[1024,128]{0,1:T(8,128)}), f32[1024,128]{0,1:T(8,128)}) %all-reduce.2.cloned.1.call-update) | async-done | bytes 524304 | tf_op jit(solution)/shard_map/psum | solution.py:85
  195.4 2.0 copy.17
  (26 shorter events, 0.3 us)
Async XLA Ops:
  7.2 1.6 copy-start
  7.2 8.5 %copy-start.4 = (bf16[512]{0:T(512)(128)(2,1)S(1)}, bf16[512]{0:T(512)(128)(2,1)}, u32[]{:S(2)}) copy-start(bf16[512]{0:T(512)(128)(2,1)} %param.6) | copy-start | bytes 3076
  7.2 36.2 %reduce-scatter.6.cloned.1.call-start = ((), (), s32[]{:S(2)}) async-start(), calls=%async_computation.4 | async-start | bytes 786432 | tf_op jit(solution)/shard_map/reduce_scatter | solution.py:67
  10.6 22.2 %copy-start.5 = (s32[512]{0:T(512)S(1)}, s32[512]{0:T(512)}, u32[]{:S(2)}) copy-start(s32[512]{0:T(512)} %param.7) | copy-start | bytes 6148
  12.8 13.6 %collective-permute-start.3 = (bf16[1024,128]{0,1:T(8,128)(2,1)S(1)}, bf16[1024,128]{0,1:T(8,128)(2,1)S(1)}, u32[]{:S(2)}, u32[]{:S(2)}) collective-permute-start(bf16[1024,128]{0,1:T(8,128)(2,1)S(1)} %all_gather.6), channel_id=1, source_target_pairs={{0,8},{2,10},{4,12},{6,14},{8,16},{10,18},{12,20},{14,22},{16,24},... | collective-permute-start | bytes 786440 | tf_op jit(solution)/shard_map/ppermute | solution.py:13
  17.5 6.9 %collective-permute-start.4 = (bf16[1024]{0:T(1024)(128)(2,1)S(1)}, bf16[1024]{0:T(1024)(128)(2,1)S(1)}, u32[]{:S(2)}, u32[]{:S(2)}) collective-permute-start(bf16[1024]{0:T(1024)(128)(2,1)S(1)} %bitcast.20), channel_id=1, source_target_pairs={{0,8},{2,10},{4,12},{6,14},{8,16},{10,18},{12,20},{14,22},{16,24},... | collective-permute-start | bytes 6152 | tf_op jit(solution)/shard_map/ppermute | solution.py:13
  19.2 7.2 %collective-permute-start.1 = (bf16[1024]{0:T(1024)(128)(2,1)S(1)}, bf16[1024]{0:T(1024)(128)(2,1)S(1)}, u32[]{:S(2)}, u32[]{:S(2)}) collective-permute-start(bf16[1024]{0:T(1024)(128)(2,1)S(1)} %bitcast.21), channel_id=1, source_target_pairs={{0,2},{2,4},{4,6},{6,8},{8,10},{10,12},{12,14},{14,16},{16,18},{18... | collective-permute-start | bytes 6152 | tf_op jit(solution)/shard_map/ppermute | solution.py:13
  20.7 11.5 %collective-permute-start = (bf16[1024,128]{0,1:T(8,128)(2,1)S(1)}, bf16[1024,128]{0,1:T(8,128)(2,1)S(1)}, u32[]{:S(2)}, u32[]{:S(2)}) collective-permute-start(bf16[1024,128]{0,1:T(8,128)(2,1)S(1)} %all_gather.6), channel_id=1, source_target_pairs={{0,2},{2,4},{4,6},{6,8},{8,10},{10,12},{12,14},{14,16},{16,18},{18... | collective-permute-start | bytes 786440 | tf_op jit(solution)/shard_map/ppermute | solution.py:13
  26.3 5.8 %copy-start.2 = (bf16[1024,128]{0,1:T(8,128)(2,1)}, bf16[1024,128]{0,1:T(8,128)(2,1)S(1)}, u32[]{:S(2)}) copy-start(bf16[1024,128]{0,1:T(8,128)(2,1)S(1)} %collective-permute-done.3) | copy-start | bytes 786436
  32.1 0.7 copy-start.3
  35.8 1.0 copy-start.1
  37.9 17.0 %reduce-scatter.4.cloned.1.call-start = ((), (), s32[]{:S(2)}) async-start(), calls=%async_computation.3 | async-start | bytes 786432 | tf_op jit(solution)/shard_map/reduce_scatter | solution.py:67
  39.1 41.0 %reduce-scatter.8.cloned.1.call-start = ((), (), s32[]{:S(2)}) async-start(), calls=%async_computation.5 | async-start | bytes 1572864 | tf_op jit(solution)/shard_map/reduce_scatter | solution.py:86
  43.4 18.6 %collective-permute-start.5 = (f32[512,128]{0,1:T(8,128)}, f32[512,128]{0,1:T(8,128)}, u32[]{:S(2)}, u32[]{:S(2)}) collective-permute-start(f32[512,128]{0,1:T(8,128)} %reduce-scatter.6.cloned.1.call-done), channel_id=1, source_target_pairs={{0,24},{2,26},{4,28},{6,30},{8,0},{10,2},{12,4},{14,6},{16,8},{18,... | collective-permute-start | bytes 786440 | tf_op jit(solution)/shard_map/ppermute | solution.py:13
  54.8 11.7 %collective-permute-start.2 = (f32[512,128]{0,1:T(8,128)}, f32[512,128]{0,1:T(8,128)S(1)}, u32[]{:S(2)}, u32[]{:S(2)}) collective-permute-start(f32[512,128]{0,1:T(8,128)} %reduce-scatter.4.cloned.1.call-done), channel_id=1, source_target_pairs={{0,30},{2,0},{4,2},{6,4},{8,6},{10,8},{12,10},{14,12},{16,14},{18,... | collective-permute-start | bytes 786440 | tf_op jit(solution)/shard_map/ppermute | solution.py:13
  69.6 125.8 %all-reduce.2.cloned.1.call-start = ((), (), s32[]{:S(2)}) async-start(), calls=%async_computation.6 | async-start | bytes 1048576 | tf_op jit(solution)/shard_map/psum | solution.py:85
Sparse Core Ops, SparseCore 0:
  38.0 5.3 reduce-scatter.5
  45.7 9.1 reduce-scatter.3
  69.8 10.2 reduce-scatter.7
  85.9 109.4 all-reduce.1
where the time goes:
time: 204 us
  waiting for transfers between devices  151 us (74%)
  starting transfers between devices  16.6 us (8%)
  between operations  13.9 us (7%)
  matrix products  12.2 us (6%)
  local copies, waits for them, and re-layouts  6.09 us (3%)
  blocking collectives  3.86 us (2%)
    psum x1, waiting for transfers between devices, body(): summed = lax.psum(local_term, 'pair')  114 us
    ppermute x6, starting transfers between devices, from_behind(): return lax.ppermute(value, axis, pairs)  16.5 us
    ppermute x6, waiting for transfers between devices, from_behind(): return lax.ppermute(value, axis, pairs)  14.1 us
    reduce_scatter x2, waiting for transfers between devices, body(): lax.psum_scatter(lax.dot_general(coupling, embedded, (((0,), (0,)), ((),...  12.2 us
    reduce_scatter x1, waiting for transfers between devices, body(): lax.psum_scatter(summed, 'dp', scatter_dimension=0, tiled=True)  10.4 us
    unnamed x16, local copies, waits for them, and re-layouts  6.09 us
  transfers between devices with their start and end apart: 10, of which 8 were waited for; matrix products, arithmetic and copies ran while one was open for 2% of the time, Pallas kernels for 0%

commit v1 on v0

v1 whole, which is shorter than its diff:
```python
import functools
import math

import jax
import jax.numpy as jnp
from jax import lax
from jax.experimental import pallas as pl
from jax.experimental.pallas import tpu as pltpu
from jax.sharding import PartitionSpec as P

inverse_temperature = 10.0
exponent_scale = 10.0 * math.log2(math.e)
epsilon = 1e-06
lanes = 128
tail = 16
f32, bf16 = jnp.float32, jnp.bfloat16


def shifted(value, axis, steps):
    count = lax.axis_size(axis)
    return lax.ppermute(value, axis, [(s, (s + steps) % count) for s in range(count)])


def swapped(value, axis, mask):
    count = lax.axis_size(axis)
    return lax.ppermute(value, axis, [(s, s ^ mask) for s in range(count)])


def vmem_spec():
    return pl.BlockSpec(memory_space=pltpu.VMEM)


def smem_spec():
    return pl.BlockSpec(memory_space=pltpu.SMEM)


def project_kernel(features_ref, weight_ref, lse_ref, projected_ref, packed_ref):
    step = pl.program_id(0)
    chunk = features_ref.shape[0]
    rows = pl.ds(pl.multiple_of(step * chunk, chunk), chunk)
    projected = jnp.dot(features_ref[...], weight_ref[...], preferred_element_type=f32)
    magnitude = jnp.sqrt(jnp.sum(projected * projected, axis=-1, keepdims=True) + epsilon)
    projected_ref[rows, :] = projected
    packed_ref[rows, :] = (projected / magnitude).astype(bf16)

    @pl.when(step == 0)
    def _():
        count = packed_ref.shape[0] - tail
        packed_ref[pl.ds(count, tail), :] = lse_ref[...]


def project(features, weight, lse_rows):
    rows, units = features.shape
    width = weight.shape[1]
    chunk = min(128, rows)
    return pl.pallas_call(
        project_kernel,
        grid=(rows // chunk,),
        in_specs=[
            pl.BlockSpec((chunk, units), lambda i: (i, 0)),
            pl.BlockSpec((units, width), lambda i: (0, 0)),
            pl.BlockSpec((tail, lanes), lambda i: (0, 0)),
        ],
        out_specs=[
            pl.BlockSpec((rows, width), lambda i: (0, 0)),
            pl.BlockSpec((rows + tail, width), lambda i: (0, 0)),
        ],
        out_shape=[
            jax.ShapeDtypeStruct((rows, width), f32),
            jax.ShapeDtypeStruct((rows + tail, width), bf16),
        ],
        compiler_params=pltpu.CompilerParams(vmem_limit_bytes=32 * 2**20),
        name="project",
    )(features, weight, lse_rows)


def as_columns(rows):
    return jnp.concatenate(
        [
            jnp.broadcast_to(rows[k : k + 1, :], (lanes, lanes)).T
            for k in range(rows.shape[0])
        ],
        axis=0,
    )


def couple_kernel(count, first, base_ref, own_ref, positive_ref, *refs):
    parts = refs[:count]
    acc_ref = refs[count + (0 if first else 1)]
    rows = own_ref.shape[0] - tail
    chunk = min(256, rows)
    own_weight = as_columns(jnp.exp(-own_ref[pl.ds(rows, tail), :].astype(f32))[: rows // lanes, :])
    own_positive = as_columns(positive_ref[...].astype(f32))
    column = lax.broadcasted_iota(jnp.int32, (1, lanes), 1)
    for start in range(0, rows, chunk):
        own = own_ref[pl.ds(start, chunk), :]
        weight_i = own_weight[start : start + chunk, :]
        positive_i = own_positive[start : start + chunk, :]
        total = jnp.zeros((chunk, own.shape[1]), f32) if first else refs[count][pl.ds(start, chunk), :]
        for which, part in enumerate(parts):
            part_weight = jnp.exp(-part[pl.ds(rows, tail), :].astype(f32))
            for begin in range(0, rows, chunk):
                other = part[pl.ds(begin, chunk), :]
                cosine = lax.dot_general(
                    own, other, (((1,), (1,)), ((), ())), preferred_element_type=f32
                )
                pieces = []
                for lane in range(0, chunk, lanes):
                    k = (begin + lane) // lanes
                    grown = jnp.exp2(cosine[:, lane : lane + lanes] * exponent_scale)
                    ids = (column + (base_ref[which] + (begin + lane))).astype(f32)
                    value = grown * (weight_i + part_weight[k : k + 1, :])
                    value = value - jnp.where(positive_i == ids, 2.0, 0.0)
                    pieces.append(value.astype(bf16))
                coupling = jnp.concatenate(pieces, axis=1)
                total = total + jnp.dot(coupling, other, preferred_element_type=f32)
        acc_ref[pl.ds(start, chunk), :] = total


def couple(base, own, positive, parts, acc=None):
    rows = own.shape[0] - tail
    width = own.shape[1]
    count = len(parts)
    extra = [] if acc is None else [acc]
    pairs = rows * rows * count
    return pl.pallas_call(
        functools.partial(couple_kernel, count, acc is None),
        in_specs=[smem_spec()] + [vmem_spec()] * (2 + count + len(extra)),
        out_specs=vmem_spec(),
        out_shape=jax.ShapeDtypeStruct((rows, width), f32),
        compiler_params=pltpu.CompilerParams(vmem_limit_bytes=32 * 2**20),
        cost_estimate=pl.CostEstimate(
            flops=4 * pairs * width, bytes_accessed=rows * width * 4, transcendentals=pairs
        ),
        name="couple",
    )(base, own, positive, *parts, *extra)


def finish_kernel(acc_ref, projected_ref, grad_ref, half_ref):
    projected = projected_ref[...]
    magnitude = jnp.sqrt(jnp.sum(projected * projected, axis=-1, keepdims=True) + epsilon)
    unit = projected / magnitude
    upstream = acc_ref[...] * inverse_temperature
    grad = (upstream - unit * jnp.sum(unit * upstream, axis=-1, keepdims=True)) / magnitude
    grad_ref[...] = grad
    half_ref[...] = grad.astype(bf16)


def finish(acc, projected):
    return pl.pallas_call(
        finish_kernel,
        in_specs=[vmem_spec()] * 2,
        out_specs=[vmem_spec()] * 2,
        out_shape=[
            jax.ShapeDtypeStruct(projected.shape, f32),
            jax.ShapeDtypeStruct(projected.shape, bf16),
        ],
        name="finish",
    )(acc, projected)


def weight_kernel(which_ref, features_ref, half_ref, out_ref):
    out_ref[...] = lax.dot_general(
        features_ref[...], half_ref[...], (((0,), (0,)), ((), ())), preferred_element_type=f32
    ).astype(out_ref.dtype)


def weight_term(features, grad_half, share, shares, dtype):
    rows, units = features.shape
    width = grad_half.shape[1]
    size = units // shares
    chunk = min(256, size)
    per = size // chunk
    return pl.pallas_call(
        weight_kernel,
        grid_spec=pltpu.PrefetchScalarGridSpec(
            num_scalar_prefetch=1,
            grid=(per,),
            in_specs=[
                pl.BlockSpec((rows, chunk), lambda i, which: (0, which[0] * per + i)),
                pl.BlockSpec((rows, width), lambda i, which: (0, 0)),
            ],
            out_specs=pl.BlockSpec((chunk, width), lambda i, which: (i, 0)),
        ),
        out_shape=jax.ShapeDtypeStruct((size, width), dtype),
        cost_estimate=pl.CostEstimate(
            flops=2 * rows * size * width, bytes_accessed=rows * size * 2, transcendentals=0
        ),
        name="weight_term",
    )(share[None], features, grad_half)


def split_kernel(count, digit_ref, own_ref, *refs):
    parts, keep_ref, sends = refs[:count], refs[count], refs[count + 1 :]
    size = keep_ref.shape[0]
    for s in range(len(sends) + 1):
        rows = pl.ds(pl.multiple_of((digit_ref[0] ^ s) * size, size), size)
        total = own_ref[rows, :]
        for part in parts:
            total = total + part[rows, :].astype(f32)
        if s == 0:
            keep_ref[...] = total
        else:
            sends[s - 1][...] = total.astype(bf16)


def split(digit, own, parts, ways):
    size = own.shape[0] // ways
    return pl.pallas_call(
        functools.partial(split_kernel, len(parts)),
        in_specs=[smem_spec()] + [vmem_spec()] * (1 + len(parts)),
        out_specs=[vmem_spec()] * ways,
        out_shape=[jax.ShapeDtypeStruct((size, own.shape[1]), f32)]
        + [jax.ShapeDtypeStruct((size, own.shape[1]), bf16)] * (ways - 1),
        name="split",
    )(digit[None], own, *parts)


def join_kernel(digit_ref, *refs):
    parts, out_ref = refs[:-1], refs[-1]
    size = parts[0].shape[0]
    for s, part in enumerate(parts):
        rows = pl.ds(pl.multiple_of((digit_ref[0] ^ s) * size, size), size)
        out_ref[rows, :] = part[...].astype(f32)


def join(digit, parts):
    size, width = parts[0].shape
    return pl.pallas_call(
        join_kernel,
        in_specs=[smem_spec()] + [vmem_spec()] * len(parts),
        out_specs=vmem_spec(),
        out_shape=jax.ShapeDtypeStruct((size * len(parts), width), f32),
        name="join",
    )(digit[None], *parts)


def body(features, proj_weight, row_lse, positive):
    rows = features.shape[0]
    dp_count = lax.axis_size("dp")
    pair_count = lax.axis_size("pair")
    far = pair_count // 4
    group_rows = rows * dp_count
    block = lax.axis_index("pair").astype(jnp.int32)
    core = lax.axis_index("dp").astype(jnp.int32)

    lse_rows = jnp.pad(row_lse.reshape(rows // lanes, lanes), ((0, tail - rows // lanes), (0, 0)))
    positive_rows = positive.reshape(rows // lanes, lanes)
    projected, packed = project(features, proj_weight, lse_rows)

    bases, parts = [], []
    for offset in (1, -1, far, -far):
        part = shifted(packed, "pair", offset)
        first = jnp.remainder(block - offset, pair_count) * group_rows
        for mask in range(dp_count):
            parts.append(part if mask == 0 else swapped(part, "dp", mask))
            bases.append(first + (core ^ mask) * rows)
    acc = couple(jnp.stack(bases), packed, positive_rows, parts)
    grad_embed, grad_half = finish(acc, projected)

    received = [
        swapped(weight_term(features, grad_half, core ^ mask, dp_count, bf16), "dp", mask)
        for mask in range(1, dp_count)
    ]
    mine = weight_term(features, grad_half, core, dp_count, f32)

    ways = 4
    digit = block & (ways - 1)
    keep, *sends = split(digit, mine, received, ways)
    for s in range(1, ways):
        keep = keep + swapped(sends[s - 1], "pair", s).astype(f32)
    stride = ways
    while stride < pair_count:
        mine = keep.astype(bf16)
        near, middle, last = (swapped(mine, "pair", s * stride).astype(f32) for s in (1, 2, 3))
        keep = (mine.astype(f32) + near) + (middle + last)
        stride *= ways
    mine = keep.astype(bf16)
    quarters = [mine] + [swapped(mine, "pair", s) for s in range(1, ways)]
    return (grad_embed, join(digit, quarters))


def solution(mesh):
    return jax.shard_map(
        body,
        mesh=mesh,
        in_specs=(P(("pair", "dp"), None), P(), P(("pair", "dp")), P(("pair", "dp"))),
        out_specs=(P(("pair", "dp"), None), P("dp", None)),
        check_vma=False,
    )
```

time: 204 us -> 68.1 us (0.33)
  waiting for transfers between devices: 151 us -> 18.7 us
  Pallas kernels: 0 us -> 18.4 us
  between operations: 13.9 us -> 0.74 us
  matrix products: 12.2 us -> 0 us
  starting transfers between devices: 16.6 us -> 22.6 us
  blocking collectives: 3.86 us -> 0 us
    psum x1 -> x0, waiting for transfers between devices: 114 us -> none  [body(): summed = lax.psum(local_term, 'pair')]
    reduce_scatter x3 -> x0, waiting for transfers between devices: 22.5 us -> none  [the longest x2 12.2 us: body(): lax.psum_scatter(lax.dot_general(coupling, embedded, (((0,), (0,)), ((),...]
    pallas_call x0 -> x7, Pallas kernels: none -> 18.4 us  [the longest x2 7.56 us: weight_term(): pl.pallas_call(weight_kernel, grid_spec=pltpu.PrefetchScalarGridSpec(num_...]
    dot_general x8 -> x0, matrix products: 12.2 us -> none  [the longest x2 3.42 us: coupling_tile(): lax.dot_general(embedded, counterpart_feature_vectors, (((1,), (1,)), (()...]
    ppermute x6 -> x18, starting transfers between devices: 16.5 us -> 22.6 us  [the longest x14 11.8 us: swapped(): return lax.ppermute(value, axis, [(s, s ^ mask) for s in range(count)])]
    ppermute x6 -> x18, waiting for transfers between devices: 14.1 us -> 18.7 us  [the longest x14 10.3 us: swapped(): return lax.ppermute(value, axis, [(s, s ^ mask) for s in range(count)])]
    all_gather x2 -> x0, blocking collectives: 3.86 us -> none  [the longest x1 2.09 us: body(): lax.all_gather(embedded, 'dp', axis=0, tiled=True)]
    unnamed x16 -> x20, local copies, waits for them, and re-layouts: 6.09 us -> 5.48 us
  transfers between devices with their start and end apart: 10 -> 18, of which waited for: 8 -> 12; matrix products, arithmetic and copies ran while one was open for 2% -> 0% of each run, Pallas kernels for 0% -> 6%
where the time goes in v1:
time: 68.1 us; the launch traced here: 67.6 us
  starting transfers between devices  22.6 us (33%)
  waiting for transfers between devices  18.7 us (27%)
  Pallas kernels  18.4 us (27%)
  local copies, waits for them, and re-layouts  6.25 us (9%)
  other arithmetic  0.98 us (1%)
  between operations  0.74 us (1%)
    ppermute x14, starting transfers between devices, swapped(): return lax.ppermute(value, axis, [(s, s ^ mask) for s in range(count)])  11.8 us
    ppermute x4, starting transfers between devices, shifted(): lax.ppermute(value, axis, [(s, (s + steps) % count) for s in range(count)])  10.8 us
    ppermute x14, waiting for transfers between devices, swapped(): return lax.ppermute(value, axis, [(s, s ^ mask) for s in range(count)])  10.3 us
    ppermute x4, waiting for transfers between devices, shifted(): lax.ppermute(value, axis, [(s, (s + steps) % count) for s in range(count)])  8.44 us
    pallas_call x2, Pallas kernels, weight_term(): pl.pallas_call(weight_kernel, grid_spec=pltpu.PrefetchScalarGridSpec(num_...  7.56 us
    unnamed x20, local copies, waits for them, and re-layouts  5.48 us
    pallas_call x1, Pallas kernels, couple(): pl.pallas_call(functools.partial(couple_kernel, count, acc is None), in_s...  3.51 us
    pallas_call x1, Pallas kernels, finish(): pl.pallas_call(finish_kernel, in_specs=[vmem_spec()] * 2, out_specs=[vmem...  2.07 us
  transfers between devices with their start and end apart: 18, of which 12 were waited for; matrix products, arithmetic and copies ran while one was open for 0% of the time, Pallas kernels for 6%

profile of v1, /device:TPU:0, one launch (start us, length us, event | category | flops | bytes accessed | tf_op | source)
XLA Modules:
  0.0 67.6 jit_solution(1034459603663021562)
XLA Ops:
  0.6 0.7 %pad.4.lse_ref = bf16[16,128]{1,0:T(8,128)(2,1)S(1)} pad(bf16[4,128]{1,0:T(4,128)(2,1)} %bitcast.14, bf16[]{:T(256)} %constant.52.clone.1), padding=0_12x0_0 | pad | bytes 5122 | tf_op jit(solution)/shard_map/jit(_pad)/pad | solution.py:247
  1.3 1.6 %copy-done = bf16[512,2048]{1,0:T(8,128)(2,1)S(1)} copy-done((bf16[512,2048]{1,0:T(8,128)(2,1)S(1)}, bf16[512,2048]{1,0:T(8,128)(2,1)}, u32[]{:S(2)}) %copy-start) | copy-done | bytes 2097176
  2.9 1.0 %copy-done.1 = bf16[2048,128]{1,0:T(8,128)(2,1)S(1)} copy-done((bf16[2048,128]{1,0:T(8,128)(2,1)S(1)}, bf16[2048,128]{1,0:T(8,128)(2,1)}, u32[]{:S(2)}) %copy-start.1) | copy-done | bytes 524312
  4.0 1.6 %project.1 = (f32[512,128]{1,0:T(8,128)S(1)}, bf16[528,128]{1,0:T(8,128)(2,1)S(1)}) custom-call(bf16[512,2048]{1,0:T(8,128)(2,1)S(1)} %copy-done, bf16[2048,128]{1,0:T(8,128)(2,1)S(1)} %copy-done.1, bf16[16,128]{1,0:T(8,128)(2,1)S(1)} %pad.4.lse_ref), custom_call_target="tpu_custom_call" | custom-call | tf_op jit(solution)/shard_map/project/pallas_call | solution.py:56
  5.6 0.7 %copy-done.2 = f32[512,128]{1,0:T(8,128)} copy-done((f32[512,128]{1,0:T(8,128)}, f32[512,128]{1,0:T(8,128)S(1)}, u32[]{:S(2)}) %copy-start.2) | copy-done | bytes 262168
  6.3 5.1 %collective-permute-start.6 = (bf16[528,128]{1,0:T(8,128)(2,1)S(1)}, bf16[528,128]{1,0:T(8,128)(2,1)S(1)}, u32[]{:S(2)}, u32[]{:S(2)}) collective-permute-start(bf16[528,128]{1,0:T(8,128)(2,1)S(1)} %get-tuple-element.10.own_ref), channel_id=1, source_target_pairs={{0,24},{2,26},{4,28},{6,30},{8,0},{10,2},{12,4},{14,6},{16,8},{18,... | collective-permute-start | bytes 405512 | tf_op jit(solution)/shard_map/ppermute | solution.py:21
  11.3 5.7 %collective-permute-start.2 = (bf16[528,128]{1,0:T(8,128)(2,1)S(1)}, bf16[528,128]{1,0:T(8,128)(2,1)S(1)}, u32[]{:S(2)}, u32[]{:S(2)}) collective-permute-start(bf16[528,128]{1,0:T(8,128)(2,1)S(1)} %get-tuple-element.10.own_ref), channel_id=1, source_target_pairs={{0,30},{2,0},{4,2},{6,4},{8,6},{10,8},{12,10},{14,12},{16,14},{18,... | collective-permute-start | bytes 405512 | tf_op jit(solution)/shard_map/ppermute | solution.py:21
  17.0 2.6 %collective-permute-done.4.refs_4_ = bf16[528,128]{1,0:T(8,128)(2,1)S(1)} collective-permute-done((bf16[528,128]{1,0:T(8,128)(2,1)S(1)}, bf16[528,128]{1,0:T(8,128)(2,1)S(1)}, u32[]{:S(2)}, u32[]{:S(2)}) %collective-permute-start.4) | collective-permute-done | bytes 135200 | tf_op jit(solution)/shard_map/ppermute | solution.py:21
  20.1 5.5 %collective-permute-done.refs_0_ = bf16[528,128]{1,0:T(8,128)(2,1)S(1)} collective-permute-done((bf16[528,128]{1,0:T(8,128)(2,1)S(1)}, bf16[528,128]{1,0:T(8,128)(2,1)S(1)}, u32[]{:S(2)}, u32[]{:S(2)}) %collective-permute-start) | collective-permute-done | bytes 135200 | tf_op jit(solution)/shard_map/ppermute | solution.py:21
  25.7 1.2 %collective-permute-done.1.refs_1_ = bf16[528,128]{1,0:T(8,128)(2,1)S(1)} collective-permute-done((bf16[528,128]{1,0:T(8,128)(2,1)S(1)}, bf16[528,128]{1,0:T(8,128)(2,1)S(1)}, u32[]{:S(2)}, u32[]{:S(2)}) %collective-permute-start.1) | collective-permute-done | bytes 135200 | tf_op jit(solution)/shard_map/ppermute | solution.py:26
  27.0 3.5 %couple.1.acc_ref = f32[512,128]{1,0:T(8,128)S(1)} custom-call(s32[8]{0:T(128)S(1)} %stack.35.base_ref, bf16[528,128]{1,0:T(8,128)(2,1)S(1)} %get-tuple-element.10.own_ref, s32[4,128]{1,0:T(4,128)S(1)} %bitcast.13, bf16[528,128]{1,0:T(8,128)(2,1)S(1)} %collective-permute-done.refs_0_, bf16[528,128]{1,0:T(8,128)(2,1)S(1)} %collective-permute-done.1.refs_1_, ...), custom_call_target="tpu_custom_call" | custom-call | flops 1073741824 | bytes 262144 | tf_op jit(solution)/shard_map/couple/pallas_call | solution.py:126
  30.5 0.7 %copy-done.3 = f32[512,128]{1,0:T(8,128)} copy-done((f32[512,128]{1,0:T(8,128)}, f32[512,128]{1,0:T(8,128)S(1)}, u32[]{:S(2)}) %copy-start.3) | copy-done | bytes 262168
  31.2 2.1 %finish.1 = (f32[512,128]{1,0:T(8,128)}, bf16[512,128]{1,0:T(8,128)(2,1)}) custom-call(f32[512,128]{1,0:T(8,128)} %copy-done.3, f32[512,128]{1,0:T(8,128)} %copy-done.2), custom_call_target="tpu_custom_call" | custom-call | tf_op jit(solution)/shard_map/finish/pallas_call | solution.py:150
  33.3 3.8 %weight_term.3 = bf16[1024,128]{1,0:T(8,128)(2,1)} custom-call(s32[1]{0:T(128)} %bitcast.12.which_ref, bf16[512,2048]{1,0:T(8,128)(2,1)} %features_ref.5, bf16[512,128]{1,0:T(8,128)(2,1)} %get-tuple-element.13.half_ref), custom_call_target="tpu_custom_call" | custom-call | flops 134217728 | bytes 1048576 | tf_op jit(solution)/shard_map/weight_term/pallas_call | solution.py:174
  37.2 3.8 %weight_term.2.own_ref = f32[1024,128]{1,0:T(8,128)} custom-call(s32[1]{0:T(128)} %bitcast.11.which_ref, bf16[512,2048]{1,0:T(8,128)(2,1)} %features_ref.5, bf16[512,128]{1,0:T(8,128)(2,1)} %get-tuple-element.13.half_ref), custom_call_target="tpu_custom_call" | custom-call | flops 134217728 | bytes 1048576 | tf_op jit(solution)/shard_map/weight_term/pallas_call | solution.py:174
  41.0 0.7 %copy-done.5 = bf16[1024,128]{1,0:T(8,128)(2,1)} copy-done((bf16[1024,128]{1,0:T(8,128)(2,1)}, bf16[1024,128]{1,0:T(8,128)(2,1)S(1)}, u32[]{:S(2)}) %copy-start.5) | copy-done | bytes 262168
  41.7 1.9 %split.1 = (f32[256,128]{1,0:T(8,128)}, bf16[256,128]{1,0:T(8,128)(2,1)}, bf16[256,128]{1,0:T(8,128)(2,1)}, bf16[256,128]{1,0:T(8,128)(2,1)}) custom-call(s32[1]{0:T(128)} %bitcast.10.digit_ref, f32[1024,128]{1,0:T(8,128)} %weight_term.2.own_ref, bf16[1024,128]{1,0:T(8,128)(2,1)} %copy-done.5), custom_call_target="tpu_custom_call" | custom-call | tf_op jit(solution)/shard_map/split/pallas_call | solution.py:209
  43.6 3.5 %collective-permute-start.11 = (bf16[256,128]{1,0:T(8,128)(2,1)}, bf16[256,128]{1,0:T(8,128)(2,1)S(1)}, u32[]{:S(2)}, u32[]{:S(2)}) collective-permute-start(bf16[256,128]{1,0:T(8,128)(2,1)} %get-tuple-element.17), channel_id=1, source_target_pairs={{0,6},{2,4},{4,2},{6,0},{8,14},{10,12},{12,10},{14,8},{16,22},{18,... | collective-permute-start | bytes 196616 | tf_op jit(solution)/shard_map/ppermute | solution.py:26
  47.1 1.3 %collective-permute-done.9 = bf16[256,128]{1,0:T(8,128)(2,1)S(1)} collective-permute-done((bf16[256,128]{1,0:T(8,128)(2,1)}, bf16[256,128]{1,0:T(8,128)(2,1)S(1)}, u32[]{:S(2)}, u32[]{:S(2)}) %collective-permute-start.9) | collective-permute-done | bytes 65568 | tf_op jit(solution)/shard_map/ppermute | solution.py:26
  48.4 0.6 collective-permute-done.10
  49.0 0.6 collective-permute-done.11
  49.6 0.9 %add_convert_fusion.1 = bf16[256,128]{1,0:T(8,128)(2,1)S(1)} fusion(bf16[256,128]{1,0:T(8,128)(2,1)S(1)} %collective-permute-done.11, bf16[256,128]{1,0:T(8,128)(2,1)S(1)} %collective-permute-done.10, f32[256,128]{1,0:T(8,128)} %get-tuple-element.14, bf16[256,128]{1,0:T(8,128)(2,1)S(1)} %collective-permute-done.9), kind=kLoop, calls=%fused_computation.1 | loop fusion | flops 229376 | bytes 393216 | tf_op jit(solution)/shard_map/convert_element_type | solution.py:274
  50.5 1.4 %collective-permute-start.14 = (bf16[256,128]{1,0:T(8,128)(2,1)S(1)}, bf16[256,128]{1,0:T(8,128)(2,1)S(1)}, u32[]{:S(2)}, u32[]{:S(2)}) collective-permute-start(bf16[256,128]{1,0:T(8,128)(2,1)S(1)} %add_convert_fusion.1), channel_id=1, source_target_pairs={{0,24},{2,26},{4,28},{6,30},{8,16},{10,18},{12,20},{14,22},{16,8},... | collective-permute-start | bytes 196616 | tf_op jit(solution)/shard_map/ppermute | solution.py:26
  51.9 3.0 %collective-permute-start.12 = (bf16[256,128]{1,0:T(8,128)(2,1)S(1)}, bf16[256,128]{1,0:T(8,128)(2,1)S(1)}, u32[]{:S(2)}, u32[]{:S(2)}) collective-permute-start(bf16[256,128]{1,0:T(8,128)(2,1)S(1)} %add_convert_fusion.1), channel_id=1, source_target_pairs={{0,8},{2,10},{4,12},{6,14},{8,0},{10,2},{12,4},{14,6},{16,24},{18,... | collective-permute-start | bytes 196616 | tf_op jit(solution)/shard_map/ppermute | solution.py:26
  55.0 1.9 %collective-permute-done.14 = bf16[256,128]{1,0:T(8,128)(2,1)S(1)} collective-permute-done((bf16[256,128]{1,0:T(8,128)(2,1)S(1)}, bf16[256,128]{1,0:T(8,128)(2,1)S(1)}, u32[]{:S(2)}, u32[]{:S(2)}) %collective-permute-start.14) | collective-permute-done | bytes 65568 | tf_op jit(solution)/shard_map/ppermute | solution.py:26
  56.9 1.3 %collective-permute-done.13 = bf16[256,128]{1,0:T(8,128)(2,1)S(1)} collective-permute-done((bf16[256,128]{1,0:T(8,128)(2,1)S(1)}, bf16[256,128]{1,0:T(8,128)(2,1)S(1)}, u32[]{:S(2)}, u32[]{:S(2)}) %collective-permute-start.13) | collective-permute-done | bytes 65568 | tf_op jit(solution)/shard_map/ppermute | solution.py:26
  58.3 2.1 %collective-permute-start.17 = (bf16[256,128]{1,0:T(8,128)(2,1)S(1)}, bf16[256,128]{1,0:T(8,128)(2,1)S(1)}, u32[]{:S(2)}, u32[]{:S(2)}) collective-permute-start(bf16[256,128]{1,0:T(8,128)(2,1)S(1)} %add_convert_fusion.refs_0_), channel_id=1, source_target_pairs={{0,6},{2,4},{4,2},{6,0},{8,14},{10,12},{12,10},{14,8},{16,22},{18,... | collective-permute-start | bytes 196616 | tf_op jit(solution)/shard_map/ppermute | solution.py:26
  60.9 1.0 %collective-permute-start.15 = (bf16[256,128]{1,0:T(8,128)(2,1)S(1)}, bf16[256,128]{1,0:T(8,128)(2,1)S(1)}, u32[]{:S(2)}, u32[]{:S(2)}) collective-permute-start(bf16[256,128]{1,0:T(8,128)(2,1)S(1)} %add_convert_fusion.refs_0_), channel_id=1, source_target_pairs={{0,2},{2,0},{4,6},{6,4},{8,10},{10,8},{12,14},{14,12},{16,18},{18,... | collective-permute-start | bytes 196616 | tf_op jit(solution)/shard_map/ppermute | solution.py:26
  61.8 1.7 %collective-permute-done.17.refs_3_ = bf16[256,128]{1,0:T(8,128)(2,1)S(1)} collective-permute-done((bf16[256,128]{1,0:T(8,128)(2,1)S(1)}, bf16[256,128]{1,0:T(8,128)(2,1)S(1)}, u32[]{:S(2)}, u32[]{:S(2)}) %collective-permute-start.17) | collective-permute-done | bytes 65568 | tf_op jit(solution)/shard_map/ppermute | solution.py:26
  63.5 1.1 %collective-permute-done.16.refs_2_ = bf16[256,128]{1,0:T(8,128)(2,1)S(1)} collective-permute-done((bf16[256,128]{1,0:T(8,128)(2,1)S(1)}, bf16[256,128]{1,0:T(8,128)(2,1)S(1)}, u32[]{:S(2)}, u32[]{:S(2)}) %collective-permute-start.16) | collective-permute-done | bytes 65568 | tf_op jit(solution)/shard_map/ppermute | solution.py:26
  65.2 0.6 copy-done.9
  65.9 1.8 %join.1 = f32[1024,128]{1,0:T(8,128)} custom-call(s32[1]{0:T(128)} %bitcast.10.digit_ref, bf16[256,128]{1,0:T(8,128)(2,1)} %copy-done.6, bf16[256,128]{1,0:T(8,128)(2,1)} %copy-done.9, bf16[256,128]{1,0:T(8,128)(2,1)} %copy-done.8, bf16[256,128]{1,0:T(8,128)(2,1)} %copy-done.7), custom_call_target="tpu_custom_call" | custom-call | tf_op jit(solution)/shard_map/join/pallas_call | solution.py:229
  (35 shorter events, 2.0 us)
Async XLA Ops:
  0.6 26.4 %copy-start.4 = (s32[512]{0:T(512)S(1)}, s32[512]{0:T(512)}, u32[]{:S(2)}) copy-start(s32[512]{0:T(512)} %param.7) | copy-start | bytes 6148
  1.3 1.6 %copy-start = (bf16[512,2048]{1,0:T(8,128)(2,1)S(1)}, bf16[512,2048]{1,0:T(8,128)(2,1)}, u32[]{:S(2)}) copy-start(bf16[512,2048]{1,0:T(8,128)(2,1)} %features_ref.5) | copy-start | bytes 6291460
  2.9 1.0 %copy-start.1 = (bf16[2048,128]{1,0:T(8,128)(2,1)S(1)}, bf16[2048,128]{1,0:T(8,128)(2,1)}, u32[]{:S(2)}) copy-start(bf16[2048,128]{1,0:T(8,128)(2,1)} %weight_ref.1) | copy-start | bytes 1572868
  5.6 0.7 %copy-start.2 = (f32[512,128]{1,0:T(8,128)}, f32[512,128]{1,0:T(8,128)S(1)}, u32[]{:S(2)}) copy-start(f32[512,128]{1,0:T(8,128)S(1)} %get-tuple-element.11.projected_ref) | copy-start | bytes 786436
  6.3 10.8 %collective-permute-start.6 = (bf16[528,128]{1,0:T(8,128)(2,1)S(1)}, bf16[528,128]{1,0:T(8,128)(2,1)S(1)}, u32[]{:S(2)}, u32[]{:S(2)}) collective-permute-start(bf16[528,128]{1,0:T(8,128)(2,1)S(1)} %get-tuple-element.10.own_ref), channel_id=1, source_target_pairs={{0,24},{2,26},{4,28},{6,30},{8,0},{10,2},{12,4},{14,6},{16,8},{18,... | collective-permute-start | bytes 405512 | tf_op jit(solution)/shard_map/ppermute | solution.py:21
  11.3 8.3 %collective-permute-start.4 = (bf16[528,128]{1,0:T(8,128)(2,1)S(1)}, bf16[528,128]{1,0:T(8,128)(2,1)S(1)}, u32[]{:S(2)}, u32[]{:S(2)}) collective-permute-start(bf16[528,128]{1,0:T(8,128)(2,1)S(1)} %get-tuple-element.10.own_ref), channel_id=1, source_target_pairs={{0,8},{2,10},{4,12},{6,14},{8,16},{10,18},{12,20},{14,22},{16,24},... | collective-permute-start | bytes 405512 | tf_op jit(solution)/shard_map/ppermute | solution.py:21
  11.3 8.7 %collective-permute-start.2 = (bf16[528,128]{1,0:T(8,128)(2,1)S(1)}, bf16[528,128]{1,0:T(8,128)(2,1)S(1)}, u32[]{:S(2)}, u32[]{:S(2)}) collective-permute-start(bf16[528,128]{1,0:T(8,128)(2,1)S(1)} %get-tuple-element.10.own_ref), channel_id=1, source_target_pairs={{0,30},{2,0},{4,2},{6,4},{8,6},{10,8},{12,10},{14,12},{16,14},{18,... | collective-permute-start | bytes 405512 | tf_op jit(solution)/shard_map/ppermute | solution.py:21
  17.0 8.6 %collective-permute-start = (bf16[528,128]{1,0:T(8,128)(2,1)S(1)}, bf16[528,128]{1,0:T(8,128)(2,1)S(1)}, u32[]{:S(2)}, u32[]{:S(2)}) collective-permute-start(bf16[528,128]{1,0:T(8,128)(2,1)S(1)} %get-tuple-element.10.own_ref), channel_id=1, source_target_pairs={{0,2},{2,4},{4,6},{6,8},{8,10},{10,12},{12,14},{14,16},{16,18},{18... | collective-permute-start | bytes 405512 | tf_op jit(solution)/shard_map/ppermute | solution.py:21
  17.0 8.7 %collective-permute-start.7 = (bf16[528,128]{1,0:T(8,128)(2,1)S(1)}, bf16[528,128]{1,0:T(8,128)(2,1)S(1)}, u32[]{:S(2)}, u32[]{:S(2)}) collective-permute-start(bf16[528,128]{1,0:T(8,128)(2,1)S(1)} %collective-permute-done.6.refs_6_), channel_id=1, source_target_pairs={{0,1},{1,0},{2,3},{3,2},{4,5},{5,4},{6,7},{7,6},{8,9},{9,8},{10,11... | collective-permute-start | bytes 405512 | tf_op jit(solution)/shard_map/ppermute | solution.py:26
  19.6 6.1 %collective-permute-start.5 = (bf16[528,128]{1,0:T(8,128)(2,1)S(1)}, bf16[528,128]{1,0:T(8,128)(2,1)S(1)}, u32[]{:S(2)}, u32[]{:S(2)}) collective-permute-start(bf16[528,128]{1,0:T(8,128)(2,1)S(1)} %collective-permute-done.4.refs_4_), channel_id=1, source_target_pairs={{0,1},{1,0},{2,3},{3,2},{4,5},{5,4},{6,7},{7,6},{8,9},{9,8},{10,11... | collective-permute-start | bytes 405512 | tf_op jit(solution)/shard_map/ppermute | solution.py:26
  20.0 5.7 %collective-permute-start.3 = (bf16[528,128]{1,0:T(8,128)(2,1)S(1)}, bf16[528,128]{1,0:T(8,128)(2,1)S(1)}, u32[]{:S(2)}, u32[]{:S(2)}) collective-permute-start(bf16[528,128]{1,0:T(8,128)(2,1)S(1)} %collective-permute-done.2.refs_2_), channel_id=1, source_target_pairs={{0,1},{1,0},{2,3},{3,2},{4,5},{5,4},{6,7},{7,6},{8,9},{9,8},{10,11... | collective-permute-start | bytes 405512 | tf_op jit(solution)/shard_map/ppermute | solution.py:26
  25.6 1.4 %collective-permute-start.1 = (bf16[528,128]{1,0:T(8,128)(2,1)S(1)}, bf16[528,128]{1,0:T(8,128)(2,1)S(1)}, u32[]{:S(2)}, u32[]{:S(2)}) collective-permute-start(bf16[528,128]{1,0:T(8,128)(2,1)S(1)} %collective-permute-done.refs_0_), channel_id=1, source_target_pairs={{0,1},{1,0},{2,3},{3,2},{4,5},{5,4},{6,7},{7,6},{8,9},{9,8},{10,11... | collective-permute-start | bytes 405512 | tf_op jit(solution)/shard_map/ppermute | solution.py:26
  30.5 0.7 %copy-start.3 = (f32[512,128]{1,0:T(8,128)}, f32[512,128]{1,0:T(8,128)S(1)}, u32[]{:S(2)}) copy-start(f32[512,128]{1,0:T(8,128)S(1)} %couple.1.acc_ref) | copy-start | bytes 786436
  37.0 4.0 %collective-permute-start.8 = (bf16[1024,128]{1,0:T(8,128)(2,1)}, bf16[1024,128]{1,0:T(8,128)(2,1)S(1)}, u32[]{:S(2)}, u32[]{:S(2)}) collective-permute-start(bf16[1024,128]{1,0:T(8,128)(2,1)} %weight_term.3), channel_id=1, source_target_pairs={{0,1},{1,0},{2,3},{3,2},{4,5},{5,4},{6,7},{7,6},{8,9},{9,8},{10,11... | collective-permute-start | bytes 786440 | tf_op jit(solution)/shard_map/ppermute | solution.py:26
  41.0 0.7 %copy-start.5 = (bf16[1024,128]{1,0:T(8,128)(2,1)}, bf16[1024,128]{1,0:T(8,128)(2,1)S(1)}, u32[]{:S(2)}) copy-start(bf16[1024,128]{1,0:T(8,128)(2,1)S(1)} %collective-permute-done.8.refs_0_) | copy-start | bytes 786436
  43.6 4.9 %collective-permute-start.9 = (bf16[256,128]{1,0:T(8,128)(2,1)}, bf16[256,128]{1,0:T(8,128)(2,1)S(1)}, u32[]{:S(2)}, u32[]{:S(2)}) collective-permute-start(bf16[256,128]{1,0:T(8,128)(2,1)} %get-tuple-element.15), channel_id=1, source_target_pairs={{0,2},{2,0},{4,6},{6,4},{8,10},{10,8},{12,14},{14,12},{16,18},{18,... | collective-permute-start | bytes 196616 | tf_op jit(solution)/shard_map/ppermute | solution.py:26
  43.6 5.4 %collective-permute-start.10 = (bf16[256,128]{1,0:T(8,128)(2,1)}, bf16[256,128]{1,0:T(8,128)(2,1)S(1)}, u32[]{:S(2)}, u32[]{:S(2)}) collective-permute-start(bf16[256,128]{1,0:T(8,128)(2,1)} %get-tuple-element.16), channel_id=1, source_target_pairs={{0,4},{2,6},{4,0},{6,2},{8,12},{10,14},{12,8},{14,10},{16,20},{18,... | collective-permute-start | bytes 196616 | tf_op jit(solution)/shard_map/ppermute | solution.py:26
  43.6 6.0 %collective-permute-start.11 = (bf16[256,128]{1,0:T(8,128)(2,1)}, bf16[256,128]{1,0:T(8,128)(2,1)S(1)}, u32[]{:S(2)}, u32[]{:S(2)}) collective-permute-start(bf16[256,128]{1,0:T(8,128)(2,1)} %get-tuple-element.17), channel_id=1, source_target_pairs={{0,6},{2,4},{4,2},{6,0},{8,14},{10,12},{12,10},{14,8},{16,22},{18,... | collective-permute-start | bytes 196616 | tf_op jit(solution)/shard_map/ppermute | solution.py:26
  50.5 6.4 %collective-permute-start.14 = (bf16[256,128]{1,0:T(8,128)(2,1)S(1)}, bf16[256,128]{1,0:T(8,128)(2,1)S(1)}, u32[]{:S(2)}, u32[]{:S(2)}) collective-permute-start(bf16[256,128]{1,0:T(8,128)(2,1)S(1)} %add_convert_fusion.1), channel_id=1, source_target_pairs={{0,24},{2,26},{4,28},{6,30},{8,16},{10,18},{12,20},{14,22},{16,8},... | collective-permute-start | bytes 196616 | tf_op jit(solution)/shard_map/ppermute | solution.py:26
  51.9 6.3 %collective-permute-start.13 = (bf16[256,128]{1,0:T(8,128)(2,1)S(1)}, bf16[256,128]{1,0:T(8,128)(2,1)S(1)}, u32[]{:S(2)}, u32[]{:S(2)}) collective-permute-start(bf16[256,128]{1,0:T(8,128)(2,1)S(1)} %add_convert_fusion.1), channel_id=1, source_target_pairs={{0,16},{2,18},{4,20},{6,22},{8,24},{10,26},{12,28},{14,30},{16,0},... | collective-permute-start | bytes 196616 | tf_op jit(solution)/shard_map/ppermute | solution.py:26
  51.9 6.3 %collective-permute-start.12 = (bf16[256,128]{1,0:T(8,128)(2,1)S(1)}, bf16[256,128]{1,0:T(8,128)(2,1)S(1)}, u32[]{:S(2)}, u32[]{:S(2)}) collective-permute-start(bf16[256,128]{1,0:T(8,128)(2,1)S(1)} %add_convert_fusion.1), channel_id=1, source_target_pairs={{0,8},{2,10},{4,12},{6,14},{8,0},{10,2},{12,4},{14,6},{16,24},{18,... | collective-permute-start | bytes 196616 | tf_op jit(solution)/shard_map/ppermute | solution.py:26
  58.3 6.9 %copy-start.6 = (bf16[256,128]{1,0:T(8,128)(2,1)}, bf16[256,128]{1,0:T(8,128)(2,1)S(1)}, u32[]{:S(2)}) copy-start(bf16[256,128]{1,0:T(8,128)(2,1)S(1)} %add_convert_fusion.refs_0_) | copy-start | bytes 196612
  58.3 5.2 %collective-permute-start.17 = (bf16[256,128]{1,0:T(8,128)(2,1)S(1)}, bf16[256,128]{1,0:T(8,128)(2,1)S(1)}, u32[]{:S(2)}, u32[]{:S(2)}) collective-permute-start(bf16[256,128]{1,0:T(8,128)(2,1)S(1)} %add_convert_fusion.refs_0_), channel_id=1, source_target_pairs={{0,6},{2,4},{4,2},{6,0},{8,14},{10,12},{12,10},{14,8},{16,22},{18,... | collective-permute-start | bytes 196616 | tf_op jit(solution)/shard_map/ppermute | solution.py:26
  60.3 4.3 %collective-permute-start.16 = (bf16[256,128]{1,0:T(8,128)(2,1)S(1)}, bf16[256,128]{1,0:T(8,128)(2,1)S(1)}, u32[]{:S(2)}, u32[]{:S(2)}) collective-permute-start(bf16[256,128]{1,0:T(8,128)(2,1)S(1)} %add_convert_fusion.refs_0_), channel_id=1, source_target_pairs={{0,4},{2,6},{4,0},{6,2},{8,12},{10,14},{12,8},{14,10},{16,20},{18,... | collective-permute-start | bytes 196616 | tf_op jit(solution)/shard_map/ppermute | solution.py:26
  60.9 4.3 %collective-permute-start.15 = (bf16[256,128]{1,0:T(8,128)(2,1)S(1)}, bf16[256,128]{1,0:T(8,128)(2,1)S(1)}, u32[]{:S(2)}, u32[]{:S(2)}) collective-permute-start(bf16[256,128]{1,0:T(8,128)(2,1)S(1)} %add_convert_fusion.refs_0_), channel_id=1, source_target_pairs={{0,2},{2,0},{4,6},{6,4},{8,10},{10,8},{12,14},{14,12},{16,18},{18,... | collective-permute-start | bytes 196616 | tf_op jit(solution)/shard_map/ppermute | solution.py:26
  63.5 1.6 %copy-start.7 = (bf16[256,128]{1,0:T(8,128)(2,1)}, bf16[256,128]{1,0:T(8,128)(2,1)S(1)}, u32[]{:S(2)}) copy-start(bf16[256,128]{1,0:T(8,128)(2,1)S(1)} %collective-permute-done.17.refs_3_) | copy-start | bytes 196612
  64.6 0.6 copy-start.8
  65.2 0.6 copy-start.9

commit v2 on v1

v2 whole, which is shorter than its diff:
```python
import functools
import math

import jax
import jax.numpy as jnp
from jax import lax
from jax.experimental import pallas as pl
from jax.experimental.pallas import tpu as pltpu
from jax.sharding import PartitionSpec as P

inverse_temperature = 10.0
exponent_scale = 10.0 * math.log2(math.e)
epsilon = 1e-06
lanes = 128
tail = 16
f32, bf16 = jnp.float32, jnp.bfloat16


def shifted(value, axis, steps):
    count = lax.axis_size(axis)
    return lax.ppermute(value, axis, [(s, (s + steps) % count) for s in range(count)])


def swapped(value, axis, mask):
    count = lax.axis_size(axis)
    return lax.ppermute(value, axis, [(s, s ^ mask) for s in range(count)])


def vmem_spec():
    return pl.BlockSpec(memory_space=pltpu.VMEM)


def smem_spec():
    return pl.BlockSpec(memory_space=pltpu.SMEM)


def small_grant(mib):
    return pltpu.CompilerParams(vmem_limit_bytes=mib * 2**20)


def project_kernel(
    features_ref, weight_ref, lse_ref, projected_ref, packed_ref, held, weight, weight_sem, sems
):
    rows = held.shape[0]
    chunk = rows // sems.shape[0]
    weight_copy = pltpu.make_async_copy(weight_ref, weight, weight_sem)
    weight_copy.start()
    copies = []
    for k in range(sems.shape[0]):
        part = pl.ds(k * chunk, chunk)
        copy = pltpu.make_async_copy(features_ref.at[part, :], held.at[part, :], sems.at[k])
        copy.start()
        copies.append(copy)
    packed_ref[pl.ds(rows, tail), :] = lse_ref[...]
    weight_copy.wait()
    for k, copy in enumerate(copies):
        part = pl.ds(k * chunk, chunk)
        copy.wait()
        projected = jnp.dot(held[part, :], weight[...], preferred_element_type=f32)
        magnitude = jnp.sqrt(jnp.sum(projected * projected, axis=-1, keepdims=True) + epsilon)
        projected_ref[part, :] = projected
        packed_ref[part, :] = (projected / magnitude).astype(bf16)


def project(features, weight, lse_rows):
    rows, units = features.shape
    width = weight.shape[1]
    chunks = 4
    hbm = pl.BlockSpec(memory_space=pltpu.HBM)
    return pl.pallas_call(
        project_kernel,
        in_specs=[hbm, hbm, vmem_spec()],
        out_specs=[vmem_spec()] * 2,
        out_shape=[
            jax.ShapeDtypeStruct((rows, width), f32),
            jax.ShapeDtypeStruct((rows + tail, width), bf16),
        ],
        scratch_shapes=[
            pltpu.VMEM((rows, units), bf16),
            pltpu.VMEM((units, width), bf16),
            pltpu.SemaphoreType.DMA,
            pltpu.SemaphoreType.DMA((chunks,)),
        ],
        compiler_params=small_grant(8),
        name="project",
    )(features, weight, lse_rows)


def as_columns(rows):
    return jnp.concatenate(
        [
            jnp.broadcast_to(rows[k : k + 1, :], (lanes, lanes)).T
            for k in range(rows.shape[0])
        ],
        axis=0,
    )


def coupled_rows(start, chunk, own_weight, own_positive, base_ref, own_ref, parts, total):
    rows = own_ref.shape[0] - tail
    column = lax.broadcasted_iota(jnp.int32, (1, lanes), 1)
    own = own_ref[pl.ds(start, chunk), :]
    weight_i = own_weight[start : start + chunk, :]
    positive_i = own_positive[start : start + chunk, :]
    for which, part in enumerate(parts):
        part_weight = jnp.exp(-part[pl.ds(rows, tail), :].astype(f32))
        for begin in range(0, rows, chunk):
            other = part[pl.ds(begin, chunk), :]
            cosine = lax.dot_general(
                own, other, (((1,), (1,)), ((), ())), preferred_element_type=f32
            )
            pieces = []
            for lane in range(0, chunk, lanes):
                k = (begin + lane) // lanes
                grown = jnp.exp2(cosine[:, lane : lane + lanes] * exponent_scale)
                ids = (column + (base_ref[which] + (begin + lane))).astype(f32)
                value = grown * (weight_i + part_weight[k : k + 1, :])
                value = value - jnp.where(positive_i == ids, 2.0, 0.0)
                pieces.append(value.astype(bf16))
            coupling = jnp.concatenate(pieces, axis=1)
            total = total + jnp.dot(coupling, other, preferred_element_type=f32)
    return total


def own_columns(own_ref, positive_ref):
    rows = own_ref.shape[0] - tail
    own_weight = as_columns(jnp.exp(-own_ref[pl.ds(rows, tail), :].astype(f32))[: rows // lanes, :])
    return own_weight, as_columns(positive_ref[...].astype(f32))


def couple_kernel(base_ref, own_ref, positive_ref, *refs):
    parts, acc_ref = refs[:-1], refs[-1]
    rows = own_ref.shape[0] - tail
    chunk = min(256, rows)
    columns = own_columns(own_ref, positive_ref)
    for start in range(0, rows, chunk):
        total = jnp.zeros((chunk, own_ref.shape[1]), f32)
        acc_ref[pl.ds(start, chunk), :] = coupled_rows(
            start, chunk, *columns, base_ref, own_ref, parts, total
        )


def couple_cost(rows, width, count):
    pairs = rows * rows * count
    return pl.CostEstimate(
        flops=4 * pairs * width, bytes_accessed=rows * width * 4, transcendentals=pairs
    )


def couple(base, own, positive, parts):
    rows, width = own.shape[0] - tail, own.shape[1]
    return pl.pallas_call(
        couple_kernel,
        in_specs=[smem_spec()] + [vmem_spec()] * (2 + len(parts)),
        out_specs=vmem_spec(),
        out_shape=jax.ShapeDtypeStruct((rows, width), f32),
        compiler_params=small_grant(8),
        cost_estimate=couple_cost(rows, width, len(parts)),
        name="couple",
    )(base, own, positive, *parts)


def finish_kernel(
    count, shares, base_ref, own_ref, positive_ref, acc_ref, projected_ref, features_ref, *refs
):
    parts, grad_ref, half_ref, sends = refs[:count], refs[count], refs[count + 1], refs[count + 2 :]
    rows = own_ref.shape[0] - tail
    chunk = min(256, rows)
    columns = own_columns(own_ref, positive_ref)
    for start in range(0, rows, chunk):
        part = pl.ds(start, chunk)
        total = coupled_rows(
            start, chunk, *columns, base_ref, own_ref, parts, acc_ref[part, :]
        )
        projected = projected_ref[part, :]
        magnitude = jnp.sqrt(jnp.sum(projected * projected, axis=-1, keepdims=True) + epsilon)
        unit = projected / magnitude
        upstream = total * inverse_temperature
        grad = (upstream - unit * jnp.sum(unit * upstream, axis=-1, keepdims=True)) / magnitude
        grad_ref[part, :] = grad
        half_ref[:, part] = grad.T.astype(bf16)
    for mask, send in enumerate(sends, 1):
        share = base_ref[count] ^ mask
        weight_columns(half_ref, features_ref, share, send)


def weight_columns(half_ref, features_ref, share, out_ref):
    size = out_ref.shape[1]
    chunk = min(256, size)
    for start in range(0, size, chunk):
        columns = pl.ds(pl.multiple_of(share * size + start, chunk), chunk)
        out_ref[:, pl.ds(start, chunk)] = jnp.dot(
            half_ref[...], features_ref[:, columns], preferred_element_type=f32
        ).astype(out_ref.dtype)


def finish(base, own, positive, acc, projected, features, parts, shares):
    rows, width = projected.shape
    units = features.shape[1]
    return pl.pallas_call(
        functools.partial(finish_kernel, len(parts), shares),
        in_specs=[smem_spec()] + [vmem_spec()] * (5 + len(parts)),
        out_specs=[vmem_spec()] * (1 + shares),
        out_shape=[
            jax.ShapeDtypeStruct((rows, width), f32),
            jax.ShapeDtypeStruct((width, rows), bf16),
        ]
        + [jax.ShapeDtypeStruct((width, units // shares), bf16)] * (shares - 1),
        compiler_params=small_grant(8),
        cost_estimate=couple_cost(rows, width, len(parts)),
        name="finish",
    )(base, own, positive, acc, projected, features, *parts)


def weight_kernel(share_ref, half_ref, features_ref, out_ref):
    weight_columns(half_ref, features_ref, share_ref[0], out_ref)


def weight_term(half, features, share, shares):
    width, rows = half.shape
    size = features.shape[1] // shares
    return pl.pallas_call(
        weight_kernel,
        in_specs=[smem_spec()] + [vmem_spec()] * 2,
        out_specs=vmem_spec(),
        out_shape=jax.ShapeDtypeStruct((width, size), f32),
        compiler_params=small_grant(8),
        cost_estimate=pl.CostEstimate(
            flops=2 * rows * size * width, bytes_accessed=rows * size * 2, transcendentals=0
        ),
        name="weight_term",
    )(share[None], half, features)


def split_kernel(count, digit_ref, own_ref, *refs):
    parts, keep_ref, sends = refs[:count], refs[count], refs[count + 1 :]
    size = keep_ref.shape[1]
    for s in range(len(sends) + 1):
        columns = pl.ds(pl.multiple_of((digit_ref[0] ^ s) * size, size), size)
        total = own_ref[:, columns]
        for part in parts:
            total = total + part[:, columns].astype(f32)
        if s == 0:
            keep_ref[...] = total
        else:
            sends[s - 1][...] = total.astype(bf16)


def split(digit, own, parts, ways):
    width, size = own.shape[0], own.shape[1] // ways
    return pl.pallas_call(
        functools.partial(split_kernel, len(parts)),
        in_specs=[smem_spec()] + [vmem_spec()] * (1 + len(parts)),
        out_specs=[vmem_spec()] * ways,
        out_shape=[jax.ShapeDtypeStruct((width, size), f32)]
        + [jax.ShapeDtypeStruct((width, size), bf16)] * (ways - 1),
        compiler_params=small_grant(4),
        name="split",
    )(digit[None], own, *parts)


def join_kernel(digit_ref, *refs):
    parts, out_ref = refs[:-1], refs[-1]
    size = parts[0].shape[1]
    for s, part in enumerate(parts):
        rows = pl.ds(pl.multiple_of((digit_ref[0] ^ s) * size, size), size)
        out_ref[rows, :] = part[...].astype(f32).T


def join(digit, parts):
    width, size = parts[0].shape
    return pl.pallas_call(
        join_kernel,
        in_specs=[smem_spec()] + [vmem_spec()] * len(parts),
        out_specs=vmem_spec(),
        out_shape=jax.ShapeDtypeStruct((size * len(parts), width), f32),
        compiler_params=small_grant(4),
        name="join",
    )(digit[None], *parts)


def body(features, proj_weight, row_lse, positive):
    rows = features.shape[0]
    dp_count = lax.axis_size("dp")
    pair_count = lax.axis_size("pair")
    far = pair_count // 4
    group_rows = rows * dp_count
    block = lax.axis_index("pair").astype(jnp.int32)
    core = lax.axis_index("dp").astype(jnp.int32)

    lse_rows = jnp.pad(row_lse.reshape(rows // lanes, lanes), ((0, tail - rows // lanes), (0, 0)))
    positive_rows = positive.reshape(rows // lanes, lanes)
    projected, packed = project(features, proj_weight, lse_rows)

    def partner(*offsets):
        bases, parts = [], []
        for offset in offsets:
            part = shifted(packed, "pair", offset)
            first = jnp.remainder(block - offset, pair_count) * group_rows
            for mask in range(dp_count):
                parts.append(part if mask == 0 else swapped(part, "dp", mask))
                bases.append(first + (core ^ mask) * rows)
        return jnp.stack(bases + [core]), parts

    far_bases, far_parts = partner(far, -far)
    near_bases, near_parts = partner(1, -1)
    acc = couple(far_bases, packed, positive_rows, far_parts)
    grad_embed, half, *sends = finish(
        near_bases, packed, positive_rows, acc, projected, features, near_parts, dp_count
    )
    received = [swapped(send, "dp", mask) for mask, send in enumerate(sends, 1)]
    mine = weight_term(half, features, core, dp_count)

    ways = 4
    digit = block & (ways - 1)
    keep, *sends = split(digit, mine, received, ways)
    for s in range(1, ways):
        keep = keep + swapped(sends[s - 1], "pair", s).astype(f32)
    stride = ways
    while stride < pair_count:
        mine = keep.astype(bf16)
        near, middle, last = (swapped(mine, "pair", s * stride).astype(f32) for s in (1, 2, 3))
        keep = (mine.astype(f32) + near) + (middle + last)
        stride *= ways
    mine = keep.astype(bf16)
    quarters = [mine] + [swapped(mine, "pair", s) for s in range(1, ways)]
    return (grad_embed, join(digit, quarters))


def solution(mesh):
    return jax.shard_map(
        body,
        mesh=mesh,
        in_specs=(P(("pair", "dp"), None), P(), P(("pair", "dp")), P(("pair", "dp"))),
        out_specs=(P(("pair", "dp"), None), P("dp", None)),
        check_vma=False,
    )
```

time: 68.1 us -> 54.6 us (0.80)
  Pallas kernels: 18.4 us -> 8.89 us
  local copies, waits for them, and re-layouts: 6.25 us -> 3.5 us
  other arithmetic: 0.98 us -> 0.07 us
    pallas_call x5 -> x4, Pallas kernels: 14.7 us -> 7.88 us  [the longest x1 3.13 us: finish(): pl.pallas_call(functools.partial(finish_kernel, len(parts), shares), in_s...]
    unnamed x20 -> x8, local copies, waits for them, and re-layouts: 5.48 us -> 2.64 us
    pallas_call x1, Pallas kernels: 1.87 us -> 0.07 us  [split(): pl.pallas_call(functools.partial(split_kernel, len(parts)), in_specs=[sme...]
    convert_element_type x2, other arithmetic: 0.98 us -> 0.07 us  [body(): mine = keep.astype(bf16)]
    pallas_call x1, Pallas kernels: 1.76 us -> 0.94 us  [join(): pl.pallas_call(join_kernel, in_specs=[smem_spec()] + [vmem_spec()] * len(...]
  transfers between devices with their start and end apart: 18 -> 18, of which waited for: 12 -> 11; matrix products, arithmetic and copies ran while one was open for 0% -> 0% of each run, Pallas kernels for 6% -> 6%
where the time goes in v2:
time: 54.6 us; the launch traced here: 54.3 us
  starting transfers between devices  23 us (42%)
  waiting for transfers between devices  18.1 us (33%)
  Pallas kernels  8.89 us (16%)
  local copies, waits for them, and re-layouts  3.5 us (6%)
  between operations  0.74 us (1%)
    ppermute x14, starting transfers between devices, swapped(): return lax.ppermute(value, axis, [(s, s ^ mask) for s in range(count)])  12.2 us
    ppermute x4, starting transfers between devices, shifted(): lax.ppermute(value, axis, [(s, (s + steps) % count) for s in range(count)])  10.8 us
    ppermute x14, waiting for transfers between devices, swapped(): return lax.ppermute(value, axis, [(s, s ^ mask) for s in range(count)])  9.67 us
    ppermute x4, waiting for transfers between devices, shifted(): lax.ppermute(value, axis, [(s, (s + steps) % count) for s in range(count)])  8.44 us
    pallas_call x1, Pallas kernels, finish(): pl.pallas_call(functools.partial(finish_kernel, len(parts), shares), in_s...  3.13 us
    pallas_call x1, Pallas kernels, couple(): pl.pallas_call(couple_kernel, in_specs=[smem_spec()] + [vmem_spec()] * (2...  2.68 us
    unnamed x8, local copies, waits for them, and re-layouts  2.64 us
    pallas_call x1, Pallas kernels, project(): pl.pallas_call(project_kernel, in_specs=[hbm, hbm, vmem_spec()], out_spec...  1.75 us
  transfers between devices with their start and end apart: 18, of which 11 were waited for; matrix products, arithmetic and copies ran while one was open for 0% of the time, Pallas kernels for 6%

profile of v2, /device:TPU:0, one launch (start us, length us, event | category | flops | bytes accessed | tf_op | source)
XLA Modules:
  0.0 54.3 jit_solution(13332352787762143877)
XLA Ops:
  0.6 0.7 %pad.4.lse_ref = bf16[16,128]{1,0:T(8,128)(2,1)S(1)} pad(bf16[4,128]{1,0:T(4,128)(2,1)} %bitcast.14, bf16[]{:T(256)} %constant.50.clone.1), padding=0_12x0_0 | pad | bytes 5122 | tf_op jit(solution)/shard_map/jit(_pad)/pad | solution.py:291
  1.3 1.6 %copy-done = bf16[512,2048]{1,0:T(8,128)(2,1)S(1)} copy-done((bf16[512,2048]{1,0:T(8,128)(2,1)S(1)}, bf16[512,2048]{1,0:T(8,128)(2,1)}, u32[]{:S(2)}) %copy-start) | copy-done | bytes 2097176
  2.9 1.0 %copy-done.2 = bf16[2048,128]{1,0:T(8,128)(2,1)S(1)} copy-done((bf16[2048,128]{1,0:T(8,128)(2,1)S(1)}, bf16[2048,128]{1,0:T(8,128)(2,1)}, u32[]{:S(2)}) %copy-start.2) | copy-done | bytes 524312
  4.0 1.8 %project.1 = (f32[512,128]{1,0:T(8,128)S(1)}, bf16[528,128]{1,0:T(8,128)(2,1)S(1)}) custom-call(bf16[512,2048]{1,0:T(8,128)(2,1)S(1)} %copy-done, bf16[2048,128]{1,0:T(8,128)(2,1)S(1)} %copy-done.2, bf16[16,128]{1,0:T(8,128)(2,1)S(1)} %pad.4.lse_ref), custom_call_target="tpu_custom_call" | custom-call | tf_op jit(solution)/shard_map/project/pallas_call | solution.py:70
  5.7 5.1 %collective-permute-start.2 = (bf16[528,128]{1,0:T(8,128)(2,1)S(1)}, bf16[528,128]{1,0:T(8,128)(2,1)S(1)}, u32[]{:S(2)}, u32[]{:S(2)}) collective-permute-start(bf16[528,128]{1,0:T(8,128)(2,1)S(1)} %get-tuple-element.11.own_ref), channel_id=1, source_target_pairs={{0,24},{2,26},{4,28},{6,30},{8,0},{10,2},{12,4},{14,6},{16,8},{18,... | collective-permute-start | bytes 405512 | tf_op jit(solution)/shard_map/ppermute | solution.py:21
  10.8 5.7 %collective-permute-start.6 = (bf16[528,128]{1,0:T(8,128)(2,1)S(1)}, bf16[528,128]{1,0:T(8,128)(2,1)S(1)}, u32[]{:S(2)}, u32[]{:S(2)}) collective-permute-start(bf16[528,128]{1,0:T(8,128)(2,1)S(1)} %get-tuple-element.11.own_ref), channel_id=1, source_target_pairs={{0,30},{2,0},{4,2},{6,4},{8,6},{10,8},{12,10},{14,12},{16,14},{18,... | collective-permute-start | bytes 405512 | tf_op jit(solution)/shard_map/ppermute | solution.py:21
  16.6 2.6 %collective-permute-done.refs_0_ = bf16[528,128]{1,0:T(8,128)(2,1)S(1)} collective-permute-done((bf16[528,128]{1,0:T(8,128)(2,1)S(1)}, bf16[528,128]{1,0:T(8,128)(2,1)S(1)}, u32[]{:S(2)}, u32[]{:S(2)}) %collective-permute-start) | collective-permute-done | bytes 135200 | tf_op jit(solution)/shard_map/ppermute | solution.py:21
  19.1 0.4 collective-permute-done.6.refs_2_
  19.5 0.1 collective-permute-start.7
  19.7 5.5 %collective-permute-done.4.refs_0_ = bf16[528,128]{1,0:T(8,128)(2,1)S(1)} collective-permute-done((bf16[528,128]{1,0:T(8,128)(2,1)S(1)}, bf16[528,128]{1,0:T(8,128)(2,1)S(1)}, u32[]{:S(2)}, u32[]{:S(2)}) %collective-permute-start.4) | collective-permute-done | bytes 135200 | tf_op jit(solution)/shard_map/ppermute | solution.py:21
  25.1 0.1 stack.39.base_ref
  25.2 0.1 stack.44.base_ref
  25.3 2.7 %couple.1.acc_ref = f32[512,128]{1,0:T(8,128)S(1)} custom-call(s32[5]{0:T(128)S(1)} %stack.44.base_ref, bf16[528,128]{1,0:T(8,128)(2,1)S(1)} %get-tuple-element.11.own_ref, s32[4,128]{1,0:T(4,128)S(1)} %bitcast.12, bf16[528,128]{1,0:T(8,128)(2,1)S(1)} %collective-permute-done.refs_0_, bf16[528,128]{1,0:T(8,128)(2,1)} %collective-permute-done.1.refs_1_, ...), custom_call_target="tpu_custom_call" | custom-call | flops 536870912 | bytes 262144 | tf_op jit(solution)/shard_map/couple/pallas_call | solution.py:152
  28.1 3.1 %finish.1 = (f32[512,128]{1,0:T(8,128)}, bf16[128,512]{1,0:T(8,128)(2,1)S(1)}, bf16[128,1024]{1,0:T(8,128)(2,1)S(1)}) custom-call(s32[5]{0:T(128)S(1)} %stack.39.base_ref, bf16[528,128]{1,0:T(8,128)(2,1)S(1)} %get-tuple-element.11.own_ref, s32[4,128]{1,0:T(4,128)S(1)} %bitcast.13, f32[512,128]{1,0:T(8,128)S(1)} %couple.1.acc_ref, ...), custom_call_target="tpu_custom_call" | custom-call | flops 536870912 | bytes 262144 | tf_op jit(solution)/shard_map/finish/pallas_call | solution.py:200
  31.2 0.5 collective-permute-start.8
  31.7 0.3 weight_term.1.own_ref
  32.0 0.8 %collective-permute-done.8.refs_0_ = bf16[128,1024]{1,0:T(8,128)(2,1)S(1)} collective-permute-done((bf16[128,1024]{1,0:T(8,128)(2,1)S(1)}, bf16[128,1024]{1,0:T(8,128)(2,1)S(1)}, u32[]{:S(2)}, u32[]{:S(2)}) %collective-permute-start.8) | collective-permute-done | bytes 262176 | tf_op jit(solution)/shard_map/ppermute | solution.py:26
  32.9 0.1 split.1
  33.1 3.4 %collective-permute-start.11 = (bf16[128,256]{1,0:T(8,128)(2,1)S(1)}, bf16[128,256]{1,0:T(8,128)(2,1)S(1)}, u32[]{:S(2)}, u32[]{:S(2)}) collective-permute-start(bf16[128,256]{1,0:T(8,128)(2,1)S(1)} %get-tuple-element.19), channel_id=1, source_target_pairs={{0,6},{2,4},{4,2},{6,0},{8,14},{10,12},{12,10},{14,8},{16,22},{18,... | collective-permute-start | bytes 196616 | tf_op jit(solution)/shard_map/ppermute | solution.py:26
  36.5 1.1 %collective-permute-done.9 = bf16[128,256]{1,0:T(8,128)(2,1)S(1)} collective-permute-done((bf16[128,256]{1,0:T(8,128)(2,1)S(1)}, bf16[128,256]{1,0:T(8,128)(2,1)S(1)}, u32[]{:S(2)}, u32[]{:S(2)}) %collective-permute-start.9) | collective-permute-done | bytes 65568 | tf_op jit(solution)/shard_map/ppermute | solution.py:26
  37.6 1.3 %collective-permute-done.10 = bf16[128,256]{1,0:T(8,128)(2,1)S(1)} collective-permute-done((bf16[128,256]{1,0:T(8,128)(2,1)S(1)}, bf16[128,256]{1,0:T(8,128)(2,1)S(1)}, u32[]{:S(2)}, u32[]{:S(2)}) %collective-permute-start.10) | collective-permute-done | bytes 65568 | tf_op jit(solution)/shard_map/ppermute | solution.py:26
  38.9 1.3 %collective-permute-start.14 = (bf16[128,256]{1,0:T(8,128)(2,1)S(1)}, bf16[128,256]{1,0:T(8,128)(2,1)S(1)}, u32[]{:S(2)}, u32[]{:S(2)}) collective-permute-start(bf16[128,256]{1,0:T(8,128)(2,1)S(1)} %add_convert_fusion.1), channel_id=1, source_target_pairs={{0,24},{2,26},{4,28},{6,30},{8,16},{10,18},{12,20},{14,22},{16,8},... | collective-permute-start | bytes 196616 | tf_op jit(solution)/shard_map/ppermute | solution.py:26
  40.2 3.1 %collective-permute-start.12 = (bf16[128,256]{1,0:T(8,128)(2,1)S(1)}, bf16[128,256]{1,0:T(8,128)(2,1)S(1)}, u32[]{:S(2)}, u32[]{:S(2)}) collective-permute-start(bf16[128,256]{1,0:T(8,128)(2,1)S(1)} %add_convert_fusion.1), channel_id=1, source_target_pairs={{0,8},{2,10},{4,12},{6,14},{8,0},{10,2},{12,4},{14,6},{16,24},{18,... | collective-permute-start | bytes 196616 | tf_op jit(solution)/shard_map/ppermute | solution.py:26
  43.3 1.9 %collective-permute-done.14 = bf16[128,256]{1,0:T(8,128)(2,1)S(1)} collective-permute-done((bf16[128,256]{1,0:T(8,128)(2,1)S(1)}, bf16[128,256]{1,0:T(8,128)(2,1)S(1)}, u32[]{:S(2)}, u32[]{:S(2)}) %collective-permute-start.14) | collective-permute-done | bytes 65568 | tf_op jit(solution)/shard_map/ppermute | solution.py:26
  45.2 1.3 %collective-permute-done.13 = bf16[128,256]{1,0:T(8,128)(2,1)S(1)} collective-permute-done((bf16[128,256]{1,0:T(8,128)(2,1)S(1)}, bf16[128,256]{1,0:T(8,128)(2,1)S(1)}, u32[]{:S(2)}, u32[]{:S(2)}) %collective-permute-start.13) | collective-permute-done | bytes 65568 | tf_op jit(solution)/shard_map/ppermute | solution.py:26
  46.6 2.1 %collective-permute-start.17 = (bf16[128,256]{1,0:T(8,128)(2,1)S(1)}, bf16[128,256]{1,0:T(8,128)(2,1)S(1)}, u32[]{:S(2)}, u32[]{:S(2)}) collective-permute-start(bf16[128,256]{1,0:T(8,128)(2,1)S(1)} %add_convert_fusion.refs_0_), channel_id=1, source_target_pairs={{0,6},{2,4},{4,2},{6,0},{8,14},{10,12},{12,10},{14,8},{16,22},{18,... | collective-permute-start | bytes 196616 | tf_op jit(solution)/shard_map/ppermute | solution.py:26
  48.6 0.5 collective-permute-start.16
  49.1 1.0 %collective-permute-start.15 = (bf16[128,256]{1,0:T(8,128)(2,1)S(1)}, bf16[128,256]{1,0:T(8,128)(2,1)S(1)}, u32[]{:S(2)}, u32[]{:S(2)}) collective-permute-start(bf16[128,256]{1,0:T(8,128)(2,1)S(1)} %add_convert_fusion.refs_0_), channel_id=1, source_target_pairs={{0,2},{2,0},{4,6},{6,4},{8,10},{10,8},{12,14},{14,12},{16,18},{18,... | collective-permute-start | bytes 196616 | tf_op jit(solution)/shard_map/ppermute | solution.py:26
  50.1 1.7 %collective-permute-done.17.refs_3_ = bf16[128,256]{1,0:T(8,128)(2,1)S(1)} collective-permute-done((bf16[128,256]{1,0:T(8,128)(2,1)S(1)}, bf16[128,256]{1,0:T(8,128)(2,1)S(1)}, u32[]{:S(2)}, u32[]{:S(2)}) %collective-permute-start.17) | collective-permute-done | bytes 65568 | tf_op jit(solution)/shard_map/ppermute | solution.py:26
  51.8 1.1 %collective-permute-done.16.refs_2_ = bf16[128,256]{1,0:T(8,128)(2,1)S(1)} collective-permute-done((bf16[128,256]{1,0:T(8,128)(2,1)S(1)}, bf16[128,256]{1,0:T(8,128)(2,1)S(1)}, u32[]{:S(2)}, u32[]{:S(2)}) %collective-permute-start.16) | collective-permute-done | bytes 65568 | tf_op jit(solution)/shard_map/ppermute | solution.py:26
  52.9 0.5 collective-permute-done.15.refs_1_
  53.4 0.9 %join.1 = f32[1024,128]{1,0:T(8,128)} custom-call(s32[1]{0:T(128)} %bitcast.11.digit_ref, bf16[128,256]{1,0:T(8,128)(2,1)S(1)} %add_convert_fusion.refs_0_, bf16[128,256]{1,0:T(8,128)(2,1)S(1)} %collective-permute-done.15.refs_1_, bf16[128,256]{1,0:T(8,128)(2,1)S(1)} %collective-permute-done.16.refs_2_, bf16[128,256]{1,0:T(8,128)(2,1)S(1)} %collective-permute-done.17.refs_3_), custom_call_target="tpu_custom_call" | custom-call | tf_op jit(solution)/shard_map/join/pallas_call | solution.py:272
  (23 shorter events, 0.3 us)
Async XLA Ops:
  0.6 24.7 %copy-start.3 = (s32[512]{0:T(512)S(1)}, s32[512]{0:T(512)}, u32[]{:S(2)}) copy-start(s32[512]{0:T(512)} %param.7) | copy-start | bytes 6148
  1.3 1.6 %copy-start = (bf16[512,2048]{1,0:T(8,128)(2,1)S(1)}, bf16[512,2048]{1,0:T(8,128)(2,1)}, u32[]{:S(2)}) copy-start(bf16[512,2048]{1,0:T(8,128)(2,1)} %features_ref.5) | copy-start | bytes 6291460
  2.9 1.0 %copy-start.2 = (bf16[2048,128]{1,0:T(8,128)(2,1)S(1)}, bf16[2048,128]{1,0:T(8,128)(2,1)}, u32[]{:S(2)}) copy-start(bf16[2048,128]{1,0:T(8,128)(2,1)} %weight_ref.1) | copy-start | bytes 1572868
  4.0 24.1 %copy-start.1 = (bf16[512,2048]{1,0:T(8,128)(2,1)S(1)}, bf16[512,2048]{1,0:T(8,128)(2,1)}, u32[]{:S(2)}) copy-start(bf16[512,2048]{1,0:T(8,128)(2,1)} %features_ref.5) | copy-start | bytes 6291460
  5.7 10.8 %collective-permute-start.2 = (bf16[528,128]{1,0:T(8,128)(2,1)S(1)}, bf16[528,128]{1,0:T(8,128)(2,1)S(1)}, u32[]{:S(2)}, u32[]{:S(2)}) collective-permute-start(bf16[528,128]{1,0:T(8,128)(2,1)S(1)} %get-tuple-element.11.own_ref), channel_id=1, source_target_pairs={{0,24},{2,26},{4,28},{6,30},{8,0},{10,2},{12,4},{14,6},{16,8},{18,... | collective-permute-start | bytes 405512 | tf_op jit(solution)/shard_map/ppermute | solution.py:21
  10.8 8.3 %collective-permute-start = (bf16[528,128]{1,0:T(8,128)(2,1)S(1)}, bf16[528,128]{1,0:T(8,128)(2,1)S(1)}, u32[]{:S(2)}, u32[]{:S(2)}) collective-permute-start(bf16[528,128]{1,0:T(8,128)(2,1)S(1)} %get-tuple-element.11.own_ref), channel_id=1, source_target_pairs={{0,8},{2,10},{4,12},{6,14},{8,16},{10,18},{12,20},{14,22},{16,24},... | collective-permute-start | bytes 405512 | tf_op jit(solution)/shard_map/ppermute | solution.py:21
  10.8 8.7 %collective-permute-start.6 = (bf16[528,128]{1,0:T(8,128)(2,1)S(1)}, bf16[528,128]{1,0:T(8,128)(2,1)S(1)}, u32[]{:S(2)}, u32[]{:S(2)}) collective-permute-start(bf16[528,128]{1,0:T(8,128)(2,1)S(1)} %get-tuple-element.11.own_ref), channel_id=1, source_target_pairs={{0,30},{2,0},{4,2},{6,4},{8,6},{10,8},{12,10},{14,12},{16,14},{18,... | collective-permute-start | bytes 405512 | tf_op jit(solution)/shard_map/ppermute | solution.py:21
  16.5 8.6 %collective-permute-start.4 = (bf16[528,128]{1,0:T(8,128)(2,1)S(1)}, bf16[528,128]{1,0:T(8,128)(2,1)S(1)}, u32[]{:S(2)}, u32[]{:S(2)}) collective-permute-start(bf16[528,128]{1,0:T(8,128)(2,1)S(1)} %get-tuple-element.11.own_ref), channel_id=1, source_target_pairs={{0,2},{2,4},{4,6},{6,8},{8,10},{10,12},{12,14},{14,16},{16,18},{18... | collective-permute-start | bytes 405512 | tf_op jit(solution)/shard_map/ppermute | solution.py:21
  16.5 8.8 %collective-permute-start.3 = (bf16[528,128]{1,0:T(8,128)(2,1)S(1)}, bf16[528,128]{1,0:T(8,128)(2,1)}, u32[]{:S(2)}, u32[]{:S(2)}) collective-permute-start(bf16[528,128]{1,0:T(8,128)(2,1)S(1)} %collective-permute-done.2.refs_2_), channel_id=1, source_target_pairs={{0,1},{1,0},{2,3},{3,2},{4,5},{5,4},{6,7},{7,6},{8,9},{9,8},{10,11... | collective-permute-start | bytes 405512 | tf_op jit(solution)/shard_map/ppermute | solution.py:26
  19.1 6.2 %collective-permute-start.1 = (bf16[528,128]{1,0:T(8,128)(2,1)S(1)}, bf16[528,128]{1,0:T(8,128)(2,1)}, u32[]{:S(2)}, u32[]{:S(2)}) collective-permute-start(bf16[528,128]{1,0:T(8,128)(2,1)S(1)} %collective-permute-done.refs_0_), channel_id=1, source_target_pairs={{0,1},{1,0},{2,3},{3,2},{4,5},{5,4},{6,7},{7,6},{8,9},{9,8},{10,11... | collective-permute-start | bytes 405512 | tf_op jit(solution)/shard_map/ppermute | solution.py:26
  19.5 8.5 %collective-permute-start.7 = (bf16[528,128]{1,0:T(8,128)(2,1)S(1)}, bf16[528,128]{1,0:T(8,128)(2,1)S(1)}, u32[]{:S(2)}, u32[]{:S(2)}) collective-permute-start(bf16[528,128]{1,0:T(8,128)(2,1)S(1)} %collective-permute-done.6.refs_2_), channel_id=1, source_target_pairs={{0,1},{1,0},{2,3},{3,2},{4,5},{5,4},{6,7},{7,6},{8,9},{9,8},{10,11... | collective-permute-start | bytes 405512 | tf_op jit(solution)/shard_map/ppermute | solution.py:26
  25.1 2.9 %collective-permute-start.5 = (bf16[528,128]{1,0:T(8,128)(2,1)S(1)}, bf16[528,128]{1,0:T(8,128)(2,1)S(1)}, u32[]{:S(2)}, u32[]{:S(2)}) collective-permute-start(bf16[528,128]{1,0:T(8,128)(2,1)S(1)} %collective-permute-done.4.refs_0_), channel_id=1, source_target_pairs={{0,1},{1,0},{2,3},{3,2},{4,5},{5,4},{6,7},{7,6},{8,9},{9,8},{10,11... | collective-permute-start | bytes 405512 | tf_op jit(solution)/shard_map/ppermute | solution.py:26
  31.2 1.7 %collective-permute-start.8 = (bf16[128,1024]{1,0:T(8,128)(2,1)S(1)}, bf16[128,1024]{1,0:T(8,128)(2,1)S(1)}, u32[]{:S(2)}, u32[]{:S(2)}) collective-permute-start(bf16[128,1024]{1,0:T(8,128)(2,1)S(1)} %get-tuple-element.15), channel_id=1, source_target_pairs={{0,1},{1,0},{2,3},{3,2},{4,5},{5,4},{6,7},{7,6},{8,9},{9,8},{10,11... | collective-permute-start | bytes 786440 | tf_op jit(solution)/shard_map/ppermute | solution.py:26
  32.9 4.6 %collective-permute-start.9 = (bf16[128,256]{1,0:T(8,128)(2,1)S(1)}, bf16[128,256]{1,0:T(8,128)(2,1)S(1)}, u32[]{:S(2)}, u32[]{:S(2)}) collective-permute-start(bf16[128,256]{1,0:T(8,128)(2,1)S(1)} %get-tuple-element.17), channel_id=1, source_target_pairs={{0,2},{2,0},{4,6},{6,4},{8,10},{10,8},{12,14},{14,12},{16,18},{18,... | collective-permute-start | bytes 196616 | tf_op jit(solution)/shard_map/ppermute | solution.py:26
  33.0 5.8 %collective-permute-start.10 = (bf16[128,256]{1,0:T(8,128)(2,1)S(1)}, bf16[128,256]{1,0:T(8,128)(2,1)S(1)}, u32[]{:S(2)}, u32[]{:S(2)}) collective-permute-start(bf16[128,256]{1,0:T(8,128)(2,1)S(1)} %get-tuple-element.18), channel_id=1, source_target_pairs={{0,4},{2,6},{4,0},{6,2},{8,12},{10,14},{12,8},{14,10},{16,20},{18,... | collective-permute-start | bytes 196616 | tf_op jit(solution)/shard_map/ppermute | solution.py:26
  33.1 5.8 %collective-permute-start.11 = (bf16[128,256]{1,0:T(8,128)(2,1)S(1)}, bf16[128,256]{1,0:T(8,128)(2,1)S(1)}, u32[]{:S(2)}, u32[]{:S(2)}) collective-permute-start(bf16[128,256]{1,0:T(8,128)(2,1)S(1)} %get-tuple-element.19), channel_id=1, source_target_pairs={{0,6},{2,4},{4,2},{6,0},{8,14},{10,12},{12,10},{14,8},{16,22},{18,... | collective-permute-start | bytes 196616 | tf_op jit(solution)/shard_map/ppermute | solution.py:26
  38.9 6.3 %collective-permute-start.14 = (bf16[128,256]{1,0:T(8,128)(2,1)S(1)}, bf16[128,256]{1,0:T(8,128)(2,1)S(1)}, u32[]{:S(2)}, u32[]{:S(2)}) collective-permute-start(bf16[128,256]{1,0:T(8,128)(2,1)S(1)} %add_convert_fusion.1), channel_id=1, source_target_pairs={{0,24},{2,26},{4,28},{6,30},{8,16},{10,18},{12,20},{14,22},{16,8},... | collective-permute-start | bytes 196616 | tf_op jit(solution)/shard_map/ppermute | solution.py:26
  40.2 6.3 %collective-permute-start.13 = (bf16[128,256]{1,0:T(8,128)(2,1)S(1)}, bf16[128,256]{1,0:T(8,128)(2,1)S(1)}, u32[]{:S(2)}, u32[]{:S(2)}) collective-permute-start(bf16[128,256]{1,0:T(8,128)(2,1)S(1)} %add_convert_fusion.1), channel_id=1, source_target_pairs={{0,16},{2,18},{4,20},{6,22},{8,24},{10,26},{12,28},{14,30},{16,0},... | collective-permute-start | bytes 196616 | tf_op jit(solution)/shard_map/ppermute | solution.py:26
  40.2 6.3 %collective-permute-start.12 = (bf16[128,256]{1,0:T(8,128)(2,1)S(1)}, bf16[128,256]{1,0:T(8,128)(2,1)S(1)}, u32[]{:S(2)}, u32[]{:S(2)}) collective-permute-start(bf16[128,256]{1,0:T(8,128)(2,1)S(1)} %add_convert_fusion.1), channel_id=1, source_target_pairs={{0,8},{2,10},{4,12},{6,14},{8,0},{10,2},{12,4},{14,6},{16,24},{18,... | collective-permute-start | bytes 196616 | tf_op jit(solution)/shard_map/ppermute | solution.py:26
  46.6 5.2 %collective-permute-start.17 = (bf16[128,256]{1,0:T(8,128)(2,1)S(1)}, bf16[128,256]{1,0:T(8,128)(2,1)S(1)}, u32[]{:S(2)}, u32[]{:S(2)}) collective-permute-start(bf16[128,256]{1,0:T(8,128)(2,1)S(1)} %add_convert_fusion.refs_0_), channel_id=1, source_target_pairs={{0,6},{2,4},{4,2},{6,0},{8,14},{10,12},{12,10},{14,8},{16,22},{18,... | collective-permute-start | bytes 196616 | tf_op jit(solution)/shard_map/ppermute | solution.py:26
  48.6 4.3 %collective-permute-start.16 = (bf16[128,256]{1,0:T(8,128)(2,1)S(1)}, bf16[128,256]{1,0:T(8,128)(2,1)S(1)}, u32[]{:S(2)}, u32[]{:S(2)}) collective-permute-start(bf16[128,256]{1,0:T(8,128)(2,1)S(1)} %add_convert_fusion.refs_0_), channel_id=1, source_target_pairs={{0,4},{2,6},{4,0},{6,2},{8,12},{10,14},{12,8},{14,10},{16,20},{18,... | collective-permute-start | bytes 196616 | tf_op jit(solution)/shard_map/ppermute | solution.py:26
  49.1 4.3 %collective-permute-start.15 = (bf16[128,256]{1,0:T(8,128)(2,1)S(1)}, bf16[128,256]{1,0:T(8,128)(2,1)S(1)}, u32[]{:S(2)}, u32[]{:S(2)}) collective-permute-start(bf16[128,256]{1,0:T(8,128)(2,1)S(1)} %add_convert_fusion.refs_0_), channel_id=1, source_target_pairs={{0,2},{2,0},{4,6},{6,4},{8,10},{10,8},{12,14},{14,12},{16,18},{18,... | collective-permute-start | bytes 196616 | tf_op jit(solution)/shard_map/ppermute | solution.py:26

commit v3 on v2

--- a/solution.py
+++ b/solution.py
@@ -16,11 +16,6 @@
 f32, bf16 = jnp.float32, jnp.bfloat16
 
 
-def shifted(value, axis, steps):
-    count = lax.axis_size(axis)
-    return lax.ppermute(value, axis, [(s, (s + steps) % count) for s in range(count)])
-
-
 def swapped(value, axis, mask):
     count = lax.axis_size(axis)
     return lax.ppermute(value, axis, [(s, s ^ mask) for s in range(count)])
@@ -39,19 +34,33 @@
 
 
 def project_kernel(
-    features_ref, weight_ref, lse_ref, projected_ref, packed_ref, held, weight, weight_sem, sems
+    features_ref,
+    weight_ref,
+    lse_ref,
+    positive_ref,
+    projected_ref,
+    packed_ref,
+    held,
+    weight,
+    lse,
+    positive,
+    sems,
+    small_sems,
 ):
     rows = held.shape[0]
-    chunk = rows // sems.shape[0]
-    weight_copy = pltpu.make_async_copy(weight_ref, weight, weight_sem)
-    weight_copy.start()
+    chunks = sems.shape[0]
+    chunk = rows // chunks
+    weight_copy = pltpu.make_async_copy(weight_ref, weight, small_sems.at[0])
+    lse_copy = pltpu.make_async_copy(lse_ref, lse, small_sems.at[1])
+    positive_copy = pltpu.make_async_copy(positive_ref, positive, small_sems.at[2])
     copies = []
-    for k in range(sems.shape[0]):
+    for k in range(chunks):
         part = pl.ds(k * chunk, chunk)
-        copy = pltpu.make_async_copy(features_ref.at[part, :], held.at[part, :], sems.at[k])
+        copies.append(
+            pltpu.make_async_copy(features_ref.at[part, :], held.at[part, :], sems.at[k])
+        )
+    for copy in [weight_copy] + copies + [lse_copy, positive_copy]:
         copy.start()
-        copies.append(copy)
-    packed_ref[pl.ds(rows, tail), :] = lse_ref[...]
     weight_copy.wait()
     for k, copy in enumerate(copies):
         part = pl.ds(k * chunk, chunk)
@@ -60,30 +69,45 @@
         magnitude = jnp.sqrt(jnp.sum(projected * projected, axis=-1, keepdims=True) + epsilon)
         projected_ref[part, :] = projected
         packed_ref[part, :] = (projected / magnitude).astype(bf16)
-
-
-def project(features, weight, lse_rows):
+    lse_copy.wait()
+    positive_copy.wait()
+    index = positive[...]
+    packed_ref[pl.ds(rows, tail), :] = jnp.concatenate(
+        [lse[...].astype(f32)]
+        + [((index >> shift) & 127).astype(f32) for shift in (14, 7, 0)],
+        axis=0,
+    ).astype(bf16)
+
+
+def project(features, weight, lse_rows, positive_rows):
     rows, units = features.shape
     width = weight.shape[1]
-    chunks = 4
+    chunks = 8
     hbm = pl.BlockSpec(memory_space=pltpu.HBM)
     return pl.pallas_call(
         project_kernel,
-        in_specs=[hbm, hbm, vmem_spec()],
-        out_specs=[vmem_spec()] * 2,
+        in_specs=[hbm] * 4,
+        out_specs=[vmem_spec()] * 3,
         out_shape=[
             jax.ShapeDtypeStruct((rows, width), f32),
             jax.ShapeDtypeStruct((rows + tail, width), bf16),
+            jax.ShapeDtypeStruct((rows, units), bf16),
         ],
         scratch_shapes=[
-            pltpu.VMEM((rows, units), bf16),
             pltpu.VMEM((units, width), bf16),
-            pltpu.SemaphoreType.DMA,
+            pltpu.VMEM(lse_rows.shape, lse_rows.dtype),
+            pltpu.VMEM(positive_rows.shape, positive_rows.dtype),
             pltpu.SemaphoreType.DMA((chunks,)),
+            pltpu.SemaphoreType.DMA((3,)),
         ],
         compiler_params=small_grant(8),
         name="project",
-    )(features, weight, lse_rows)
+    )(
+        *(
+            pltpu.with_memory_space_constraint(value, pltpu.HBM)
+            for value in (features, weight, lse_rows, positive_rows)
+        )
+    )
 
 
 def as_columns(rows):
@@ -96,12 +120,11 @@
     )
 
 
-def coupled_rows(start, chunk, own_weight, own_positive, base_ref, own_ref, parts, total):
+def coupled_rows(start, chunk, columns, base_ref, own_ref, parts, total):
     rows = own_ref.shape[0] - tail
     column = lax.broadcasted_iota(jnp.int32, (1, lanes), 1)
     own = own_ref[pl.ds(start, chunk), :]
-    weight_i = own_weight[start : start + chunk, :]
-    positive_i = own_positive[start : start + chunk, :]
+    weight_i, positive_i = (values[start : start + chunk, :] for values in columns)
     for which, part in enumerate(parts):
         part_weight = jnp.exp(-part[pl.ds(rows, tail), :].astype(f32))
         for begin in range(0, rows, chunk):
@@ -122,22 +145,29 @@
     return total
 
 
-def own_columns(own_ref, positive_ref):
+def own_columns(own_ref):
     rows = own_ref.shape[0] - tail
-    own_weight = as_columns(jnp.exp(-own_ref[pl.ds(rows, tail), :].astype(f32))[: rows // lanes, :])
-    return own_weight, as_columns(positive_ref[...].astype(f32))
-
-
-def couple_kernel(base_ref, own_ref, positive_ref, *refs):
-    parts, acc_ref = refs[:-1], refs[-1]
-    rows = own_ref.shape[0] - tail
+    count = rows // lanes
+    values = own_ref[pl.ds(rows, tail), :].astype(f32)
+    lse, high, middle, low = (values[k * count : (k + 1) * count, :] for k in range(4))
+    positive = (high * 128.0 + middle) * 128.0 + low
+    return as_columns(jnp.exp(-lse)), as_columns(positive)
+
+
+def couple_kernel(owners, count, base_ref, *refs):
+    owns, parts, before, acc_ref = (
+        refs[:owners], refs[owners : owners + count], refs[owners + count : -1], refs[-1]
+    )
+    rows = owns[0].shape[0] - tail
     chunk = min(256, rows)
-    columns = own_columns(own_ref, positive_ref)
-    for start in range(0, rows, chunk):
-        total = jnp.zeros((chunk, own_ref.shape[1]), f32)
-        acc_ref[pl.ds(start, chunk), :] = coupled_rows(
-            start, chunk, *columns, base_ref, own_ref, parts, total
-        )
+    for k, own_ref in enumerate(owns):
+        columns = own_columns(own_ref)
+        for start in range(0, rows, chunk):
+            part = pl.ds(start, chunk)
+            total = before[0][k, part, :] if before else jnp.zeros((chunk, own_ref.shape[1]), f32)
+            acc_ref[k, part, :] = coupled_rows(
+                start, chunk, columns, base_ref, own_ref, parts, total
+            )
 
 
 def couple_cost(rows, width, count):
@@ -147,31 +177,28 @@
     )
 
 
-def couple(base, own, positive, parts):
-    rows, width = own.shape[0] - tail, own.shape[1]
-    return pl.pallas_call(
-        couple_kernel,
-        in_specs=[smem_spec()] + [vmem_spec()] * (2 + len(parts)),
+def couple(bases, owns, parts, before=()):
+    rows, width = owns[0].shape[0] - tail, owns[0].shape[1]
+    return pl.pallas_call(
+        functools.partial(couple_kernel, len(owns), len(parts)),
+        in_specs=[smem_spec()] + [vmem_spec()] * (len(owns) + len(parts) + len(before)),
         out_specs=vmem_spec(),
-        out_shape=jax.ShapeDtypeStruct((rows, width), f32),
+        out_shape=jax.ShapeDtypeStruct((len(owns), rows, width), f32),
         compiler_params=small_grant(8),
-        cost_estimate=couple_cost(rows, width, len(parts)),
+        cost_estimate=couple_cost(rows, width, len(parts) * len(owns)),
         name="couple",
-    )(base, own, positive, *parts)
-
-
-def finish_kernel(
-    count, shares, base_ref, own_ref, positive_ref, acc_ref, projected_ref, features_ref, *refs
-):
-    parts, grad_ref, half_ref, sends = refs[:count], refs[count], refs[count + 1], refs[count + 2 :]
-    rows = own_ref.shape[0] - tail
+    )(bases, *owns, *parts, *before)
+
+
+def finish_kernel(count, core_ref, acc_ref, projected_ref, features_ref, *refs):
+    received, grad_ref, half_ref, sends = refs[:count], refs[count], refs[count + 1], refs[count + 2 :]
+    rows = projected_ref.shape[0]
     chunk = min(256, rows)
-    columns = own_columns(own_ref, positive_ref)
     for start in range(0, rows, chunk):
         part = pl.ds(start, chunk)
-        total = coupled_rows(
-            start, chunk, *columns, base_ref, own_ref, parts, acc_ref[part, :]
-        )
+        total = acc_ref[0, part, :]
+        for other in received:
+            total = total + other[part, :]
         projected = projected_ref[part, :]
         magnitude = jnp.sqrt(jnp.sum(projected * projected, axis=-1, keepdims=True) + epsilon)
         unit = projected / magnitude
@@ -180,8 +207,7 @@
         grad_ref[part, :] = grad
         half_ref[:, part] = grad.T.astype(bf16)
     for mask, send in enumerate(sends, 1):
-        share = base_ref[count] ^ mask
-        weight_columns(half_ref, features_ref, share, send)
+        weight_columns(half_ref, features_ref, core_ref[0] ^ mask, send)
 
 
 def weight_columns(half_ref, features_ref, share, out_ref):
@@ -194,12 +220,12 @@
         ).astype(out_ref.dtype)
 
 
-def finish(base, own, positive, acc, projected, features, parts, shares):
+def finish(core, acc, projected, features, received, shares):
     rows, width = projected.shape
     units = features.shape[1]
     return pl.pallas_call(
-        functools.partial(finish_kernel, len(parts), shares),
-        in_specs=[smem_spec()] + [vmem_spec()] * (5 + len(parts)),
+        functools.partial(finish_kernel, len(received)),
+        in_specs=[smem_spec()] + [vmem_spec()] * (3 + len(received)),
         out_specs=[vmem_spec()] * (1 + shares),
         out_shape=[
             jax.ShapeDtypeStruct((rows, width), f32),
@@ -207,9 +233,8 @@
         ]
         + [jax.ShapeDtypeStruct((width, units // shares), bf16)] * (shares - 1),
         compiler_params=small_grant(8),
-        cost_estimate=couple_cost(rows, width, len(parts)),
         name="finish",
-    )(base, own, positive, acc, projected, features, *parts)
+    )(core[None], acc, projected, features, *received)
 
 
 def weight_kernel(share_ref, half_ref, features_ref, out_ref):
@@ -288,43 +313,47 @@
     block = lax.axis_index("pair").astype(jnp.int32)
     core = lax.axis_index("dp").astype(jnp.int32)
 
-    lse_rows = jnp.pad(row_lse.reshape(rows // lanes, lanes), ((0, tail - rows // lanes), (0, 0)))
+    lse_rows = row_lse.reshape(rows // lanes, lanes)
     positive_rows = positive.reshape(rows // lanes, lanes)
-    projected, packed = project(features, proj_weight, lse_rows)
-
-    def partner(*offsets):
-        bases, parts = [], []
-        for offset in offsets:
-            part = shifted(packed, "pair", offset)
-            first = jnp.remainder(block - offset, pair_count) * group_rows
-            for mask in range(dp_count):
-                parts.append(part if mask == 0 else swapped(part, "dp", mask))
-                bases.append(first + (core ^ mask) * rows)
-        return jnp.stack(bases + [core]), parts
-
-    far_bases, far_parts = partner(far, -far)
-    near_bases, near_parts = partner(1, -1)
-    acc = couple(far_bases, packed, positive_rows, far_parts)
-    grad_embed, half, *sends = finish(
-        near_bases, packed, positive_rows, acc, projected, features, near_parts, dp_count
-    )
+    projected, packed, held = project(features, proj_weight, lse_rows, positive_rows)
+
+    def pairing(count, stride, odd):
+        size = count // stride
+        return lambda i: (((i // stride + odd) % size ^ 1) + size - odd) % size * stride + i % stride
+
+    def partner(stride, odd):
+        to = pairing(pair_count, stride, odd)
+        part = lax.ppermute(packed, "pair", [(i, to(i)) for i in range(pair_count)])
+        return part, to(block) * group_rows + core * rows
+
+    (near_even, base_a), (far_even, base_b) = partner(1, 0), partner(far, 0)
+    (far_odd, base_c), (near_odd, base_d) = partner(far, 1), partner(1, 1)
+    siblings = [swapped(packed, "dp", mask) for mask in range(1, dp_count)]
+    owns = siblings + [packed]
+    acc = couple(jnp.stack([base_c]), owns, [far_odd])
+    acc = couple(jnp.stack([base_a, base_b]), owns, [near_even, far_even], (acc,))
+    acc_siblings = couple(jnp.stack([base_d]), siblings, [near_odd], (acc,))
+    returned = [swapped(acc_siblings[mask - 1], "dp", mask) for mask in range(1, dp_count)]
+    acc = couple(jnp.stack([base_d]), [packed], [near_odd], (acc[dp_count - 1 :],))
+    grad_embed, half, *sends = finish(core, acc, projected, held, returned, dp_count)
     received = [swapped(send, "dp", mask) for mask, send in enumerate(sends, 1)]
-    mine = weight_term(half, features, core, dp_count)
+    mine = weight_term(half, held, core, dp_count)
 
     ways = 4
     digit = block & (ways - 1)
     keep, *sends = split(digit, mine, received, ways)
-    for s in range(1, ways):
-        keep = keep + swapped(sends[s - 1], "pair", s).astype(f32)
+    moved = [swapped(sends[s - 1], "pair", s) for s in reversed(range(1, ways))]
+    for part in moved:
+        keep = keep + part.astype(f32)
     stride = ways
     while stride < pair_count:
         mine = keep.astype(bf16)
-        near, middle, last = (swapped(mine, "pair", s * stride).astype(f32) for s in (1, 2, 3))
+        last, middle, near = (swapped(mine, "pair", s * stride).astype(f32) for s in (3, 2, 1))
         keep = (mine.astype(f32) + near) + (middle + last)
         stride *= ways
     mine = keep.astype(bf16)
-    quarters = [mine] + [swapped(mine, "pair", s) for s in range(1, ways)]
-    return (grad_embed, join(digit, quarters))
+    moved = [swapped(mine, "pair", s) for s in reversed(range(1, ways))]
+    return (grad_embed, join(digit, [mine] + moved[::-1]))
 
 
 def solution(mesh):

time: 54.6 us -> 50.6 us (0.927)
  local copies, waits for them, and re-layouts: 3.5 us -> 0.02 us
  starting transfers between devices: 23 us -> 20.3 us
  Pallas kernels: 8.89 us -> 11.1 us
    ppermute x14 -> x12, waiting for transfers between devices: 9.67 us -> 13 us  [swapped(): return lax.ppermute(value, axis, [(s, s ^ mask) for s in range(count)])]
    ppermute x4, waiting for transfers between devices: 8.44 us -> 5.26 us  [partner(): part = lax.ppermute(packed, 'pair', [(i, to(i)) for i in range(pair_count)])]
    ppermute x4, starting transfers between devices: 10.8 us -> 7.99 us  [partner(): part = lax.ppermute(packed, 'pair', [(i, to(i)) for i in range(pair_count)])]
    unnamed x8 -> x0, local copies, waits for them, and re-layouts: 2.64 us -> none
    pallas_call x3 -> x6, Pallas kernels: 7.56 us -> 9.77 us  [the longest x4 4.66 us: couple(): pl.pallas_call(functools.partial(couple_kernel, len(owns), len(parts)), i...]
    pad x1 -> x0, local copies, waits for them, and re-layouts: 0.69 us -> none  [body(): jnp.pad(row_lse.reshape(rows // lanes, lanes), ((0, tail - rows // lanes)...]
    ppermute x14 -> x12, starting transfers between devices: 12.2 us -> 12.3 us  [swapped(): return lax.ppermute(value, axis, [(s, s ^ mask) for s in range(count)])]
  transfers between devices with their start and end apart: 18 -> 16, of which waited for: 11 -> 13; matrix products, arithmetic and copies ran while one was open for 0% -> 0% of each run, Pallas kernels for 6% -> 8%
where the time goes in v3:
time: 50.6 us; the launch traced here: 50.5 us
  starting transfers between devices  20.3 us (40%)
  waiting for transfers between devices  18.2 us (36%)
  Pallas kernels  11.1 us (22%)
  between operations  0.72 us (1%)
    ppermute x12, waiting for transfers between devices, swapped(): return lax.ppermute(value, axis, [(s, s ^ mask) for s in range(count)])  13 us
    ppermute x12, starting transfers between devices, swapped(): return lax.ppermute(value, axis, [(s, s ^ mask) for s in range(count)])  12.3 us
    ppermute x4, starting transfers between devices, partner(): part = lax.ppermute(packed, 'pair', [(i, to(i)) for i in range(pair_count)])  7.99 us
    ppermute x4, waiting for transfers between devices, partner(): part = lax.ppermute(packed, 'pair', [(i, to(i)) for i in range(pair_count)])  5.26 us
    pallas_call x4, Pallas kernels, couple(): pl.pallas_call(functools.partial(couple_kernel, len(owns), len(parts)), i...  4.66 us
    pallas_call x1, Pallas kernels, project(): pl.pallas_call(project_kernel, in_specs=[hbm] * 4, out_specs=[vmem_spec()...  4.08 us
    pallas_call x1, Pallas kernels, finish(): pl.pallas_call(functools.partial(finish_kernel, len(received)), in_specs=...  1.03 us
  transfers between devices with their start and end apart: 16, of which 13 were waited for; matrix products, arithmetic and copies ran while one was open for 0% of the time, Pallas kernels for 8%

profile of v3, /device:TPU:0, one launch (start us, length us, event | category | flops | bytes accessed | tf_op | source)
XLA Modules:
  0.0 50.5 jit_solution(10625352254921063666)
XLA Ops:
  0.6 4.1 %project.1 = (f32[512,128]{1,0:T(8,128)S(1)}, bf16[528,128]{1,0:T(8,128)(2,1)S(1)}, bf16[512,2048]{1,0:T(8,128)(2,1)S(1)}) custom-call(bf16[512,2048]{1,0:T(8,128)(2,1)} %features_ref.1, bf16[2048,128]{1,0:T(8,128)(2,1)} %weight_ref.1, bf16[4,128]{1,0:T(4,128)(2,1)} %bitcast.11, s32[4,128]{1,0:T(4,128)} %bitcast.10), custom_call_target="tpu_custom_call" | custom-call | tf_op jit(solution)/shard_map/project/pallas_call | solution.py:87
  4.7 0.5 %collective-permute-start.1 = (bf16[528,128]{1,0:T(8,128)(2,1)S(1)}, bf16[528,128]{1,0:T(8,128)(2,1)S(1)}, u32[]{:S(2)}, u32[]{:S(2)}) collective-permute-start(bf16[528,128]{1,0:T(8,128)(2,1)S(1)} %get-tuple-element.12.refs_1_.refs_0_), channel_id=1, source_target_pairs={{0,1},{1,0},{2,3},{3,2},{4,5},{5,4},{6,7},{7,6},{8,9},{9,8},{10,11... | collective-permute-start | bytes 405512 | tf_op jit(solution)/shard_map/ppermute | solution.py:21
  5.2 4.7 %collective-permute-start.4 = (bf16[528,128]{1,0:T(8,128)(2,1)S(1)}, bf16[528,128]{1,0:T(8,128)(2,1)S(1)}, u32[]{:S(2)}, u32[]{:S(2)}) collective-permute-start(bf16[528,128]{1,0:T(8,128)(2,1)S(1)} %get-tuple-element.12.refs_1_.refs_0_), channel_id=1, source_target_pairs={{0,24},{2,26},{4,28},{6,30},{8,16},{10,18},{12,20},{14,22},{16,8},... | collective-permute-start | bytes 405512 | tf_op jit(solution)/shard_map/ppermute | solution.py:326
  9.9 1.5 %collective-permute-start.2 = (bf16[528,128]{1,0:T(8,128)(2,1)S(1)}, bf16[528,128]{1,0:T(8,128)(2,1)S(1)}, u32[]{:S(2)}, u32[]{:S(2)}) collective-permute-start(bf16[528,128]{1,0:T(8,128)(2,1)S(1)} %get-tuple-element.12.refs_1_.refs_0_), channel_id=1, source_target_pairs={{0,2},{2,0},{4,6},{6,4},{8,10},{10,8},{12,14},{14,12},{16,18},{18,... | collective-permute-start | bytes 405512 | tf_op jit(solution)/shard_map/ppermute | solution.py:326
  11.4 1.8 %collective-permute-start = (bf16[528,128]{1,0:T(8,128)(2,1)S(1)}, bf16[528,128]{1,0:T(8,128)(2,1)S(1)}, u32[]{:S(2)}, u32[]{:S(2)}) collective-permute-start(bf16[528,128]{1,0:T(8,128)(2,1)S(1)} %get-tuple-element.12.refs_1_.refs_0_), channel_id=1, source_target_pairs={{0,30},{2,4},{4,2},{6,8},{8,6},{10,12},{12,10},{14,16},{16,14},{18... | collective-permute-start | bytes 405512 | tf_op jit(solution)/shard_map/ppermute | solution.py:326
  13.3 1.1 %collective-permute-done.4.refs_2_ = bf16[528,128]{1,0:T(8,128)(2,1)S(1)} collective-permute-done((bf16[528,128]{1,0:T(8,128)(2,1)S(1)}, bf16[528,128]{1,0:T(8,128)(2,1)S(1)}, u32[]{:S(2)}, u32[]{:S(2)}) %collective-permute-start.4) | collective-permute-done | bytes 135200 | tf_op jit(solution)/shard_map/ppermute | solution.py:326
  14.4 1.1 %couple.4.refs_4_ = f32[2,512,128]{2,1,0:T(8,128)S(1)} custom-call(s32[1]{0:T(128)} %bitcast.6.base_ref, bf16[528,128]{1,0:T(8,128)(2,1)S(1)} %collective-permute-done.1.refs_0_, bf16[528,128]{1,0:T(8,128)(2,1)S(1)} %get-tuple-element.12.refs_1_.refs_0_, bf16[528,128]{1,0:T(8,128)(2,1)S(1)} %collective-permute-done.4.refs_2_), custom_call_target="tpu_custom_call" | custom-call | flops 268435456 | bytes 262144 | tf_op jit(solution)/shard_map/couple/pallas_call | solution.py:182
  15.5 0.7 %collective-permute-done.2.refs_2_ = bf16[528,128]{1,0:T(8,128)(2,1)S(1)} collective-permute-done((bf16[528,128]{1,0:T(8,128)(2,1)S(1)}, bf16[528,128]{1,0:T(8,128)(2,1)S(1)}, u32[]{:S(2)}, u32[]{:S(2)}) %collective-permute-start.2) | collective-permute-done | bytes 135200 | tf_op jit(solution)/shard_map/ppermute | solution.py:326
  16.2 1.6 %collective-permute-done.3.refs_3_ = bf16[528,128]{1,0:T(8,128)(2,1)S(1)} collective-permute-done((bf16[528,128]{1,0:T(8,128)(2,1)S(1)}, bf16[528,128]{1,0:T(8,128)(2,1)S(1)}, u32[]{:S(2)}, u32[]{:S(2)}) %collective-permute-start.3) | collective-permute-done | bytes 135200 | tf_op jit(solution)/shard_map/ppermute | solution.py:326
  17.9 2.1 %couple.5.refs_2_ = f32[2,512,128]{2,1,0:T(8,128)S(1)} custom-call(s32[2]{0:T(128)S(1)} %pad_add_fusion.base_ref, bf16[528,128]{1,0:T(8,128)(2,1)S(1)} %collective-permute-done.1.refs_0_, bf16[528,128]{1,0:T(8,128)(2,1)S(1)} %get-tuple-element.12.refs_1_.refs_0_, bf16[528,128]{1,0:T(8,128)(2,1)S(1)} %collective-permute-done.2.refs_2_, ...), custom_call_target="tpu_custom_call" | custom-call | flops 536870912 | bytes 262144 | tf_op jit(solution)/shard_map/couple/pallas_call | solution.py:182
  20.0 1.8 %collective-permute-done.refs_1_ = bf16[528,128]{1,0:T(8,128)(2,1)S(1)} collective-permute-done((bf16[528,128]{1,0:T(8,128)(2,1)S(1)}, bf16[528,128]{1,0:T(8,128)(2,1)S(1)}, u32[]{:S(2)}, u32[]{:S(2)}) %collective-permute-start) | collective-permute-done | bytes 135200 | tf_op jit(solution)/shard_map/ppermute | solution.py:326
  21.9 0.7 %couple.7 = f32[1,512,128]{2,1,0:T(8,128)S(1)} custom-call(s32[1]{0:T(128)} %bitcast.1.base_ref, bf16[528,128]{1,0:T(8,128)(2,1)S(1)} %collective-permute-done.1.refs_0_, bf16[528,128]{1,0:T(8,128)(2,1)S(1)} %collective-permute-done.refs_1_, f32[2,512,128]{2,1,0:T(8,128)S(1)} %couple.5.refs_2_), custom_call_target="tpu_custom_call" | custom-call | flops 134217728 | bytes 262144 | tf_op jit(solution)/shard_map/couple/pallas_call | solution.py:182
  22.7 0.7 %couple.6.acc_ref = f32[1,512,128]{2,1,0:T(8,128)S(1)} custom-call(s32[1]{0:T(128)} %bitcast.1.base_ref, bf16[528,128]{1,0:T(8,128)(2,1)S(1)} %get-tuple-element.12.refs_1_.refs_0_, bf16[528,128]{1,0:T(8,128)(2,1)S(1)} %collective-permute-done.refs_1_, f32[1,512,128]{2,1,0:T(8,128)S(1)} %slice.4.refs_2_), custom_call_target="tpu_custom_call" | custom-call | flops 134217728 | bytes 262144 | tf_op jit(solution)/shard_map/couple/pallas_call | solution.py:182
  23.4 0.8 %collective-permute-done.5.refs_0_ = f32[512,128]{1,0:T(8,128)S(1)} collective-permute-done((f32[512,128]{1,0:T(8,128)S(1)}, f32[512,128]{1,0:T(8,128)S(1)}, u32[]{:S(2)}, u32[]{:S(2)}) %collective-permute-start.5) | collective-permute-done | bytes 262176 | tf_op jit(solution)/shard_map/ppermute | solution.py:21
  24.2 1.0 %finish.1 = (f32[512,128]{1,0:T(8,128)}, bf16[128,512]{1,0:T(8,128)(2,1)S(1)}, bf16[128,1024]{1,0:T(8,128)(2,1)S(1)}) custom-call(s32[1]{0:T(128)} %bitcast.core_ref.share_ref, f32[1,512,128]{2,1,0:T(8,128)S(1)} %couple.6.acc_ref, f32[512,128]{1,0:T(8,128)S(1)} %get-tuple-element.13.projected_ref, bf16[512,2048]{1,0:T(8,128)(2,1)S(1)} %get-tuple-element.14.features_ref, ...), custom_call_target="tpu_custom_call" | custom-call | tf_op jit(solution)/shard_map/finish/pallas_call | solution.py:226
  25.3 0.3 weight_term.1.own_ref
  25.7 1.1 %collective-permute-done.6.refs_0_ = bf16[128,1024]{1,0:T(8,128)(2,1)S(1)} collective-permute-done((bf16[128,1024]{1,0:T(8,128)(2,1)S(1)}, bf16[128,1024]{1,0:T(8,128)(2,1)S(1)}, u32[]{:S(2)}, u32[]{:S(2)}) %collective-permute-start.6) | collective-permute-done | bytes 262176 | tf_op jit(solution)/shard_map/ppermute | solution.py:21
  26.8 0.5 %collective-permute-start.7 = (bf16[128,256]{1,0:T(8,128)(2,1)S(1)}, bf16[128,256]{1,0:T(8,128)(2,1)S(1)}, u32[]{:S(2)}, u32[]{:S(2)}) collective-permute-start(bf16[128,256]{1,0:T(8,128)(2,1)S(1)} %get-tuple-element.19), channel_id=1, source_target_pairs={{0,6},{2,4},{4,2},{6,0},{8,14},{10,12},{12,10},{14,8},{16,22},{18,... | collective-permute-start | bytes 196616 | tf_op jit(solution)/shard_map/ppermute | solution.py:21
  27.4 3.0 %collective-permute-start.9 = (bf16[128,256]{1,0:T(8,128)(2,1)S(1)}, bf16[128,256]{1,0:T(8,128)(2,1)S(1)}, u32[]{:S(2)}, u32[]{:S(2)}) collective-permute-start(bf16[128,256]{1,0:T(8,128)(2,1)S(1)} %get-tuple-element.21), channel_id=1, source_target_pairs={{0,2},{2,0},{4,6},{6,4},{8,10},{10,8},{12,14},{14,12},{16,18},{18,... | collective-permute-start | bytes 196616 | tf_op jit(solution)/shard_map/ppermute | solution.py:21
  30.4 2.3 %collective-permute-done.7 = bf16[128,256]{1,0:T(8,128)(2,1)S(1)} collective-permute-done((bf16[128,256]{1,0:T(8,128)(2,1)S(1)}, bf16[128,256]{1,0:T(8,128)(2,1)S(1)}, u32[]{:S(2)}, u32[]{:S(2)}) %collective-permute-start.7) | collective-permute-done | bytes 65568 | tf_op jit(solution)/shard_map/ppermute | solution.py:21
  32.7 1.8 %collective-permute-start.10 = (bf16[128,256]{1,0:T(8,128)(2,1)S(1)}, bf16[128,256]{1,0:T(8,128)(2,1)S(1)}, u32[]{:S(2)}, u32[]{:S(2)}) collective-permute-start(bf16[128,256]{1,0:T(8,128)(2,1)S(1)} %add_convert_fusion.1), channel_id=1, source_target_pairs={{0,8},{2,10},{4,12},{6,14},{8,0},{10,2},{12,4},{14,6},{16,24},{18,... | collective-permute-start | bytes 196616 | tf_op jit(solution)/shard_map/ppermute | solution.py:21
  34.4 1.6 %collective-permute-start.11 = (bf16[128,256]{1,0:T(8,128)(2,1)S(1)}, bf16[128,256]{1,0:T(8,128)(2,1)S(1)}, u32[]{:S(2)}, u32[]{:S(2)}) collective-permute-start(bf16[128,256]{1,0:T(8,128)(2,1)S(1)} %add_convert_fusion.1), channel_id=1, source_target_pairs={{0,16},{2,18},{4,20},{6,22},{8,24},{10,26},{12,28},{14,30},{16,0},... | collective-permute-start | bytes 196616 | tf_op jit(solution)/shard_map/ppermute | solution.py:21
  36.0 1.1 %collective-permute-start.12 = (bf16[128,256]{1,0:T(8,128)(2,1)S(1)}, bf16[128,256]{1,0:T(8,128)(2,1)S(1)}, u32[]{:S(2)}, u32[]{:S(2)}) collective-permute-start(bf16[128,256]{1,0:T(8,128)(2,1)S(1)} %add_convert_fusion.1), channel_id=1, source_target_pairs={{0,24},{2,26},{4,28},{6,30},{8,16},{10,18},{12,20},{14,22},{16,8},... | collective-permute-start | bytes 196616 | tf_op jit(solution)/shard_map/ppermute | solution.py:21
  37.2 3.6 %collective-permute-done.11 = bf16[128,256]{1,0:T(8,128)(2,1)S(1)} collective-permute-done((bf16[128,256]{1,0:T(8,128)(2,1)S(1)}, bf16[128,256]{1,0:T(8,128)(2,1)S(1)}, u32[]{:S(2)}, u32[]{:S(2)}) %collective-permute-start.11) | collective-permute-done | bytes 65568 | tf_op jit(solution)/shard_map/ppermute | solution.py:21
  40.8 1.3 %collective-permute-done.12 = bf16[128,256]{1,0:T(8,128)(2,1)S(1)} collective-permute-done((bf16[128,256]{1,0:T(8,128)(2,1)S(1)}, bf16[128,256]{1,0:T(8,128)(2,1)S(1)}, u32[]{:S(2)}, u32[]{:S(2)}) %collective-permute-start.12) | collective-permute-done | bytes 65568 | tf_op jit(solution)/shard_map/ppermute | solution.py:21
  42.2 1.2 %collective-permute-start.13 = (bf16[128,256]{1,0:T(8,128)(2,1)S(1)}, bf16[128,256]{1,0:T(8,128)(2,1)S(1)}, u32[]{:S(2)}, u32[]{:S(2)}) collective-permute-start(bf16[128,256]{1,0:T(8,128)(2,1)S(1)} %add_convert_fusion.refs_0_), channel_id=1, source_target_pairs={{0,2},{2,0},{4,6},{6,4},{8,10},{10,8},{12,14},{14,12},{16,18},{18,... | collective-permute-start | bytes 196616 | tf_op jit(solution)/shard_map/ppermute | solution.py:21
  43.5 0.9 %collective-permute-start.14 = (bf16[128,256]{1,0:T(8,128)(2,1)S(1)}, bf16[128,256]{1,0:T(8,128)(2,1)S(1)}, u32[]{:S(2)}, u32[]{:S(2)}) collective-permute-start(bf16[128,256]{1,0:T(8,128)(2,1)S(1)} %add_convert_fusion.refs_0_), channel_id=1, source_target_pairs={{0,4},{2,6},{4,0},{6,2},{8,12},{10,14},{12,8},{14,10},{16,20},{18,... | collective-permute-start | bytes 196616 | tf_op jit(solution)/shard_map/ppermute | solution.py:21
  44.4 1.4 %collective-permute-start.15 = (bf16[128,256]{1,0:T(8,128)(2,1)S(1)}, bf16[128,256]{1,0:T(8,128)(2,1)S(1)}, u32[]{:S(2)}, u32[]{:S(2)}) collective-permute-start(bf16[128,256]{1,0:T(8,128)(2,1)S(1)} %add_convert_fusion.refs_0_), channel_id=1, source_target_pairs={{0,6},{2,4},{4,2},{6,0},{8,14},{10,12},{12,10},{14,8},{16,22},{18,... | collective-permute-start | bytes 196616 | tf_op jit(solution)/shard_map/ppermute | solution.py:21
  45.8 0.8 %collective-permute-done.13.refs_1_ = bf16[128,256]{1,0:T(8,128)(2,1)S(1)} collective-permute-done((bf16[128,256]{1,0:T(8,128)(2,1)S(1)}, bf16[128,256]{1,0:T(8,128)(2,1)S(1)}, u32[]{:S(2)}, u32[]{:S(2)}) %collective-permute-start.13) | collective-permute-done | bytes 65568 | tf_op jit(solution)/shard_map/ppermute | solution.py:21
  46.6 1.2 %collective-permute-done.14.refs_2_ = bf16[128,256]{1,0:T(8,128)(2,1)S(1)} collective-permute-done((bf16[128,256]{1,0:T(8,128)(2,1)S(1)}, bf16[128,256]{1,0:T(8,128)(2,1)S(1)}, u32[]{:S(2)}, u32[]{:S(2)}) %collective-permute-start.14) | collective-permute-done | bytes 65568 | tf_op jit(solution)/shard_map/ppermute | solution.py:21
  47.7 1.8 %collective-permute-done.15.refs_3_ = bf16[128,256]{1,0:T(8,128)(2,1)S(1)} collective-permute-done((bf16[128,256]{1,0:T(8,128)(2,1)S(1)}, bf16[128,256]{1,0:T(8,128)(2,1)S(1)}, u32[]{:S(2)}, u32[]{:S(2)}) %collective-permute-start.15) | collective-permute-done | bytes 65568 | tf_op jit(solution)/shard_map/ppermute | solution.py:21
  49.5 0.9 %join.1 = f32[1024,128]{1,0:T(8,128)} custom-call(s32[1]{0:T(128)} %bitcast.8.digit_ref, bf16[128,256]{1,0:T(8,128)(2,1)S(1)} %add_convert_fusion.refs_0_, bf16[128,256]{1,0:T(8,128)(2,1)S(1)} %collective-permute-done.13.refs_1_, bf16[128,256]{1,0:T(8,128)(2,1)S(1)} %collective-permute-done.14.refs_2_, bf16[128,256]{1,0:T(8,128)(2,1)S(1)} %collective-permute-done.15.refs_3_), custom_call_target="tpu_custom_call" | custom-call | tf_op jit(solution)/shard_map/join/pallas_call | solution.py:297
  (13 shorter events, 0.6 us)
Async XLA Ops:
  4.7 8.6 %collective-permute-start.1 = (bf16[528,128]{1,0:T(8,128)(2,1)S(1)}, bf16[528,128]{1,0:T(8,128)(2,1)S(1)}, u32[]{:S(2)}, u32[]{:S(2)}) collective-permute-start(bf16[528,128]{1,0:T(8,128)(2,1)S(1)} %get-tuple-element.12.refs_1_.refs_0_), channel_id=1, source_target_pairs={{0,1},{1,0},{2,3},{3,2},{4,5},{5,4},{6,7},{7,6},{8,9},{9,8},{10,11... | collective-permute-start | bytes 405512 | tf_op jit(solution)/shard_map/ppermute | solution.py:21
  5.2 9.2 %collective-permute-start.4 = (bf16[528,128]{1,0:T(8,128)(2,1)S(1)}, bf16[528,128]{1,0:T(8,128)(2,1)S(1)}, u32[]{:S(2)}, u32[]{:S(2)}) collective-permute-start(bf16[528,128]{1,0:T(8,128)(2,1)S(1)} %get-tuple-element.12.refs_1_.refs_0_), channel_id=1, source_target_pairs={{0,24},{2,26},{4,28},{6,30},{8,16},{10,18},{12,20},{14,22},{16,8},... | collective-permute-start | bytes 405512 | tf_op jit(solution)/shard_map/ppermute | solution.py:326
  9.9 6.3 %collective-permute-start.2 = (bf16[528,128]{1,0:T(8,128)(2,1)S(1)}, bf16[528,128]{1,0:T(8,128)(2,1)S(1)}, u32[]{:S(2)}, u32[]{:S(2)}) collective-permute-start(bf16[528,128]{1,0:T(8,128)(2,1)S(1)} %get-tuple-element.12.refs_1_.refs_0_), channel_id=1, source_target_pairs={{0,2},{2,0},{4,6},{6,4},{8,10},{10,8},{12,14},{14,12},{16,18},{18,... | collective-permute-start | bytes 405512 | tf_op jit(solution)/shard_map/ppermute | solution.py:326
  11.4 6.5 %collective-permute-start.3 = (bf16[528,128]{1,0:T(8,128)(2,1)S(1)}, bf16[528,128]{1,0:T(8,128)(2,1)S(1)}, u32[]{:S(2)}, u32[]{:S(2)}) collective-permute-start(bf16[528,128]{1,0:T(8,128)(2,1)S(1)} %get-tuple-element.12.refs_1_.refs_0_), channel_id=1, source_target_pairs={{0,8},{2,10},{4,12},{6,14},{8,0},{10,2},{12,4},{14,6},{16,24},{18,... | collective-permute-start | bytes 405512 | tf_op jit(solution)/shard_map/ppermute | solution.py:326
  11.4 10.5 %collective-permute-start = (bf16[528,128]{1,0:T(8,128)(2,1)S(1)}, bf16[528,128]{1,0:T(8,128)(2,1)S(1)}, u32[]{:S(2)}, u32[]{:S(2)}) collective-permute-start(bf16[528,128]{1,0:T(8,128)(2,1)S(1)} %get-tuple-element.12.refs_1_.refs_0_), channel_id=1, source_target_pairs={{0,30},{2,4},{4,2},{6,8},{8,6},{10,12},{12,10},{14,16},{16,14},{18... | collective-permute-start | bytes 405512 | tf_op jit(solution)/shard_map/ppermute | solution.py:326
  22.6 1.6 %collective-permute-start.5 = (f32[512,128]{1,0:T(8,128)S(1)}, f32[512,128]{1,0:T(8,128)S(1)}, u32[]{:S(2)}, u32[]{:S(2)}) collective-permute-start(f32[512,128]{1,0:T(8,128)S(1)} %bitcast.9), channel_id=1, source_target_pairs={{0,1},{1,0},{2,3},{3,2},{4,5},{5,4},{6,7},{7,6},{8,9},{9,8},{10,11... | collective-permute-start | bytes 786440 | tf_op jit(solution)/shard_map/ppermute | solution.py:21
  25.2 1.5 %collective-permute-start.6 = (bf16[128,1024]{1,0:T(8,128)(2,1)S(1)}, bf16[128,1024]{1,0:T(8,128)(2,1)S(1)}, u32[]{:S(2)}, u32[]{:S(2)}) collective-permute-start(bf16[128,1024]{1,0:T(8,128)(2,1)S(1)} %get-tuple-element.17), channel_id=1, source_target_pairs={{0,1},{1,0},{2,3},{3,2},{4,5},{5,4},{6,7},{7,6},{8,9},{9,8},{10,11... | collective-permute-start | bytes 786440 | tf_op jit(solution)/shard_map/ppermute | solution.py:21
  26.8 5.8 %collective-permute-start.7 = (bf16[128,256]{1,0:T(8,128)(2,1)S(1)}, bf16[128,256]{1,0:T(8,128)(2,1)S(1)}, u32[]{:S(2)}, u32[]{:S(2)}) collective-permute-start(bf16[128,256]{1,0:T(8,128)(2,1)S(1)} %get-tuple-element.19), channel_id=1, source_target_pairs={{0,6},{2,4},{4,2},{6,0},{8,14},{10,12},{12,10},{14,8},{16,22},{18,... | collective-permute-start | bytes 196616 | tf_op jit(solution)/shard_map/ppermute | solution.py:21
  27.4 5.3 %collective-permute-start.8 = (bf16[128,256]{1,0:T(8,128)(2,1)S(1)}, bf16[128,256]{1,0:T(8,128)(2,1)S(1)}, u32[]{:S(2)}, u32[]{:S(2)}) collective-permute-start(bf16[128,256]{1,0:T(8,128)(2,1)S(1)} %get-tuple-element.20), channel_id=1, source_target_pairs={{0,4},{2,6},{4,0},{6,2},{8,12},{10,14},{12,8},{14,10},{16,20},{18,... | collective-permute-start | bytes 196616 | tf_op jit(solution)/shard_map/ppermute | solution.py:21
  27.4 5.2 %collective-permute-start.9 = (bf16[128,256]{1,0:T(8,128)(2,1)S(1)}, bf16[128,256]{1,0:T(8,128)(2,1)S(1)}, u32[]{:S(2)}, u32[]{:S(2)}) collective-permute-start(bf16[128,256]{1,0:T(8,128)(2,1)S(1)} %get-tuple-element.21), channel_id=1, source_target_pairs={{0,2},{2,0},{4,6},{6,4},{8,10},{10,8},{12,14},{14,12},{16,18},{18,... | collective-permute-start | bytes 196616 | tf_op jit(solution)/shard_map/ppermute | solution.py:21
  32.7 4.5 %collective-permute-start.10 = (bf16[128,256]{1,0:T(8,128)(2,1)S(1)}, bf16[128,256]{1,0:T(8,128)(2,1)S(1)}, u32[]{:S(2)}, u32[]{:S(2)}) collective-permute-start(bf16[128,256]{1,0:T(8,128)(2,1)S(1)} %add_convert_fusion.1), channel_id=1, source_target_pairs={{0,8},{2,10},{4,12},{6,14},{8,0},{10,2},{12,4},{14,6},{16,24},{18,... | collective-permute-start | bytes 196616 | tf_op jit(solution)/shard_map/ppermute | solution.py:21
  34.4 6.4 %collective-permute-start.11 = (bf16[128,256]{1,0:T(8,128)(2,1)S(1)}, bf16[128,256]{1,0:T(8,128)(2,1)S(1)}, u32[]{:S(2)}, u32[]{:S(2)}) collective-permute-start(bf16[128,256]{1,0:T(8,128)(2,1)S(1)} %add_convert_fusion.1), channel_id=1, source_target_pairs={{0,16},{2,18},{4,20},{6,22},{8,24},{10,26},{12,28},{14,30},{16,0},... | collective-permute-start | bytes 196616 | tf_op jit(solution)/shard_map/ppermute | solution.py:21
  36.0 6.2 %collective-permute-start.12 = (bf16[128,256]{1,0:T(8,128)(2,1)S(1)}, bf16[128,256]{1,0:T(8,128)(2,1)S(1)}, u32[]{:S(2)}, u32[]{:S(2)}) collective-permute-start(bf16[128,256]{1,0:T(8,128)(2,1)S(1)} %add_convert_fusion.1), channel_id=1, source_target_pairs={{0,24},{2,26},{4,28},{6,30},{8,16},{10,18},{12,20},{14,22},{16,8},... | collective-permute-start | bytes 196616 | tf_op jit(solution)/shard_map/ppermute | solution.py:21
  42.2 4.3 %collective-permute-start.13 = (bf16[128,256]{1,0:T(8,128)(2,1)S(1)}, bf16[128,256]{1,0:T(8,128)(2,1)S(1)}, u32[]{:S(2)}, u32[]{:S(2)}) collective-permute-start(bf16[128,256]{1,0:T(8,128)(2,1)S(1)} %add_convert_fusion.refs_0_), channel_id=1, source_target_pairs={{0,2},{2,0},{4,6},{6,4},{8,10},{10,8},{12,14},{14,12},{16,18},{18,... | collective-permute-start | bytes 196616 | tf_op jit(solution)/shard_map/ppermute | solution.py:21
  43.5 4.3 %collective-permute-start.14 = (bf16[128,256]{1,0:T(8,128)(2,1)S(1)}, bf16[128,256]{1,0:T(8,128)(2,1)S(1)}, u32[]{:S(2)}, u32[]{:S(2)}) collective-permute-start(bf16[128,256]{1,0:T(8,128)(2,1)S(1)} %add_convert_fusion.refs_0_), channel_id=1, source_target_pairs={{0,4},{2,6},{4,0},{6,2},{8,12},{10,14},{12,8},{14,10},{16,20},{18,... | collective-permute-start | bytes 196616 | tf_op jit(solution)/shard_map/ppermute | solution.py:21
  44.4 5.2 %collective-permute-start.15 = (bf16[128,256]{1,0:T(8,128)(2,1)S(1)}, bf16[128,256]{1,0:T(8,128)(2,1)S(1)}, u32[]{:S(2)}, u32[]{:S(2)}) collective-permute-start(bf16[128,256]{1,0:T(8,128)(2,1)S(1)} %add_convert_fusion.refs_0_), channel_id=1, source_target_pairs={{0,6},{2,4},{4,2},{6,0},{8,14},{10,12},{12,10},{14,8},{16,22},{18,... | collective-permute-start | bytes 196616 | tf_op jit(solution)/shard_map/ppermute | solution.py:21

commit v4 on v3

--- a/solution.py
+++ b/solution.py
@@ -16,9 +16,24 @@
 f32, bf16 = jnp.float32, jnp.bfloat16
 
 
-def swapped(value, axis, mask):
-    count = lax.axis_size(axis)
-    return lax.ppermute(value, axis, [(s, s ^ mask) for s in range(count)])
+def swapped(value, mask):
+    count = lax.axis_size("dp")
+    return lax.ppermute(value, "dp", [(d, d ^ mask) for d in range(count)])
+
+
+def exchanged(value, mask):
+    count = lax.axis_size("pair")
+    return lax.ppermute(value, "pair", [(p, p ^ mask) for p in range(count)])
+
+
+def crossed(value, to):
+    blocks, cores = lax.axis_size("pair"), lax.axis_size("dp")
+    pairs = [
+        (block * cores + core, to(block) * cores + (core ^ 1))
+        for block in range(blocks)
+        for core in range(cores)
+    ]
+    return lax.ppermute(value, ("pair", "dp"), pairs)
 
 
 def vmem_spec():
@@ -82,7 +97,7 @@
 def project(features, weight, lse_rows, positive_rows):
     rows, units = features.shape
     width = weight.shape[1]
-    chunks = 8
+    chunks = 2
     hbm = pl.BlockSpec(memory_space=pltpu.HBM)
     return pl.pallas_call(
         project_kernel,
@@ -287,7 +302,7 @@
 def join_kernel(digit_ref, *refs):
     parts, out_ref = refs[:-1], refs[-1]
     size = parts[0].shape[1]
-    for s, part in enumerate(parts):
+    for s, part in enumerate(reversed(parts)):
         rows = pl.ds(pl.multiple_of((digit_ref[0] ^ s) * size, size), size)
         out_ref[rows, :] = part[...].astype(f32).T
 
@@ -323,37 +338,36 @@
 
     def partner(stride, odd):
         to = pairing(pair_count, stride, odd)
-        part = lax.ppermute(packed, "pair", [(i, to(i)) for i in range(pair_count)])
-        return part, to(block) * group_rows + core * rows
+        return crossed(packed, to), to(block) * group_rows + (core ^ 1) * rows
 
     (near_even, base_a), (far_even, base_b) = partner(1, 0), partner(far, 0)
     (far_odd, base_c), (near_odd, base_d) = partner(far, 1), partner(1, 1)
-    siblings = [swapped(packed, "dp", mask) for mask in range(1, dp_count)]
+    siblings = [swapped(packed, mask) for mask in range(1, dp_count)]
     owns = siblings + [packed]
     acc = couple(jnp.stack([base_c]), owns, [far_odd])
     acc = couple(jnp.stack([base_a, base_b]), owns, [near_even, far_even], (acc,))
     acc_siblings = couple(jnp.stack([base_d]), siblings, [near_odd], (acc,))
-    returned = [swapped(acc_siblings[mask - 1], "dp", mask) for mask in range(1, dp_count)]
+    returned = [swapped(acc_siblings[mask - 1], mask) for mask in range(1, dp_count)]
     acc = couple(jnp.stack([base_d]), [packed], [near_odd], (acc[dp_count - 1 :],))
     grad_embed, half, *sends = finish(core, acc, projected, held, returned, dp_count)
-    received = [swapped(send, "dp", mask) for mask, send in enumerate(sends, 1)]
+    received = [swapped(send, mask) for mask, send in enumerate(sends, 1)]
     mine = weight_term(half, held, core, dp_count)
 
     ways = 4
     digit = block & (ways - 1)
     keep, *sends = split(digit, mine, received, ways)
-    moved = [swapped(sends[s - 1], "pair", s) for s in reversed(range(1, ways))]
+    moved = [exchanged(sends[s - 1], s) for s in reversed(range(1, ways))]
     for part in moved:
         keep = keep + part.astype(f32)
     stride = ways
     while stride < pair_count:
         mine = keep.astype(bf16)
-        last, middle, near = (swapped(mine, "pair", s * stride).astype(f32) for s in (3, 2, 1))
-        keep = (mine.astype(f32) + near) + (middle + last)
+        last, middle, near = (exchanged(mine, s * stride).astype(f32) for s in (3, 2, 1))
+        keep = (last + middle) + (near + mine.astype(f32))
         stride *= ways
     mine = keep.astype(bf16)
-    moved = [swapped(mine, "pair", s) for s in reversed(range(1, ways))]
-    return (grad_embed, join(digit, [mine] + moved[::-1]))
+    moved = [exchanged(mine, s) for s in reversed(range(1, ways))]
+    return (grad_embed, join(digit, moved + [mine]))
 
 
 def solution(mesh):

time: 50.6 us -> 47.7 us (0.943)
  Pallas kernels: 11.1 us -> 9.49 us
  waiting for transfers between devices: 18.2 us -> 17 us
    pallas_call x1, Pallas kernels: 4.08 us -> 2.48 us  [project(): pl.pallas_call(project_kernel, in_specs=[hbm] * 4, out_specs=[vmem_spec()...]
    ppermute x16, waiting for transfers between devices: 18.2 us -> 17 us  [the longest x9 10.2 us: exchanged(): return lax.ppermute(value, 'pair', [(p, p ^ mask) for p in range(count)])]
  transfers between devices with their start and end apart: 16 -> 16, of which waited for: 13 -> 13; matrix products, arithmetic and copies ran while one was open for 0% -> 0% of each run, Pallas kernels for 8% -> 9%
where the time goes in v4:
time: 47.7 us; the launch traced here: 47.5 us
  starting transfers between devices  20.1 us (42%)
  waiting for transfers between devices  17 us (36%)
  Pallas kernels  9.49 us (20%)
  between operations  0.71 us (1%)
    ppermute x9, starting transfers between devices, exchanged(): return lax.ppermute(value, 'pair', [(p, p ^ mask) for p in range(count)])  11.6 us
    ppermute x9, waiting for transfers between devices, exchanged(): return lax.ppermute(value, 'pair', [(p, p ^ mask) for p in range(count)])  10.2 us
    ppermute x4, starting transfers between devices, crossed(): return lax.ppermute(value, ('pair', 'dp'), pairs)  7.43 us
    ppermute x4, waiting for transfers between devices, crossed(): return lax.ppermute(value, ('pair', 'dp'), pairs)  5.35 us
    pallas_call x4, Pallas kernels, couple(): pl.pallas_call(functools.partial(couple_kernel, len(owns), len(parts)), i...  4.65 us
    pallas_call x1, Pallas kernels, project(): pl.pallas_call(project_kernel, in_specs=[hbm] * 4, out_specs=[vmem_spec()...  2.48 us
    ppermute x3, waiting for transfers between devices, swapped(): return lax.ppermute(value, 'dp', [(d, d ^ mask) for d in range(count)])  1.46 us
    ppermute x3, starting transfers between devices, swapped(): return lax.ppermute(value, 'dp', [(d, d ^ mask) for d in range(count)])  1.16 us
  transfers between devices with their start and end apart: 16, of which 13 were waited for; matrix products, arithmetic and copies ran while one was open for 0% of the time, Pallas kernels for 9%

profile of v4, /device:TPU:0, one launch (start us, length us, event | category | flops | bytes accessed | tf_op | source)
XLA Modules:
  0.0 47.5 jit_solution(12875276126193198387)
XLA Ops:
  0.6 2.5 %project.1 = (f32[512,128]{1,0:T(8,128)S(1)}, bf16[528,128]{1,0:T(8,128)(2,1)S(1)}, bf16[512,2048]{1,0:T(8,128)(2,1)S(1)}) custom-call(bf16[512,2048]{1,0:T(8,128)(2,1)} %features_ref.1, bf16[2048,128]{1,0:T(8,128)(2,1)} %weight_ref.1, bf16[4,128]{1,0:T(4,128)(2,1)} %bitcast.11, s32[4,128]{1,0:T(4,128)} %bitcast.10), custom_call_target="tpu_custom_call" | custom-call | tf_op jit(solution)/shard_map/project/pallas_call | solution.py:102
  3.1 0.5 %collective-permute-start.1 = (bf16[528,128]{1,0:T(8,128)(2,1)S(1)}, bf16[528,128]{1,0:T(8,128)(2,1)S(1)}, u32[]{:S(2)}, u32[]{:S(2)}) collective-permute-start(bf16[528,128]{1,0:T(8,128)(2,1)S(1)} %get-tuple-element.12.refs_1_.refs_0_), channel_id=1, source_target_pairs={{0,1},{1,0},{2,3},{3,2},{4,5},{5,4},{6,7},{7,6},{8,9},{9,8},{10,11... | collective-permute-start | bytes 405512 | tf_op jit(solution)/shard_map/ppermute | solution.py:21
  3.6 4.7 %collective-permute-start.4 = (bf16[528,128]{1,0:T(8,128)(2,1)S(1)}, bf16[528,128]{1,0:T(8,128)(2,1)S(1)}, u32[]{:S(2)}, u32[]{:S(2)}) collective-permute-start(bf16[528,128]{1,0:T(8,128)(2,1)S(1)} %get-tuple-element.12.refs_1_.refs_0_), channel_id=1, source_target_pairs={{0,25},{1,24},{2,27},{3,26},{4,29},{5,28},{6,31},{7,30},{8,17},{9,... | collective-permute-start | bytes 405512 | tf_op jit(solution)/shard_map/ppermute | solution.py:36
  8.4 1.2 %collective-permute-start.2 = (bf16[528,128]{1,0:T(8,128)(2,1)S(1)}, bf16[528,128]{1,0:T(8,128)(2,1)S(1)}, u32[]{:S(2)}, u32[]{:S(2)}) collective-permute-start(bf16[528,128]{1,0:T(8,128)(2,1)S(1)} %get-tuple-element.12.refs_1_.refs_0_), channel_id=1, source_target_pairs={{0,3},{1,2},{2,1},{3,0},{4,7},{5,6},{6,5},{7,4},{8,11},{9,10},{10,... | collective-permute-start | bytes 405512 | tf_op jit(solution)/shard_map/ppermute | solution.py:36
  9.5 1.5 %collective-permute-start = (bf16[528,128]{1,0:T(8,128)(2,1)S(1)}, bf16[528,128]{1,0:T(8,128)(2,1)S(1)}, u32[]{:S(2)}, u32[]{:S(2)}) collective-permute-start(bf16[528,128]{1,0:T(8,128)(2,1)S(1)} %get-tuple-element.12.refs_1_.refs_0_), channel_id=1, source_target_pairs={{0,31},{1,30},{2,5},{3,4},{4,3},{5,2},{6,9},{7,8},{8,7},{9,6},{10,... | collective-permute-start | bytes 405512 | tf_op jit(solution)/shard_map/ppermute | solution.py:36
  11.1 1.2 %collective-permute-done.4.refs_2_ = bf16[528,128]{1,0:T(8,128)(2,1)S(1)} collective-permute-done((bf16[528,128]{1,0:T(8,128)(2,1)S(1)}, bf16[528,128]{1,0:T(8,128)(2,1)S(1)}, u32[]{:S(2)}, u32[]{:S(2)}) %collective-permute-start.4) | collective-permute-done | bytes 135200 | tf_op jit(solution)/shard_map/ppermute | solution.py:36
  12.3 1.1 %couple.4.refs_4_ = f32[2,512,128]{2,1,0:T(8,128)S(1)} custom-call(s32[1]{0:T(128)} %bitcast.6.base_ref, bf16[528,128]{1,0:T(8,128)(2,1)S(1)} %collective-permute-done.1.refs_0_, bf16[528,128]{1,0:T(8,128)(2,1)S(1)} %get-tuple-element.12.refs_1_.refs_0_, bf16[528,128]{1,0:T(8,128)(2,1)S(1)} %collective-permute-done.4.refs_2_), custom_call_target="tpu_custom_call" | custom-call | flops 268435456 | bytes 262144 | tf_op jit(solution)/shard_map/couple/pallas_call | solution.py:197
  13.5 0.5 %collective-permute-done.2.refs_2_ = bf16[528,128]{1,0:T(8,128)(2,1)S(1)} collective-permute-done((bf16[528,128]{1,0:T(8,128)(2,1)S(1)}, bf16[528,128]{1,0:T(8,128)(2,1)S(1)}, u32[]{:S(2)}, u32[]{:S(2)}) %collective-permute-start.2) | collective-permute-done | bytes 135200 | tf_op jit(solution)/shard_map/ppermute | solution.py:36
  14.0 1.2 %collective-permute-done.3.refs_3_ = bf16[528,128]{1,0:T(8,128)(2,1)S(1)} collective-permute-done((bf16[528,128]{1,0:T(8,128)(2,1)S(1)}, bf16[528,128]{1,0:T(8,128)(2,1)S(1)}, u32[]{:S(2)}, u32[]{:S(2)}) %collective-permute-start.3) | collective-permute-done | bytes 135200 | tf_op jit(solution)/shard_map/ppermute | solution.py:36
  15.2 2.1 %couple.5.refs_2_ = f32[2,512,128]{2,1,0:T(8,128)S(1)} custom-call(s32[2]{0:T(128)S(1)} %pad_add_fusion.base_ref, bf16[528,128]{1,0:T(8,128)(2,1)S(1)} %collective-permute-done.1.refs_0_, bf16[528,128]{1,0:T(8,128)(2,1)S(1)} %get-tuple-element.12.refs_1_.refs_0_, bf16[528,128]{1,0:T(8,128)(2,1)S(1)} %collective-permute-done.2.refs_2_, ...), custom_call_target="tpu_custom_call" | custom-call | flops 536870912 | bytes 262144 | tf_op jit(solution)/shard_map/couple/pallas_call | solution.py:197
  17.4 2.4 %collective-permute-done.refs_1_ = bf16[528,128]{1,0:T(8,128)(2,1)S(1)} collective-permute-done((bf16[528,128]{1,0:T(8,128)(2,1)S(1)}, bf16[528,128]{1,0:T(8,128)(2,1)S(1)}, u32[]{:S(2)}, u32[]{:S(2)}) %collective-permute-start) | collective-permute-done | bytes 135200 | tf_op jit(solution)/shard_map/ppermute | solution.py:36
  19.8 0.7 %couple.7 = f32[1,512,128]{2,1,0:T(8,128)S(1)} custom-call(s32[1]{0:T(128)} %bitcast.1.base_ref, bf16[528,128]{1,0:T(8,128)(2,1)S(1)} %collective-permute-done.1.refs_0_, bf16[528,128]{1,0:T(8,128)(2,1)S(1)} %collective-permute-done.refs_1_, f32[2,512,128]{2,1,0:T(8,128)S(1)} %couple.5.refs_2_), custom_call_target="tpu_custom_call" | custom-call | flops 134217728 | bytes 262144 | tf_op jit(solution)/shard_map/couple/pallas_call | solution.py:197
  20.5 0.4 collective-permute-start.5
  20.9 0.7 %couple.6.acc_ref = f32[1,512,128]{2,1,0:T(8,128)S(1)} custom-call(s32[1]{0:T(128)} %bitcast.1.base_ref, bf16[528,128]{1,0:T(8,128)(2,1)S(1)} %get-tuple-element.12.refs_1_.refs_0_, bf16[528,128]{1,0:T(8,128)(2,1)S(1)} %collective-permute-done.refs_1_, f32[1,512,128]{2,1,0:T(8,128)S(1)} %slice.4.refs_2_), custom_call_target="tpu_custom_call" | custom-call | flops 134217728 | bytes 262144 | tf_op jit(solution)/shard_map/couple/pallas_call | solution.py:197
  21.6 0.5 %collective-permute-done.5.refs_0_ = f32[512,128]{1,0:T(8,128)S(1)} collective-permute-done((f32[512,128]{1,0:T(8,128)S(1)}, f32[512,128]{1,0:T(8,128)S(1)}, u32[]{:S(2)}, u32[]{:S(2)}) %collective-permute-start.5) | collective-permute-done | bytes 262176 | tf_op jit(solution)/shard_map/ppermute | solution.py:21
  22.1 1.0 %finish.1 = (f32[512,128]{1,0:T(8,128)}, bf16[128,512]{1,0:T(8,128)(2,1)S(1)}, bf16[128,1024]{1,0:T(8,128)(2,1)S(1)}) custom-call(s32[1]{0:T(128)} %bitcast.core_ref.share_ref, f32[1,512,128]{2,1,0:T(8,128)S(1)} %couple.6.acc_ref, f32[512,128]{1,0:T(8,128)S(1)} %get-tuple-element.13.projected_ref, bf16[512,2048]{1,0:T(8,128)(2,1)S(1)} %get-tuple-element.14.features_ref, ...), custom_call_target="tpu_custom_call" | custom-call | tf_op jit(solution)/shard_map/finish/pallas_call | solution.py:241
  23.4 0.3 weight_term.1.own_ref
  23.7 0.9 %collective-permute-done.6.refs_0_ = bf16[128,1024]{1,0:T(8,128)(2,1)S(1)} collective-permute-done((bf16[128,1024]{1,0:T(8,128)(2,1)S(1)}, bf16[128,1024]{1,0:T(8,128)(2,1)S(1)}, u32[]{:S(2)}, u32[]{:S(2)}) %collective-permute-start.6) | collective-permute-done | bytes 262176 | tf_op jit(solution)/shard_map/ppermute | solution.py:21
  24.7 0.8 %collective-permute-start.7 = (bf16[128,256]{1,0:T(8,128)(2,1)S(1)}, bf16[128,256]{1,0:T(8,128)(2,1)S(1)}, u32[]{:S(2)}, u32[]{:S(2)}) collective-permute-start(bf16[128,256]{1,0:T(8,128)(2,1)S(1)} %get-tuple-element.19), channel_id=1, source_target_pairs={{0,6},{2,4},{4,2},{6,0},{8,14},{10,12},{12,10},{14,8},{16,22},{18,... | collective-permute-start | bytes 196616 | tf_op jit(solution)/shard_map/ppermute | solution.py:26
  25.8 2.5 %collective-permute-start.9 = (bf16[128,256]{1,0:T(8,128)(2,1)S(1)}, bf16[128,256]{1,0:T(8,128)(2,1)S(1)}, u32[]{:S(2)}, u32[]{:S(2)}) collective-permute-start(bf16[128,256]{1,0:T(8,128)(2,1)S(1)} %get-tuple-element.21), channel_id=1, source_target_pairs={{0,2},{2,0},{4,6},{6,4},{8,10},{10,8},{12,14},{14,12},{16,18},{18,... | collective-permute-start | bytes 196616 | tf_op jit(solution)/shard_map/ppermute | solution.py:26
  28.3 2.3 %collective-permute-done.7 = bf16[128,256]{1,0:T(8,128)(2,1)S(1)} collective-permute-done((bf16[128,256]{1,0:T(8,128)(2,1)S(1)}, bf16[128,256]{1,0:T(8,128)(2,1)S(1)}, u32[]{:S(2)}, u32[]{:S(2)}) %collective-permute-start.7) | collective-permute-done | bytes 65568 | tf_op jit(solution)/shard_map/ppermute | solution.py:26
  30.9 2.8 %collective-permute-start.10 = (bf16[128,256]{1,0:T(8,128)(2,1)S(1)}, bf16[128,256]{1,0:T(8,128)(2,1)S(1)}, u32[]{:S(2)}, u32[]{:S(2)}) collective-permute-start(bf16[128,256]{1,0:T(8,128)(2,1)S(1)} %add_convert_fusion.1), channel_id=1, source_target_pairs={{0,24},{2,26},{4,28},{6,30},{8,16},{10,18},{12,20},{14,22},{16,8},... | collective-permute-start | bytes 196616 | tf_op jit(solution)/shard_map/ppermute | solution.py:26
  33.7 0.5 collective-permute-start.11
  34.1 1.2 %collective-permute-start.12 = (bf16[128,256]{1,0:T(8,128)(2,1)S(1)}, bf16[128,256]{1,0:T(8,128)(2,1)S(1)}, u32[]{:S(2)}, u32[]{:S(2)}) collective-permute-start(bf16[128,256]{1,0:T(8,128)(2,1)S(1)} %add_convert_fusion.1), channel_id=1, source_target_pairs={{0,8},{2,10},{4,12},{6,14},{8,0},{10,2},{12,4},{14,6},{16,24},{18,... | collective-permute-start | bytes 196616 | tf_op jit(solution)/shard_map/ppermute | solution.py:26
  35.3 1.8 %collective-permute-done.10 = bf16[128,256]{1,0:T(8,128)(2,1)S(1)} collective-permute-done((bf16[128,256]{1,0:T(8,128)(2,1)S(1)}, bf16[128,256]{1,0:T(8,128)(2,1)S(1)}, u32[]{:S(2)}, u32[]{:S(2)}) %collective-permute-start.10) | collective-permute-done | bytes 65568 | tf_op jit(solution)/shard_map/ppermute | solution.py:26
  37.1 2.7 %collective-permute-done.11 = bf16[128,256]{1,0:T(8,128)(2,1)S(1)} collective-permute-done((bf16[128,256]{1,0:T(8,128)(2,1)S(1)}, bf16[128,256]{1,0:T(8,128)(2,1)S(1)}, u32[]{:S(2)}, u32[]{:S(2)}) %collective-permute-start.11) | collective-permute-done | bytes 65568 | tf_op jit(solution)/shard_map/ppermute | solution.py:26
  39.8 1.5 %collective-permute-start.13 = (bf16[128,256]{1,0:T(8,128)(2,1)S(1)}, bf16[128,256]{1,0:T(8,128)(2,1)S(1)}, u32[]{:S(2)}, u32[]{:S(2)}) collective-permute-start(bf16[128,256]{1,0:T(8,128)(2,1)S(1)} %add_convert_fusion.refs_3_), channel_id=1, source_target_pairs={{0,6},{2,4},{4,2},{6,0},{8,14},{10,12},{12,10},{14,8},{16,22},{18,... | collective-permute-start | bytes 196616 | tf_op jit(solution)/shard_map/ppermute | solution.py:26
  41.3 1.0 %collective-permute-start.14 = (bf16[128,256]{1,0:T(8,128)(2,1)S(1)}, bf16[128,256]{1,0:T(8,128)(2,1)S(1)}, u32[]{:S(2)}, u32[]{:S(2)}) collective-permute-start(bf16[128,256]{1,0:T(8,128)(2,1)S(1)} %add_convert_fusion.refs_3_), channel_id=1, source_target_pairs={{0,4},{2,6},{4,0},{6,2},{8,12},{10,14},{12,8},{14,10},{16,20},{18,... | collective-permute-start | bytes 196616 | tf_op jit(solution)/shard_map/ppermute | solution.py:26
  42.3 1.1 %collective-permute-start.15 = (bf16[128,256]{1,0:T(8,128)(2,1)S(1)}, bf16[128,256]{1,0:T(8,128)(2,1)S(1)}, u32[]{:S(2)}, u32[]{:S(2)}) collective-permute-start(bf16[128,256]{1,0:T(8,128)(2,1)S(1)} %add_convert_fusion.refs_3_), channel_id=1, source_target_pairs={{0,2},{2,0},{4,6},{6,4},{8,10},{10,8},{12,14},{14,12},{16,18},{18,... | collective-permute-start | bytes 196616 | tf_op jit(solution)/shard_map/ppermute | solution.py:26
  43.4 2.4 %collective-permute-done.13.refs_0_ = bf16[128,256]{1,0:T(8,128)(2,1)S(1)} collective-permute-done((bf16[128,256]{1,0:T(8,128)(2,1)S(1)}, bf16[128,256]{1,0:T(8,128)(2,1)S(1)}, u32[]{:S(2)}, u32[]{:S(2)}) %collective-permute-start.13) | collective-permute-done | bytes 65568 | tf_op jit(solution)/shard_map/ppermute | solution.py:26
  46.0 0.5 %collective-permute-done.15.refs_2_ = bf16[128,256]{1,0:T(8,128)(2,1)S(1)} collective-permute-done((bf16[128,256]{1,0:T(8,128)(2,1)S(1)}, bf16[128,256]{1,0:T(8,128)(2,1)S(1)}, u32[]{:S(2)}, u32[]{:S(2)}) %collective-permute-start.15) | collective-permute-done | bytes 65568 | tf_op jit(solution)/shard_map/ppermute | solution.py:26
  46.6 0.9 %join.1 = f32[1024,128]{1,0:T(8,128)} custom-call(s32[1]{0:T(128)} %bitcast.8.digit_ref, bf16[128,256]{1,0:T(8,128)(2,1)S(1)} %collective-permute-done.13.refs_0_, bf16[128,256]{1,0:T(8,128)(2,1)S(1)} %collective-permute-done.14.refs_1_, bf16[128,256]{1,0:T(8,128)(2,1)S(1)} %collective-permute-done.15.refs_2_, bf16[128,256]{1,0:T(8,128)(2,1)S(1)} %add_convert_fusion.refs_3_), custom_call_target="tpu_custom_call" | custom-call | tf_op jit(solution)/shard_map/join/pallas_call | solution.py:312
  (13 shorter events, 1.3 us)
Async XLA Ops:
  3.1 8.0 %collective-permute-start.1 = (bf16[528,128]{1,0:T(8,128)(2,1)S(1)}, bf16[528,128]{1,0:T(8,128)(2,1)S(1)}, u32[]{:S(2)}, u32[]{:S(2)}) collective-permute-start(bf16[528,128]{1,0:T(8,128)(2,1)S(1)} %get-tuple-element.12.refs_1_.refs_0_), channel_id=1, source_target_pairs={{0,1},{1,0},{2,3},{3,2},{4,5},{5,4},{6,7},{7,6},{8,9},{9,8},{10,11... | collective-permute-start | bytes 405512 | tf_op jit(solution)/shard_map/ppermute | solution.py:21
  3.6 8.7 %collective-permute-start.4 = (bf16[528,128]{1,0:T(8,128)(2,1)S(1)}, bf16[528,128]{1,0:T(8,128)(2,1)S(1)}, u32[]{:S(2)}, u32[]{:S(2)}) collective-permute-start(bf16[528,128]{1,0:T(8,128)(2,1)S(1)} %get-tuple-element.12.refs_1_.refs_0_), channel_id=1, source_target_pairs={{0,25},{1,24},{2,27},{3,26},{4,29},{5,28},{6,31},{7,30},{8,17},{9,... | collective-permute-start | bytes 405512 | tf_op jit(solution)/shard_map/ppermute | solution.py:36
  8.4 5.6 %collective-permute-start.2 = (bf16[528,128]{1,0:T(8,128)(2,1)S(1)}, bf16[528,128]{1,0:T(8,128)(2,1)S(1)}, u32[]{:S(2)}, u32[]{:S(2)}) collective-permute-start(bf16[528,128]{1,0:T(8,128)(2,1)S(1)} %get-tuple-element.12.refs_1_.refs_0_), channel_id=1, source_target_pairs={{0,3},{1,2},{2,1},{3,0},{4,7},{5,6},{6,5},{7,4},{8,11},{9,10},{10,... | collective-permute-start | bytes 405512 | tf_op jit(solution)/shard_map/ppermute | solution.py:36
  9.5 5.7 %collective-permute-start.3 = (bf16[528,128]{1,0:T(8,128)(2,1)S(1)}, bf16[528,128]{1,0:T(8,128)(2,1)S(1)}, u32[]{:S(2)}, u32[]{:S(2)}) collective-permute-start(bf16[528,128]{1,0:T(8,128)(2,1)S(1)} %get-tuple-element.12.refs_1_.refs_0_), channel_id=1, source_target_pairs={{0,9},{1,8},{2,11},{3,10},{4,13},{5,12},{6,15},{7,14},{8,1},{9,0},... | collective-permute-start | bytes 405512 | tf_op jit(solution)/shard_map/ppermute | solution.py:36
  9.5 10.3 %collective-permute-start = (bf16[528,128]{1,0:T(8,128)(2,1)S(1)}, bf16[528,128]{1,0:T(8,128)(2,1)S(1)}, u32[]{:S(2)}, u32[]{:S(2)}) collective-permute-start(bf16[528,128]{1,0:T(8,128)(2,1)S(1)} %get-tuple-element.12.refs_1_.refs_0_), channel_id=1, source_target_pairs={{0,31},{1,30},{2,5},{3,4},{4,3},{5,2},{6,9},{7,8},{8,7},{9,6},{10,... | collective-permute-start | bytes 405512 | tf_op jit(solution)/shard_map/ppermute | solution.py:36
  20.5 1.6 %collective-permute-start.5 = (f32[512,128]{1,0:T(8,128)S(1)}, f32[512,128]{1,0:T(8,128)S(1)}, u32[]{:S(2)}, u32[]{:S(2)}) collective-permute-start(f32[512,128]{1,0:T(8,128)S(1)} %bitcast.9), channel_id=1, source_target_pairs={{0,1},{1,0},{2,3},{3,2},{4,5},{5,4},{6,7},{7,6},{8,9},{9,8},{10,11... | collective-permute-start | bytes 786440 | tf_op jit(solution)/shard_map/ppermute | solution.py:21
  23.1 1.5 %collective-permute-start.6 = (bf16[128,1024]{1,0:T(8,128)(2,1)S(1)}, bf16[128,1024]{1,0:T(8,128)(2,1)S(1)}, u32[]{:S(2)}, u32[]{:S(2)}) collective-permute-start(bf16[128,1024]{1,0:T(8,128)(2,1)S(1)} %get-tuple-element.17), channel_id=1, source_target_pairs={{0,1},{1,0},{2,3},{3,2},{4,5},{5,4},{6,7},{7,6},{8,9},{9,8},{10,11... | collective-permute-start | bytes 786440 | tf_op jit(solution)/shard_map/ppermute | solution.py:21
  24.7 5.9 %collective-permute-start.7 = (bf16[128,256]{1,0:T(8,128)(2,1)S(1)}, bf16[128,256]{1,0:T(8,128)(2,1)S(1)}, u32[]{:S(2)}, u32[]{:S(2)}) collective-permute-start(bf16[128,256]{1,0:T(8,128)(2,1)S(1)} %get-tuple-element.19), channel_id=1, source_target_pairs={{0,6},{2,4},{4,2},{6,0},{8,14},{10,12},{12,10},{14,8},{16,22},{18,... | collective-permute-start | bytes 196616 | tf_op jit(solution)/shard_map/ppermute | solution.py:26
  25.5 5.3 %collective-permute-start.8 = (bf16[128,256]{1,0:T(8,128)(2,1)S(1)}, bf16[128,256]{1,0:T(8,128)(2,1)S(1)}, u32[]{:S(2)}, u32[]{:S(2)}) collective-permute-start(bf16[128,256]{1,0:T(8,128)(2,1)S(1)} %get-tuple-element.20), channel_id=1, source_target_pairs={{0,4},{2,6},{4,0},{6,2},{8,12},{10,14},{12,8},{14,10},{16,20},{18,... | collective-permute-start | bytes 196616 | tf_op jit(solution)/shard_map/ppermute | solution.py:26
  25.8 5.0 %collective-permute-start.9 = (bf16[128,256]{1,0:T(8,128)(2,1)S(1)}, bf16[128,256]{1,0:T(8,128)(2,1)S(1)}, u32[]{:S(2)}, u32[]{:S(2)}) collective-permute-start(bf16[128,256]{1,0:T(8,128)(2,1)S(1)} %get-tuple-element.21), channel_id=1, source_target_pairs={{0,2},{2,0},{4,6},{6,4},{8,10},{10,8},{12,14},{14,12},{16,18},{18,... | collective-permute-start | bytes 196616 | tf_op jit(solution)/shard_map/ppermute | solution.py:26
  30.9 6.2 %collective-permute-start.10 = (bf16[128,256]{1,0:T(8,128)(2,1)S(1)}, bf16[128,256]{1,0:T(8,128)(2,1)S(1)}, u32[]{:S(2)}, u32[]{:S(2)}) collective-permute-start(bf16[128,256]{1,0:T(8,128)(2,1)S(1)} %add_convert_fusion.1), channel_id=1, source_target_pairs={{0,24},{2,26},{4,28},{6,30},{8,16},{10,18},{12,20},{14,22},{16,8},... | collective-permute-start | bytes 196616 | tf_op jit(solution)/shard_map/ppermute | solution.py:26
  33.7 6.1 %collective-permute-start.11 = (bf16[128,256]{1,0:T(8,128)(2,1)S(1)}, bf16[128,256]{1,0:T(8,128)(2,1)S(1)}, u32[]{:S(2)}, u32[]{:S(2)}) collective-permute-start(bf16[128,256]{1,0:T(8,128)(2,1)S(1)} %add_convert_fusion.1), channel_id=1, source_target_pairs={{0,16},{2,18},{4,20},{6,22},{8,24},{10,26},{12,28},{14,30},{16,0},... | collective-permute-start | bytes 196616 | tf_op jit(solution)/shard_map/ppermute | solution.py:26
  34.1 5.7 %collective-permute-start.12 = (bf16[128,256]{1,0:T(8,128)(2,1)S(1)}, bf16[128,256]{1,0:T(8,128)(2,1)S(1)}, u32[]{:S(2)}, u32[]{:S(2)}) collective-permute-start(bf16[128,256]{1,0:T(8,128)(2,1)S(1)} %add_convert_fusion.1), channel_id=1, source_target_pairs={{0,8},{2,10},{4,12},{6,14},{8,0},{10,2},{12,4},{14,6},{16,24},{18,... | collective-permute-start | bytes 196616 | tf_op jit(solution)/shard_map/ppermute | solution.py:26
  39.8 6.0 %collective-permute-start.13 = (bf16[128,256]{1,0:T(8,128)(2,1)S(1)}, bf16[128,256]{1,0:T(8,128)(2,1)S(1)}, u32[]{:S(2)}, u32[]{:S(2)}) collective-permute-start(bf16[128,256]{1,0:T(8,128)(2,1)S(1)} %add_convert_fusion.refs_3_), channel_id=1, source_target_pairs={{0,6},{2,4},{4,2},{6,0},{8,14},{10,12},{12,10},{14,8},{16,22},{18,... | collective-permute-start | bytes 196616 | tf_op jit(solution)/shard_map/ppermute | solution.py:26
  41.3 4.7 %collective-permute-start.14 = (bf16[128,256]{1,0:T(8,128)(2,1)S(1)}, bf16[128,256]{1,0:T(8,128)(2,1)S(1)}, u32[]{:S(2)}, u32[]{:S(2)}) collective-permute-start(bf16[128,256]{1,0:T(8,128)(2,1)S(1)} %add_convert_fusion.refs_3_), channel_id=1, source_target_pairs={{0,4},{2,6},{4,0},{6,2},{8,12},{10,14},{12,8},{14,10},{16,20},{18,... | collective-permute-start | bytes 196616 | tf_op jit(solution)/shard_map/ppermute | solution.py:26
  42.3 4.3 %collective-permute-start.15 = (bf16[128,256]{1,0:T(8,128)(2,1)S(1)}, bf16[128,256]{1,0:T(8,128)(2,1)S(1)}, u32[]{:S(2)}, u32[]{:S(2)}) collective-permute-start(bf16[128,256]{1,0:T(8,128)(2,1)S(1)} %add_convert_fusion.refs_3_), channel_id=1, source_target_pairs={{0,2},{2,0},{4,6},{6,4},{8,10},{10,8},{12,14},{14,12},{16,18},{18,... | collective-permute-start | bytes 196616 | tf_op jit(solution)/shard_map/ppermute | solution.py:26

commit v5 on v4

--- a/solution.py
+++ b/solution.py
@@ -135,20 +135,21 @@
     )
 
 
-def coupled_rows(start, chunk, columns, base_ref, own_ref, parts, total):
+def coupled_rows(columns, base_ref, own_ref, parts, total):
     rows = own_ref.shape[0] - tail
+    step = min(256, rows)
     column = lax.broadcasted_iota(jnp.int32, (1, lanes), 1)
-    own = own_ref[pl.ds(start, chunk), :]
-    weight_i, positive_i = (values[start : start + chunk, :] for values in columns)
+    own = own_ref[pl.ds(0, rows), :]
+    weight_i, positive_i = columns
     for which, part in enumerate(parts):
         part_weight = jnp.exp(-part[pl.ds(rows, tail), :].astype(f32))
-        for begin in range(0, rows, chunk):
-            other = part[pl.ds(begin, chunk), :]
+        for begin in range(0, rows, step):
+            other = part[pl.ds(begin, step), :]
             cosine = lax.dot_general(
                 own, other, (((1,), (1,)), ((), ())), preferred_element_type=f32
             )
             pieces = []
-            for lane in range(0, chunk, lanes):
+            for lane in range(0, step, lanes):
                 k = (begin + lane) // lanes
                 grown = jnp.exp2(cosine[:, lane : lane + lanes] * exponent_scale)
                 ids = (column + (base_ref[which] + (begin + lane))).astype(f32)
@@ -174,15 +175,10 @@
         refs[:owners], refs[owners : owners + count], refs[owners + count : -1], refs[-1]
     )
     rows = owns[0].shape[0] - tail
-    chunk = min(256, rows)
     for k, own_ref in enumerate(owns):
         columns = own_columns(own_ref)
-        for start in range(0, rows, chunk):
-            part = pl.ds(start, chunk)
-            total = before[0][k, part, :] if before else jnp.zeros((chunk, own_ref.shape[1]), f32)
-            acc_ref[k, part, :] = coupled_rows(
-                start, chunk, columns, base_ref, own_ref, parts, total
-            )
+        total = before[0][k] if before else jnp.zeros((rows, own_ref.shape[1]), f32)
+        acc_ref[k] = coupled_rows(columns, base_ref, own_ref, parts, total)
 
 
 def couple_cost(rows, width, count):
@@ -243,7 +239,7 @@
         in_specs=[smem_spec()] + [vmem_spec()] * (3 + len(received)),
         out_specs=[vmem_spec()] * (1 + shares),
         out_shape=[
-            jax.ShapeDtypeStruct((rows, width), f32),
+            pltpu.VMEM((rows, width), f32),
             jax.ShapeDtypeStruct((width, rows), bf16),
         ]
         + [jax.ShapeDtypeStruct((width, units // shares), bf16)] * (shares - 1),

time: 47.7 us -> 47.2 us (0.990)
  Pallas kernels: 9.49 us -> 8.41 us
  local copies, waits for them, and re-layouts: 0.02 us -> 0.72 us
    ppermute x9, waiting for transfers between devices: 10.2 us -> 9.49 us  [exchanged(): return lax.ppermute(value, 'pair', [(p, p ^ mask) for p in range(count)])]
    unnamed x0 -> x1, local copies, waits for them, and re-layouts: none -> 0.7 us
    pallas_call x4, Pallas kernels: 4.65 us -> 3.98 us  [couple(): pl.pallas_call(functools.partial(couple_kernel, len(owns), len(parts)), i...]
  transfers between devices with their start and end apart: 16 -> 16, of which waited for: 13 -> 13; matrix products, arithmetic and copies ran while one was open for 0% -> 2% of each run, Pallas kernels for 9% -> 8%
where the time goes in v5:
time: 47.2 us; the launch traced here: 47 us
  starting transfers between devices  20.2 us (43%)
  waiting for transfers between devices  16.8 us (36%)
  Pallas kernels  8.41 us (18%)
  local copies, waits for them, and re-layouts  0.72 us (2%)
  between operations  0.7 us (1%)
    ppermute x9, starting transfers between devices, exchanged(): return lax.ppermute(value, 'pair', [(p, p ^ mask) for p in range(count)])  11.6 us
    ppermute x9, waiting for transfers between devices, exchanged(): return lax.ppermute(value, 'pair', [(p, p ^ mask) for p in range(count)])  9.49 us
    ppermute x4, starting transfers between devices, crossed(): return lax.ppermute(value, ('pair', 'dp'), pairs)  7.43 us
    ppermute x4, waiting for transfers between devices, crossed(): return lax.ppermute(value, ('pair', 'dp'), pairs)  5.75 us
    pallas_call x4, Pallas kernels, couple(): pl.pallas_call(functools.partial(couple_kernel, len(owns), len(parts)), i...  3.98 us
    pallas_call x1, Pallas kernels, project(): pl.pallas_call(project_kernel, in_specs=[hbm] * 4, out_specs=[vmem_spec()...  2.48 us
    ppermute x3, waiting for transfers between devices, swapped(): return lax.ppermute(value, 'dp', [(d, d ^ mask) for d in range(count)])  1.6 us
    ppermute x3, starting transfers between devices, swapped(): return lax.ppermute(value, 'dp', [(d, d ^ mask) for d in range(count)])  1.22 us
  transfers between devices with their start and end apart: 16, of which 13 were waited for; matrix products, arithmetic and copies ran while one was open for 2% of the time, Pallas kernels for 8%

profile of v5, /device:TPU:0, one launch (start us, length us, event | category | flops | bytes accessed | tf_op | source)
XLA Modules:
  0.0 47.0 jit_solution(2305011726823205908)
XLA Ops:
  0.6 2.5 %project.1 = (f32[512,128]{1,0:T(8,128)S(1)}, bf16[528,128]{1,0:T(8,128)(2,1)S(1)}, bf16[512,2048]{1,0:T(8,128)(2,1)S(1)}) custom-call(bf16[512,2048]{1,0:T(8,128)(2,1)} %features_ref.1, bf16[2048,128]{1,0:T(8,128)(2,1)} %weight_ref.1, bf16[4,128]{1,0:T(4,128)(2,1)} %bitcast.11, s32[4,128]{1,0:T(4,128)} %bitcast.10), custom_call_target="tpu_custom_call" | custom-call | tf_op jit(solution)/shard_map/project/pallas_call | solution.py:102
  3.1 0.5 %collective-permute-start.1 = (bf16[528,128]{1,0:T(8,128)(2,1)S(1)}, bf16[528,128]{1,0:T(8,128)(2,1)S(1)}, u32[]{:S(2)}, u32[]{:S(2)}) collective-permute-start(bf16[528,128]{1,0:T(8,128)(2,1)S(1)} %get-tuple-element.12.refs_1_.refs_0_), channel_id=1, source_target_pairs={{0,1},{1,0},{2,3},{3,2},{4,5},{5,4},{6,7},{7,6},{8,9},{9,8},{10,11... | collective-permute-start | bytes 405512 | tf_op jit(solution)/shard_map/ppermute | solution.py:21
  3.6 4.7 %collective-permute-start.4 = (bf16[528,128]{1,0:T(8,128)(2,1)S(1)}, bf16[528,128]{1,0:T(8,128)(2,1)S(1)}, u32[]{:S(2)}, u32[]{:S(2)}) collective-permute-start(bf16[528,128]{1,0:T(8,128)(2,1)S(1)} %get-tuple-element.12.refs_1_.refs_0_), channel_id=1, source_target_pairs={{0,25},{1,24},{2,27},{3,26},{4,29},{5,28},{6,31},{7,30},{8,17},{9,... | collective-permute-start | bytes 405512 | tf_op jit(solution)/shard_map/ppermute | solution.py:36
  8.4 1.2 %collective-permute-start.2 = (bf16[528,128]{1,0:T(8,128)(2,1)S(1)}, bf16[528,128]{1,0:T(8,128)(2,1)S(1)}, u32[]{:S(2)}, u32[]{:S(2)}) collective-permute-start(bf16[528,128]{1,0:T(8,128)(2,1)S(1)} %get-tuple-element.12.refs_1_.refs_0_), channel_id=1, source_target_pairs={{0,3},{1,2},{2,1},{3,0},{4,7},{5,6},{6,5},{7,4},{8,11},{9,10},{10,... | collective-permute-start | bytes 405512 | tf_op jit(solution)/shard_map/ppermute | solution.py:36
  9.5 1.5 %collective-permute-start = (bf16[528,128]{1,0:T(8,128)(2,1)S(1)}, bf16[528,128]{1,0:T(8,128)(2,1)S(1)}, u32[]{:S(2)}, u32[]{:S(2)}) collective-permute-start(bf16[528,128]{1,0:T(8,128)(2,1)S(1)} %get-tuple-element.12.refs_1_.refs_0_), channel_id=1, source_target_pairs={{0,31},{1,30},{2,5},{3,4},{4,3},{5,2},{6,9},{7,8},{8,7},{9,6},{10,... | collective-permute-start | bytes 405512 | tf_op jit(solution)/shard_map/ppermute | solution.py:36
  11.1 1.2 %collective-permute-done.4.refs_2_ = bf16[528,128]{1,0:T(8,128)(2,1)S(1)} collective-permute-done((bf16[528,128]{1,0:T(8,128)(2,1)S(1)}, bf16[528,128]{1,0:T(8,128)(2,1)S(1)}, u32[]{:S(2)}, u32[]{:S(2)}) %collective-permute-start.4) | collective-permute-done | bytes 135200 | tf_op jit(solution)/shard_map/ppermute | solution.py:36
  12.3 1.0 %couple.4.refs_4_ = f32[2,512,128]{2,1,0:T(8,128)S(1)} custom-call(s32[1]{0:T(128)} %bitcast.6.base_ref, bf16[528,128]{1,0:T(8,128)(2,1)S(1)} %collective-permute-done.1.refs_0_, bf16[528,128]{1,0:T(8,128)(2,1)S(1)} %get-tuple-element.12.refs_1_.refs_0_, bf16[528,128]{1,0:T(8,128)(2,1)S(1)} %collective-permute-done.4.refs_2_), custom_call_target="tpu_custom_call" | custom-call | flops 268435456 | bytes 262144 | tf_op jit(solution)/shard_map/couple/pallas_call | solution.py:193
  13.3 0.7 %collective-permute-done.2.refs_2_ = bf16[528,128]{1,0:T(8,128)(2,1)S(1)} collective-permute-done((bf16[528,128]{1,0:T(8,128)(2,1)S(1)}, bf16[528,128]{1,0:T(8,128)(2,1)S(1)}, u32[]{:S(2)}, u32[]{:S(2)}) %collective-permute-start.2) | collective-permute-done | bytes 135200 | tf_op jit(solution)/shard_map/ppermute | solution.py:36
  14.0 1.2 %collective-permute-done.3.refs_3_ = bf16[528,128]{1,0:T(8,128)(2,1)S(1)} collective-permute-done((bf16[528,128]{1,0:T(8,128)(2,1)S(1)}, bf16[528,128]{1,0:T(8,128)(2,1)S(1)}, u32[]{:S(2)}, u32[]{:S(2)}) %collective-permute-start.3) | collective-permute-done | bytes 135200 | tf_op jit(solution)/shard_map/ppermute | solution.py:36
  15.2 1.9 %couple.5.refs_2_ = f32[2,512,128]{2,1,0:T(8,128)S(1)} custom-call(s32[2]{0:T(128)S(1)} %pad_add_fusion.base_ref, bf16[528,128]{1,0:T(8,128)(2,1)S(1)} %collective-permute-done.1.refs_0_, bf16[528,128]{1,0:T(8,128)(2,1)S(1)} %get-tuple-element.12.refs_1_.refs_0_, bf16[528,128]{1,0:T(8,128)(2,1)S(1)} %collective-permute-done.2.refs_2_, ...), custom_call_target="tpu_custom_call" | custom-call | flops 536870912 | bytes 262144 | tf_op jit(solution)/shard_map/couple/pallas_call | solution.py:193
  17.1 2.7 %collective-permute-done.refs_1_ = bf16[528,128]{1,0:T(8,128)(2,1)S(1)} collective-permute-done((bf16[528,128]{1,0:T(8,128)(2,1)S(1)}, bf16[528,128]{1,0:T(8,128)(2,1)S(1)}, u32[]{:S(2)}, u32[]{:S(2)}) %collective-permute-start) | collective-permute-done | bytes 135200 | tf_op jit(solution)/shard_map/ppermute | solution.py:36
  19.8 0.5 %couple.7 = f32[1,512,128]{2,1,0:T(8,128)S(1)} custom-call(s32[1]{0:T(128)} %bitcast.1.base_ref, bf16[528,128]{1,0:T(8,128)(2,1)S(1)} %collective-permute-done.1.refs_0_, bf16[528,128]{1,0:T(8,128)(2,1)S(1)} %collective-permute-done.refs_1_, f32[2,512,128]{2,1,0:T(8,128)S(1)} %couple.5.refs_2_), custom_call_target="tpu_custom_call" | custom-call | flops 134217728 | bytes 262144 | tf_op jit(solution)/shard_map/couple/pallas_call | solution.py:193
  20.7 0.5 %couple.6.acc_ref = f32[1,512,128]{2,1,0:T(8,128)S(1)} custom-call(s32[1]{0:T(128)} %bitcast.1.base_ref, bf16[528,128]{1,0:T(8,128)(2,1)S(1)} %get-tuple-element.12.refs_1_.refs_0_, bf16[528,128]{1,0:T(8,128)(2,1)S(1)} %collective-permute-done.refs_1_, f32[1,512,128]{2,1,0:T(8,128)S(1)} %slice.4.refs_2_), custom_call_target="tpu_custom_call" | custom-call | flops 134217728 | bytes 262144 | tf_op jit(solution)/shard_map/couple/pallas_call | solution.py:193
  21.3 0.7 %collective-permute-done.5.refs_0_ = f32[512,128]{1,0:T(8,128)S(1)} collective-permute-done((f32[512,128]{1,0:T(8,128)S(1)}, f32[512,128]{1,0:T(8,128)S(1)}, u32[]{:S(2)}, u32[]{:S(2)}) %collective-permute-start.5) | collective-permute-done | bytes 262176 | tf_op jit(solution)/shard_map/ppermute | solution.py:21
  21.9 0.6 %finish.1 = (f32[512,128]{1,0:T(8,128)S(1)}, bf16[128,512]{1,0:T(8,128)(2,1)S(1)}, bf16[128,1024]{1,0:T(8,128)(2,1)S(1)}) custom-call(s32[1]{0:T(128)} %bitcast.core_ref.share_ref, f32[1,512,128]{2,1,0:T(8,128)S(1)} %couple.6.acc_ref, f32[512,128]{1,0:T(8,128)S(1)} %get-tuple-element.13.projected_ref, bf16[512,2048]{1,0:T(8,128)(2,1)S(1)} %get-tuple-element.14.features_ref, ...), custom_call_target="tpu_custom_call" | custom-call | tf_op jit(solution)/shard_map/finish/pallas_call | solution.py:237
  23.3 0.9 %collective-permute-done.6.refs_0_ = bf16[128,1024]{1,0:T(8,128)(2,1)S(1)} collective-permute-done((bf16[128,1024]{1,0:T(8,128)(2,1)S(1)}, bf16[128,1024]{1,0:T(8,128)(2,1)S(1)}, u32[]{:S(2)}, u32[]{:S(2)}) %collective-permute-start.6) | collective-permute-done | bytes 262176 | tf_op jit(solution)/shard_map/ppermute | solution.py:21
  24.3 0.7 %collective-permute-start.7 = (bf16[128,256]{1,0:T(8,128)(2,1)S(1)}, bf16[128,256]{1,0:T(8,128)(2,1)S(1)}, u32[]{:S(2)}, u32[]{:S(2)}) collective-permute-start(bf16[128,256]{1,0:T(8,128)(2,1)S(1)} %get-tuple-element.19), channel_id=1, source_target_pairs={{0,6},{2,4},{4,2},{6,0},{8,14},{10,12},{12,10},{14,8},{16,22},{18,... | collective-permute-start | bytes 196616 | tf_op jit(solution)/shard_map/ppermute | solution.py:26
  24.9 0.4 collective-permute-start.8
  25.3 2.5 %collective-permute-start.9 = (bf16[128,256]{1,0:T(8,128)(2,1)S(1)}, bf16[128,256]{1,0:T(8,128)(2,1)S(1)}, u32[]{:S(2)}, u32[]{:S(2)}) collective-permute-start(bf16[128,256]{1,0:T(8,128)(2,1)S(1)} %get-tuple-element.21), channel_id=1, source_target_pairs={{0,2},{2,0},{4,6},{6,4},{8,10},{10,8},{12,14},{14,12},{16,18},{18,... | collective-permute-start | bytes 196616 | tf_op jit(solution)/shard_map/ppermute | solution.py:26
  27.8 2.3 %collective-permute-done.7 = bf16[128,256]{1,0:T(8,128)(2,1)S(1)} collective-permute-done((bf16[128,256]{1,0:T(8,128)(2,1)S(1)}, bf16[128,256]{1,0:T(8,128)(2,1)S(1)}, u32[]{:S(2)}, u32[]{:S(2)}) %collective-permute-start.7) | collective-permute-done | bytes 65568 | tf_op jit(solution)/shard_map/ppermute | solution.py:26
  30.3 2.9 %collective-permute-start.10 = (bf16[128,256]{1,0:T(8,128)(2,1)S(1)}, bf16[128,256]{1,0:T(8,128)(2,1)S(1)}, u32[]{:S(2)}, u32[]{:S(2)}) collective-permute-start(bf16[128,256]{1,0:T(8,128)(2,1)S(1)} %add_convert_fusion.1), channel_id=1, source_target_pairs={{0,24},{2,26},{4,28},{6,30},{8,16},{10,18},{12,20},{14,22},{16,8},... | collective-permute-start | bytes 196616 | tf_op jit(solution)/shard_map/ppermute | solution.py:26
  33.4 1.3 %collective-permute-start.12 = (bf16[128,256]{1,0:T(8,128)(2,1)S(1)}, bf16[128,256]{1,0:T(8,128)(2,1)S(1)}, u32[]{:S(2)}, u32[]{:S(2)}) collective-permute-start(bf16[128,256]{1,0:T(8,128)(2,1)S(1)} %add_convert_fusion.1), channel_id=1, source_target_pairs={{0,8},{2,10},{4,12},{6,14},{8,0},{10,2},{12,4},{14,6},{16,24},{18,... | collective-permute-start | bytes 196616 | tf_op jit(solution)/shard_map/ppermute | solution.py:26
  34.8 1.8 %collective-permute-done.10 = bf16[128,256]{1,0:T(8,128)(2,1)S(1)} collective-permute-done((bf16[128,256]{1,0:T(8,128)(2,1)S(1)}, bf16[128,256]{1,0:T(8,128)(2,1)S(1)}, u32[]{:S(2)}, u32[]{:S(2)}) %collective-permute-start.10) | collective-permute-done | bytes 65568 | tf_op jit(solution)/shard_map/ppermute | solution.py:26
  36.6 2.5 %collective-permute-done.11 = bf16[128,256]{1,0:T(8,128)(2,1)S(1)} collective-permute-done((bf16[128,256]{1,0:T(8,128)(2,1)S(1)}, bf16[128,256]{1,0:T(8,128)(2,1)S(1)}, u32[]{:S(2)}, u32[]{:S(2)}) %collective-permute-start.11) | collective-permute-done | bytes 65568 | tf_op jit(solution)/shard_map/ppermute | solution.py:26
  39.1 1.7 %collective-permute-start.13 = (bf16[128,256]{1,0:T(8,128)(2,1)S(1)}, bf16[128,256]{1,0:T(8,128)(2,1)S(1)}, u32[]{:S(2)}, u32[]{:S(2)}) collective-permute-start(bf16[128,256]{1,0:T(8,128)(2,1)S(1)} %add_convert_fusion.refs_3_), channel_id=1, source_target_pairs={{0,6},{2,4},{4,2},{6,0},{8,14},{10,12},{12,10},{14,8},{16,22},{18,... | collective-permute-start | bytes 196616 | tf_op jit(solution)/shard_map/ppermute | solution.py:26
  40.8 1.0 %collective-permute-start.14 = (bf16[128,256]{1,0:T(8,128)(2,1)S(1)}, bf16[128,256]{1,0:T(8,128)(2,1)S(1)}, u32[]{:S(2)}, u32[]{:S(2)}) collective-permute-start(bf16[128,256]{1,0:T(8,128)(2,1)S(1)} %add_convert_fusion.refs_3_), channel_id=1, source_target_pairs={{0,4},{2,6},{4,0},{6,2},{8,12},{10,14},{12,8},{14,10},{16,20},{18,... | collective-permute-start | bytes 196616 | tf_op jit(solution)/shard_map/ppermute | solution.py:26
  41.8 0.9 %collective-permute-start.15 = (bf16[128,256]{1,0:T(8,128)(2,1)S(1)}, bf16[128,256]{1,0:T(8,128)(2,1)S(1)}, u32[]{:S(2)}, u32[]{:S(2)}) collective-permute-start(bf16[128,256]{1,0:T(8,128)(2,1)S(1)} %add_convert_fusion.refs_3_), channel_id=1, source_target_pairs={{0,2},{2,0},{4,6},{6,4},{8,10},{10,8},{12,14},{14,12},{16,18},{18,... | collective-permute-start | bytes 196616 | tf_op jit(solution)/shard_map/ppermute | solution.py:26
  42.7 0.7 %copy.6 = f32[512,128]{1,0:T(8,128)} copy(f32[512,128]{1,0:T(8,128)S(1)} %get-tuple-element.22) | data formatting | bytes 524288
  43.4 1.5 %collective-permute-done.13.refs_0_ = bf16[128,256]{1,0:T(8,128)(2,1)S(1)} collective-permute-done((bf16[128,256]{1,0:T(8,128)(2,1)S(1)}, bf16[128,256]{1,0:T(8,128)(2,1)S(1)}, u32[]{:S(2)}, u32[]{:S(2)}) %collective-permute-start.13) | collective-permute-done | bytes 65568 | tf_op jit(solution)/shard_map/ppermute | solution.py:26
  44.9 0.4 collective-permute-done.14.refs_1_
  45.4 0.7 %collective-permute-done.15.refs_2_ = bf16[128,256]{1,0:T(8,128)(2,1)S(1)} collective-permute-done((bf16[128,256]{1,0:T(8,128)(2,1)S(1)}, bf16[128,256]{1,0:T(8,128)(2,1)S(1)}, u32[]{:S(2)}, u32[]{:S(2)}) %collective-permute-start.15) | collective-permute-done | bytes 65568 | tf_op jit(solution)/shard_map/ppermute | solution.py:26
  46.1 0.9 %join.1 = f32[1024,128]{1,0:T(8,128)} custom-call(s32[1]{0:T(128)} %bitcast.8.digit_ref, bf16[128,256]{1,0:T(8,128)(2,1)S(1)} %collective-permute-done.13.refs_0_, bf16[128,256]{1,0:T(8,128)(2,1)S(1)} %collective-permute-done.14.refs_1_, bf16[128,256]{1,0:T(8,128)(2,1)S(1)} %collective-permute-done.15.refs_2_, bf16[128,256]{1,0:T(8,128)(2,1)S(1)} %add_convert_fusion.refs_3_), custom_call_target="tpu_custom_call" | custom-call | tf_op jit(solution)/shard_map/join/pallas_call | solution.py:308
  (14 shorter events, 1.6 us)
Async XLA Ops:
  3.1 8.0 %collective-permute-start.1 = (bf16[528,128]{1,0:T(8,128)(2,1)S(1)}, bf16[528,128]{1,0:T(8,128)(2,1)S(1)}, u32[]{:S(2)}, u32[]{:S(2)}) collective-permute-start(bf16[528,128]{1,0:T(8,128)(2,1)S(1)} %get-tuple-element.12.refs_1_.refs_0_), channel_id=1, source_target_pairs={{0,1},{1,0},{2,3},{3,2},{4,5},{5,4},{6,7},{7,6},{8,9},{9,8},{10,11... | collective-permute-start | bytes 405512 | tf_op jit(solution)/shard_map/ppermute | solution.py:21
  3.6 8.7 %collective-permute-start.4 = (bf16[528,128]{1,0:T(8,128)(2,1)S(1)}, bf16[528,128]{1,0:T(8,128)(2,1)S(1)}, u32[]{:S(2)}, u32[]{:S(2)}) collective-permute-start(bf16[528,128]{1,0:T(8,128)(2,1)S(1)} %get-tuple-element.12.refs_1_.refs_0_), channel_id=1, source_target_pairs={{0,25},{1,24},{2,27},{3,26},{4,29},{5,28},{6,31},{7,30},{8,17},{9,... | collective-permute-start | bytes 405512 | tf_op jit(solution)/shard_map/ppermute | solution.py:36
  8.4 5.6 %collective-permute-start.2 = (bf16[528,128]{1,0:T(8,128)(2,1)S(1)}, bf16[528,128]{1,0:T(8,128)(2,1)S(1)}, u32[]{:S(2)}, u32[]{:S(2)}) collective-permute-start(bf16[528,128]{1,0:T(8,128)(2,1)S(1)} %get-tuple-element.12.refs_1_.refs_0_), channel_id=1, source_target_pairs={{0,3},{1,2},{2,1},{3,0},{4,7},{5,6},{6,5},{7,4},{8,11},{9,10},{10,... | collective-permute-start | bytes 405512 | tf_op jit(solution)/shard_map/ppermute | solution.py:36
  9.5 5.7 %collective-permute-start.3 = (bf16[528,128]{1,0:T(8,128)(2,1)S(1)}, bf16[528,128]{1,0:T(8,128)(2,1)S(1)}, u32[]{:S(2)}, u32[]{:S(2)}) collective-permute-start(bf16[528,128]{1,0:T(8,128)(2,1)S(1)} %get-tuple-element.12.refs_1_.refs_0_), channel_id=1, source_target_pairs={{0,9},{1,8},{2,11},{3,10},{4,13},{5,12},{6,15},{7,14},{8,1},{9,0},... | collective-permute-start | bytes 405512 | tf_op jit(solution)/shard_map/ppermute | solution.py:36
  9.5 10.3 %collective-permute-start = (bf16[528,128]{1,0:T(8,128)(2,1)S(1)}, bf16[528,128]{1,0:T(8,128)(2,1)S(1)}, u32[]{:S(2)}, u32[]{:S(2)}) collective-permute-start(bf16[528,128]{1,0:T(8,128)(2,1)S(1)} %get-tuple-element.12.refs_1_.refs_0_), channel_id=1, source_target_pairs={{0,31},{1,30},{2,5},{3,4},{4,3},{5,2},{6,9},{7,8},{8,7},{9,6},{10,... | collective-permute-start | bytes 405512 | tf_op jit(solution)/shard_map/ppermute | solution.py:36
  20.3 1.6 %collective-permute-start.5 = (f32[512,128]{1,0:T(8,128)S(1)}, f32[512,128]{1,0:T(8,128)S(1)}, u32[]{:S(2)}, u32[]{:S(2)}) collective-permute-start(f32[512,128]{1,0:T(8,128)S(1)} %bitcast.9), channel_id=1, source_target_pairs={{0,1},{1,0},{2,3},{3,2},{4,5},{5,4},{6,7},{7,6},{8,9},{9,8},{10,11... | collective-permute-start | bytes 786440 | tf_op jit(solution)/shard_map/ppermute | solution.py:21
  22.6 1.6 %collective-permute-start.6 = (bf16[128,1024]{1,0:T(8,128)(2,1)S(1)}, bf16[128,1024]{1,0:T(8,128)(2,1)S(1)}, u32[]{:S(2)}, u32[]{:S(2)}) collective-permute-start(bf16[128,1024]{1,0:T(8,128)(2,1)S(1)} %get-tuple-element.17), channel_id=1, source_target_pairs={{0,1},{1,0},{2,3},{3,2},{4,5},{5,4},{6,7},{7,6},{8,9},{9,8},{10,11... | collective-permute-start | bytes 786440 | tf_op jit(solution)/shard_map/ppermute | solution.py:21
  24.3 5.9 %collective-permute-start.7 = (bf16[128,256]{1,0:T(8,128)(2,1)S(1)}, bf16[128,256]{1,0:T(8,128)(2,1)S(1)}, u32[]{:S(2)}, u32[]{:S(2)}) collective-permute-start(bf16[128,256]{1,0:T(8,128)(2,1)S(1)} %get-tuple-element.19), channel_id=1, source_target_pairs={{0,6},{2,4},{4,2},{6,0},{8,14},{10,12},{12,10},{14,8},{16,22},{18,... | collective-permute-start | bytes 196616 | tf_op jit(solution)/shard_map/ppermute | solution.py:26
  24.9 5.4 %collective-permute-start.8 = (bf16[128,256]{1,0:T(8,128)(2,1)S(1)}, bf16[128,256]{1,0:T(8,128)(2,1)S(1)}, u32[]{:S(2)}, u32[]{:S(2)}) collective-permute-start(bf16[128,256]{1,0:T(8,128)(2,1)S(1)} %get-tuple-element.20), channel_id=1, source_target_pairs={{0,4},{2,6},{4,0},{6,2},{8,12},{10,14},{12,8},{14,10},{16,20},{18,... | collective-permute-start | bytes 196616 | tf_op jit(solution)/shard_map/ppermute | solution.py:26
  25.3 5.0 %collective-permute-start.9 = (bf16[128,256]{1,0:T(8,128)(2,1)S(1)}, bf16[128,256]{1,0:T(8,128)(2,1)S(1)}, u32[]{:S(2)}, u32[]{:S(2)}) collective-permute-start(bf16[128,256]{1,0:T(8,128)(2,1)S(1)} %get-tuple-element.21), channel_id=1, source_target_pairs={{0,2},{2,0},{4,6},{6,4},{8,10},{10,8},{12,14},{14,12},{16,18},{18,... | collective-permute-start | bytes 196616 | tf_op jit(solution)/shard_map/ppermute | solution.py:26
  30.3 6.2 %collective-permute-start.10 = (bf16[128,256]{1,0:T(8,128)(2,1)S(1)}, bf16[128,256]{1,0:T(8,128)(2,1)S(1)}, u32[]{:S(2)}, u32[]{:S(2)}) collective-permute-start(bf16[128,256]{1,0:T(8,128)(2,1)S(1)} %add_convert_fusion.1), channel_id=1, source_target_pairs={{0,24},{2,26},{4,28},{6,30},{8,16},{10,18},{12,20},{14,22},{16,8},... | collective-permute-start | bytes 196616 | tf_op jit(solution)/shard_map/ppermute | solution.py:26
  33.2 5.9 %collective-permute-start.11 = (bf16[128,256]{1,0:T(8,128)(2,1)S(1)}, bf16[128,256]{1,0:T(8,128)(2,1)S(1)}, u32[]{:S(2)}, u32[]{:S(2)}) collective-permute-start(bf16[128,256]{1,0:T(8,128)(2,1)S(1)} %add_convert_fusion.1), channel_id=1, source_target_pairs={{0,16},{2,18},{4,20},{6,22},{8,24},{10,26},{12,28},{14,30},{16,0},... | collective-permute-start | bytes 196616 | tf_op jit(solution)/shard_map/ppermute | solution.py:26
  33.4 5.7 %collective-permute-start.12 = (bf16[128,256]{1,0:T(8,128)(2,1)S(1)}, bf16[128,256]{1,0:T(8,128)(2,1)S(1)}, u32[]{:S(2)}, u32[]{:S(2)}) collective-permute-start(bf16[128,256]{1,0:T(8,128)(2,1)S(1)} %add_convert_fusion.1), channel_id=1, source_target_pairs={{0,8},{2,10},{4,12},{6,14},{8,0},{10,2},{12,4},{14,6},{16,24},{18,... | collective-permute-start | bytes 196616 | tf_op jit(solution)/shard_map/ppermute | solution.py:26
  39.1 5.8 %collective-permute-start.13 = (bf16[128,256]{1,0:T(8,128)(2,1)S(1)}, bf16[128,256]{1,0:T(8,128)(2,1)S(1)}, u32[]{:S(2)}, u32[]{:S(2)}) collective-permute-start(bf16[128,256]{1,0:T(8,128)(2,1)S(1)} %add_convert_fusion.refs_3_), channel_id=1, source_target_pairs={{0,6},{2,4},{4,2},{6,0},{8,14},{10,12},{12,10},{14,8},{16,22},{18,... | collective-permute-start | bytes 196616 | tf_op jit(solution)/shard_map/ppermute | solution.py:26
  40.8 4.5 %collective-permute-start.14 = (bf16[128,256]{1,0:T(8,128)(2,1)S(1)}, bf16[128,256]{1,0:T(8,128)(2,1)S(1)}, u32[]{:S(2)}, u32[]{:S(2)}) collective-permute-start(bf16[128,256]{1,0:T(8,128)(2,1)S(1)} %add_convert_fusion.refs_3_), channel_id=1, source_target_pairs={{0,4},{2,6},{4,0},{6,2},{8,12},{10,14},{12,8},{14,10},{16,20},{18,... | collective-permute-start | bytes 196616 | tf_op jit(solution)/shard_map/ppermute | solution.py:26
  41.8 4.3 %collective-permute-start.15 = (bf16[128,256]{1,0:T(8,128)(2,1)S(1)}, bf16[128,256]{1,0:T(8,128)(2,1)S(1)}, u32[]{:S(2)}, u32[]{:S(2)}) collective-permute-start(bf16[128,256]{1,0:T(8,128)(2,1)S(1)} %add_convert_fusion.refs_3_), channel_id=1, source_target_pairs={{0,2},{2,0},{4,6},{6,4},{8,10},{10,8},{12,14},{14,12},{16,18},{18,... | collective-permute-start | bytes 196616 | tf_op jit(solution)/shard_map/ppermute | solution.py:26

commit v6 on v5

--- a/solution.py
+++ b/solution.py
@@ -26,10 +26,10 @@
     return lax.ppermute(value, "pair", [(p, p ^ mask) for p in range(count)])
 
 
-def crossed(value, to):
+def crossed(value, to, turn=1):
     blocks, cores = lax.axis_size("pair"), lax.axis_size("dp")
     pairs = [
-        (block * cores + core, to(block) * cores + (core ^ 1))
+        (block * cores + core, to(block) * cores + (core ^ turn))
         for block in range(blocks)
         for core in range(cores)
     ]
@@ -135,7 +135,7 @@
     )
 
 
-def coupled_rows(columns, base_ref, own_ref, parts, total):
+def coupled_rows(columns, bases, own_ref, parts, total):
     rows = own_ref.shape[0] - tail
     step = min(256, rows)
     column = lax.broadcasted_iota(jnp.int32, (1, lanes), 1)
@@ -152,7 +152,7 @@
             for lane in range(0, step, lanes):
                 k = (begin + lane) // lanes
                 grown = jnp.exp2(cosine[:, lane : lane + lanes] * exponent_scale)
-                ids = (column + (base_ref[which] + (begin + lane))).astype(f32)
+                ids = (column + (bases[which][0] + (begin + lane))).astype(f32)
                 value = grown * (weight_i + part_weight[k : k + 1, :])
                 value = value - jnp.where(positive_i == ids, 2.0, 0.0)
                 pieces.append(value.astype(bf16))
@@ -170,7 +170,8 @@
     return as_columns(jnp.exp(-lse)), as_columns(positive)
 
 
-def couple_kernel(owners, count, base_ref, *refs):
+def couple_kernel(owners, count, *refs):
+    bases, refs = refs[:count], refs[count:]
     owns, parts, before, acc_ref = (
         refs[:owners], refs[owners : owners + count], refs[owners + count : -1], refs[-1]
     )
@@ -178,7 +179,7 @@
     for k, own_ref in enumerate(owns):
         columns = own_columns(own_ref)
         total = before[0][k] if before else jnp.zeros((rows, own_ref.shape[1]), f32)
-        acc_ref[k] = coupled_rows(columns, base_ref, own_ref, parts, total)
+        acc_ref[k] = coupled_rows(columns, bases, own_ref, parts, total)
 
 
 def couple_cost(rows, width, count):
@@ -192,13 +193,13 @@
     rows, width = owns[0].shape[0] - tail, owns[0].shape[1]
     return pl.pallas_call(
         functools.partial(couple_kernel, len(owns), len(parts)),
-        in_specs=[smem_spec()] + [vmem_spec()] * (len(owns) + len(parts) + len(before)),
+        in_specs=[smem_spec()] * len(parts) + [vmem_spec()] * (len(owns) + len(parts) + len(before)),
         out_specs=vmem_spec(),
         out_shape=jax.ShapeDtypeStruct((len(owns), rows, width), f32),
         compiler_params=small_grant(8),
         cost_estimate=couple_cost(rows, width, len(parts) * len(owns)),
         name="couple",
-    )(bases, *owns, *parts, *before)
+    )(*(base[None] for base in bases), *owns, *parts, *before)
 
 
 def finish_kernel(count, core_ref, acc_ref, projected_ref, features_ref, *refs):
@@ -332,19 +333,19 @@
         size = count // stride
         return lambda i: (((i // stride + odd) % size ^ 1) + size - odd) % size * stride + i % stride
 
-    def partner(stride, odd):
+    def partner(stride, odd, turn=1):
         to = pairing(pair_count, stride, odd)
-        return crossed(packed, to), to(block) * group_rows + (core ^ 1) * rows
-
-    (near_even, base_a), (far_even, base_b) = partner(1, 0), partner(far, 0)
-    (far_odd, base_c), (near_odd, base_d) = partner(far, 1), partner(1, 1)
+        return crossed(packed, to, turn), to(block) * group_rows + (core ^ turn) * rows
+
+    (near_even, base_a), (far_even, base_b) = partner(1, 0, 1), partner(far, 0, 1)
+    (far_odd, base_c), (near_odd, base_d) = partner(far, 1, 0), partner(1, 1, 1)
     siblings = [swapped(packed, mask) for mask in range(1, dp_count)]
     owns = siblings + [packed]
-    acc = couple(jnp.stack([base_c]), owns, [far_odd])
-    acc = couple(jnp.stack([base_a, base_b]), owns, [near_even, far_even], (acc,))
-    acc_siblings = couple(jnp.stack([base_d]), siblings, [near_odd], (acc,))
+    acc = couple([base_c], owns, [far_odd])
+    acc = couple([base_a, base_b], owns, [near_even, far_even], (acc,))
+    acc_siblings = couple([base_d], siblings, [near_odd], (acc,))
     returned = [swapped(acc_siblings[mask - 1], mask) for mask in range(1, dp_count)]
-    acc = couple(jnp.stack([base_d]), [packed], [near_odd], (acc[dp_count - 1 :],))
+    acc = couple([base_d], [packed], [near_odd], (acc[dp_count - 1 :],))
     grad_embed, half, *sends = finish(core, acc, projected, held, returned, dp_count)
     received = [swapped(send, mask) for mask, send in enumerate(sends, 1)]
     mine = weight_term(half, held, core, dp_count)
@@ -352,14 +353,14 @@
     ways = 4
     digit = block & (ways - 1)
     keep, *sends = split(digit, mine, received, ways)
-    moved = [exchanged(sends[s - 1], s) for s in reversed(range(1, ways))]
+    moved = [exchanged(sends[s - 1], s) for s in (1, 2, 3)]
     for part in moved:
         keep = keep + part.astype(f32)
     stride = ways
     while stride < pair_count:
         mine = keep.astype(bf16)
         last, middle, near = (exchanged(mine, s * stride).astype(f32) for s in (3, 2, 1))
-        keep = (last + middle) + (near + mine.astype(f32))
+        keep = (last + near) + (middle + mine.astype(f32))
         stride *= ways
     mine = keep.astype(bf16)
     moved = [exchanged(mine, s) for s in reversed(range(1, ways))]

time: 47.2 us -> 46.9 us (level)
  Pallas kernels: 8.41 us -> 7.87 us
  waiting for transfers between devices: 16.8 us -> 17.3 us
    ppermute x4, waiting for transfers between devices: 5.75 us -> 6.38 us  [crossed(): return lax.ppermute(value, ('pair', 'dp'), pairs)]
    pallas_call x4, Pallas kernels: 3.98 us -> 3.44 us  [couple(): pl.pallas_call(functools.partial(couple_kernel, len(owns), len(parts)), i...]
  transfers between devices with their start and end apart: 16 -> 16, of which waited for: 13 -> 14; matrix products, arithmetic and copies ran while one was open for 2% -> 2% of each run, Pallas kernels for 8% -> 7%
where the time goes in v6:
time: 46.9 us; the launch traced here: 46.8 us
  starting transfers between devices  20.1 us (43%)
  waiting for transfers between devices  17.3 us (37%)
  Pallas kernels  7.87 us (17%)
  local copies, waits for them, and re-layouts  0.72 us (2%)
  between operations  0.71 us (2%)
    ppermute x9, starting transfers between devices, exchanged(): return lax.ppermute(value, 'pair', [(p, p ^ mask) for p in range(count)])  11.6 us
    ppermute x9, waiting for transfers between devices, exchanged(): return lax.ppermute(value, 'pair', [(p, p ^ mask) for p in range(count)])  9.17 us
    ppermute x4, starting transfers between devices, crossed(): return lax.ppermute(value, ('pair', 'dp'), pairs)  7.48 us
    ppermute x4, waiting for transfers between devices, crossed(): return lax.ppermute(value, ('pair', 'dp'), pairs)  6.38 us
    pallas_call x4, Pallas kernels, couple(): pl.pallas_call(functools.partial(couple_kernel, len(owns), len(parts)), i...  3.44 us
    pallas_call x1, Pallas kernels, project(): pl.pallas_call(project_kernel, in_specs=[hbm] * 4, out_specs=[vmem_spec()...  2.48 us
    ppermute x3, waiting for transfers between devices, swapped(): return lax.ppermute(value, 'dp', [(d, d ^ mask) for d in range(count)])  1.72 us
    ppermute x3, starting transfers between devices, swapped(): return lax.ppermute(value, 'dp', [(d, d ^ mask) for d in range(count)])  1.11 us
  transfers between devices with their start and end apart: 16, of which 14 were waited for; matrix products, arithmetic and copies ran while one was open for 2% of the time, Pallas kernels for 7%

profile of v6, /device:TPU:0, one launch (start us, length us, event | category | flops | bytes accessed | tf_op | source)
XLA Modules:
  0.0 46.8 jit_solution(6768110825378411337)
XLA Ops:
  0.6 2.5 %project.1 = (f32[512,128]{1,0:T(8,128)S(1)}, bf16[528,128]{1,0:T(8,128)(2,1)S(1)}, bf16[512,2048]{1,0:T(8,128)(2,1)S(1)}) custom-call(bf16[512,2048]{1,0:T(8,128)(2,1)} %features_ref.1, bf16[2048,128]{1,0:T(8,128)(2,1)} %weight_ref.1, bf16[4,128]{1,0:T(4,128)(2,1)} %bitcast.11, s32[4,128]{1,0:T(4,128)} %bitcast.10), custom_call_target="tpu_custom_call" | custom-call | tf_op jit(solution)/shard_map/project/pallas_call | solution.py:102
  3.1 0.5 %collective-permute-start.1 = (bf16[528,128]{1,0:T(8,128)(2,1)S(1)}, bf16[528,128]{1,0:T(8,128)(2,1)S(1)}, u32[]{:S(2)}, u32[]{:S(2)}) collective-permute-start(bf16[528,128]{1,0:T(8,128)(2,1)S(1)} %get-tuple-element.12.refs_2_.refs_3_.refs_1_), channel_id=1, source_target_pairs={{0,1},{1,0},{2,3},{3,2},{4,5},{5,4},{6,7},{7,6},{8,9},{9,8},{10,11... | collective-permute-start | bytes 405512 | tf_op jit(solution)/shard_map/ppermute | solution.py:21
  3.6 4.7 %collective-permute-start.4 = (bf16[528,128]{1,0:T(8,128)(2,1)S(1)}, bf16[528,128]{1,0:T(8,128)(2,1)S(1)}, u32[]{:S(2)}, u32[]{:S(2)}) collective-permute-start(bf16[528,128]{1,0:T(8,128)(2,1)S(1)} %get-tuple-element.12.refs_2_.refs_3_.refs_1_), channel_id=1, source_target_pairs={{0,24},{1,25},{2,26},{3,27},{4,28},{5,29},{6,30},{7,31},{8,16},{9,... | collective-permute-start | bytes 405512 | tf_op jit(solution)/shard_map/ppermute | solution.py:36
  8.3 1.3 %collective-permute-start.2 = (bf16[528,128]{1,0:T(8,128)(2,1)S(1)}, bf16[528,128]{1,0:T(8,128)(2,1)S(1)}, u32[]{:S(2)}, u32[]{:S(2)}) collective-permute-start(bf16[528,128]{1,0:T(8,128)(2,1)S(1)} %get-tuple-element.12.refs_2_.refs_3_.refs_1_), channel_id=1, source_target_pairs={{0,3},{1,2},{2,1},{3,0},{4,7},{5,6},{6,5},{7,4},{8,11},{9,10},{10,... | collective-permute-start | bytes 405512 | tf_op jit(solution)/shard_map/ppermute | solution.py:36
  9.6 1.5 %collective-permute-start = (bf16[528,128]{1,0:T(8,128)(2,1)S(1)}, bf16[528,128]{1,0:T(8,128)(2,1)S(1)}, u32[]{:S(2)}, u32[]{:S(2)}) collective-permute-start(bf16[528,128]{1,0:T(8,128)(2,1)S(1)} %get-tuple-element.12.refs_2_.refs_3_.refs_1_), channel_id=1, source_target_pairs={{0,31},{1,30},{2,5},{3,4},{4,3},{5,2},{6,9},{7,8},{8,7},{9,6},{10,... | collective-permute-start | bytes 405512 | tf_op jit(solution)/shard_map/ppermute | solution.py:36
  11.1 1.7 %collective-permute-done.4.refs_3_ = bf16[528,128]{1,0:T(8,128)(2,1)S(1)} collective-permute-done((bf16[528,128]{1,0:T(8,128)(2,1)S(1)}, bf16[528,128]{1,0:T(8,128)(2,1)S(1)}, u32[]{:S(2)}, u32[]{:S(2)}) %collective-permute-start.4) | collective-permute-done | bytes 135200 | tf_op jit(solution)/shard_map/ppermute | solution.py:36
  12.8 1.0 %couple.4.refs_6_ = f32[2,512,128]{2,1,0:T(8,128)S(1)} custom-call(s32[1]{0:T(128)} %bitcast.6.refs_0_, bf16[528,128]{1,0:T(8,128)(2,1)S(1)} %collective-permute-done.1.refs_1_.refs_2_, bf16[528,128]{1,0:T(8,128)(2,1)S(1)} %get-tuple-element.12.refs_2_.refs_3_.refs_1_, bf16[528,128]{1,0:T(8,128)(2,1)S(1)} %collective-permute-done.4.refs_3_), custom_call_target="tpu_custom_call" | custom-call | flops 268435456 | bytes 262144 | tf_op jit(solution)/shard_map/couple/pallas_call | solution.py:194
  13.9 1.4 %collective-permute-done.3.refs_5_ = bf16[528,128]{1,0:T(8,128)(2,1)S(1)} collective-permute-done((bf16[528,128]{1,0:T(8,128)(2,1)S(1)}, bf16[528,128]{1,0:T(8,128)(2,1)S(1)}, u32[]{:S(2)}, u32[]{:S(2)}) %collective-permute-start.3) | collective-permute-done | bytes 135200 | tf_op jit(solution)/shard_map/ppermute | solution.py:36
  15.2 1.4 %couple.5.refs_3_ = f32[2,512,128]{2,1,0:T(8,128)S(1)} custom-call(s32[1]{0:T(128)} %bitcast.4.refs_0_, s32[1]{0:T(128)} %bitcast.5.refs_1_, bf16[528,128]{1,0:T(8,128)(2,1)S(1)} %collective-permute-done.1.refs_1_.refs_2_, bf16[528,128]{1,0:T(8,128)(2,1)S(1)} %get-tuple-element.12.refs_2_.refs_3_.refs_1_, ...), custom_call_target="tpu_custom_call" | custom-call | flops 536870912 | bytes 262144 | tf_op jit(solution)/shard_map/couple/pallas_call | solution.py:194
  16.6 3.2 %collective-permute-done.refs_2_ = bf16[528,128]{1,0:T(8,128)(2,1)S(1)} collective-permute-done((bf16[528,128]{1,0:T(8,128)(2,1)S(1)}, bf16[528,128]{1,0:T(8,128)(2,1)S(1)}, u32[]{:S(2)}, u32[]{:S(2)}) %collective-permute-start) | collective-permute-done | bytes 135200 | tf_op jit(solution)/shard_map/ppermute | solution.py:36
  19.9 0.5 %couple.7 = f32[1,512,128]{2,1,0:T(8,128)S(1)} custom-call(s32[1]{0:T(128)} %bitcast.1.refs_0_, bf16[528,128]{1,0:T(8,128)(2,1)S(1)} %collective-permute-done.1.refs_1_.refs_2_, bf16[528,128]{1,0:T(8,128)(2,1)S(1)} %collective-permute-done.refs_2_, f32[2,512,128]{2,1,0:T(8,128)S(1)} %couple.5.refs_3_), custom_call_target="tpu_custom_call" | custom-call | flops 134217728 | bytes 262144 | tf_op jit(solution)/shard_map/couple/pallas_call | solution.py:194
  20.7 0.5 %couple.6.acc_ref = f32[1,512,128]{2,1,0:T(8,128)S(1)} custom-call(s32[1]{0:T(128)} %bitcast.1.refs_0_, bf16[528,128]{1,0:T(8,128)(2,1)S(1)} %get-tuple-element.12.refs_2_.refs_3_.refs_1_, bf16[528,128]{1,0:T(8,128)(2,1)S(1)} %collective-permute-done.refs_2_, f32[1,512,128]{2,1,0:T(8,128)S(1)} %slice.4.refs_3_), custom_call_target="tpu_custom_call" | custom-call | flops 134217728 | bytes 262144 | tf_op jit(solution)/shard_map/couple/pallas_call | solution.py:194
  21.3 0.7 %collective-permute-done.5.refs_0_ = f32[512,128]{1,0:T(8,128)S(1)} collective-permute-done((f32[512,128]{1,0:T(8,128)S(1)}, f32[512,128]{1,0:T(8,128)S(1)}, u32[]{:S(2)}, u32[]{:S(2)}) %collective-permute-start.5) | collective-permute-done | bytes 262176 | tf_op jit(solution)/shard_map/ppermute | solution.py:21
  22.0 0.6 %finish.1 = (f32[512,128]{1,0:T(8,128)S(1)}, bf16[128,512]{1,0:T(8,128)(2,1)S(1)}, bf16[128,1024]{1,0:T(8,128)(2,1)S(1)}) custom-call(s32[1]{0:T(128)} %bitcast.core_ref.share_ref, f32[1,512,128]{2,1,0:T(8,128)S(1)} %couple.6.acc_ref, f32[512,128]{1,0:T(8,128)S(1)} %get-tuple-element.13.projected_ref, bf16[512,2048]{1,0:T(8,128)(2,1)S(1)} %get-tuple-element.14.features_ref, ...), custom_call_target="tpu_custom_call" | custom-call | tf_op jit(solution)/shard_map/finish/pallas_call | solution.py:238
  23.3 1.0 %collective-permute-done.6.refs_0_ = bf16[128,1024]{1,0:T(8,128)(2,1)S(1)} collective-permute-done((bf16[128,1024]{1,0:T(8,128)(2,1)S(1)}, bf16[128,1024]{1,0:T(8,128)(2,1)S(1)}, u32[]{:S(2)}, u32[]{:S(2)}) %collective-permute-start.6) | collective-permute-done | bytes 262176 | tf_op jit(solution)/shard_map/ppermute | solution.py:21
  24.4 1.2 %collective-permute-start.8 = (bf16[128,256]{1,0:T(8,128)(2,1)S(1)}, bf16[128,256]{1,0:T(8,128)(2,1)S(1)}, u32[]{:S(2)}, u32[]{:S(2)}) collective-permute-start(bf16[128,256]{1,0:T(8,128)(2,1)S(1)} %get-tuple-element.20), channel_id=1, source_target_pairs={{0,4},{2,6},{4,0},{6,2},{8,12},{10,14},{12,8},{14,10},{16,20},{18,... | collective-permute-start | bytes 196616 | tf_op jit(solution)/shard_map/ppermute | solution.py:26
  25.6 2.3 %collective-permute-start.9 = (bf16[128,256]{1,0:T(8,128)(2,1)S(1)}, bf16[128,256]{1,0:T(8,128)(2,1)S(1)}, u32[]{:S(2)}, u32[]{:S(2)}) collective-permute-start(bf16[128,256]{1,0:T(8,128)(2,1)S(1)} %get-tuple-element.21), channel_id=1, source_target_pairs={{0,6},{2,4},{4,2},{6,0},{8,14},{10,12},{12,10},{14,8},{16,22},{18,... | collective-permute-start | bytes 196616 | tf_op jit(solution)/shard_map/ppermute | solution.py:26
  27.9 1.0 %collective-permute-done.7 = bf16[128,256]{1,0:T(8,128)(2,1)S(1)} collective-permute-done((bf16[128,256]{1,0:T(8,128)(2,1)S(1)}, bf16[128,256]{1,0:T(8,128)(2,1)S(1)}, u32[]{:S(2)}, u32[]{:S(2)}) %collective-permute-start.7) | collective-permute-done | bytes 65568 | tf_op jit(solution)/shard_map/ppermute | solution.py:26
  28.9 1.8 %collective-permute-done.9 = bf16[128,256]{1,0:T(8,128)(2,1)S(1)} collective-permute-done((bf16[128,256]{1,0:T(8,128)(2,1)S(1)}, bf16[128,256]{1,0:T(8,128)(2,1)S(1)}, u32[]{:S(2)}, u32[]{:S(2)}) %collective-permute-start.9) | collective-permute-done | bytes 65568 | tf_op jit(solution)/shard_map/ppermute | solution.py:26
  30.8 3.4 %collective-permute-start.10 = (bf16[128,256]{1,0:T(8,128)(2,1)S(1)}, bf16[128,256]{1,0:T(8,128)(2,1)S(1)}, u32[]{:S(2)}, u32[]{:S(2)}) collective-permute-start(bf16[128,256]{1,0:T(8,128)(2,1)S(1)} %add_convert_fusion.1), channel_id=1, source_target_pairs={{0,24},{2,26},{4,28},{6,30},{8,16},{10,18},{12,20},{14,22},{16,8},... | collective-permute-start | bytes 196616 | tf_op jit(solution)/shard_map/ppermute | solution.py:26
  34.2 1.1 %collective-permute-start.12 = (bf16[128,256]{1,0:T(8,128)(2,1)S(1)}, bf16[128,256]{1,0:T(8,128)(2,1)S(1)}, u32[]{:S(2)}, u32[]{:S(2)}) collective-permute-start(bf16[128,256]{1,0:T(8,128)(2,1)S(1)} %add_convert_fusion.1), channel_id=1, source_target_pairs={{0,16},{2,18},{4,20},{6,22},{8,24},{10,26},{12,28},{14,30},{16,0},... | collective-permute-start | bytes 196616 | tf_op jit(solution)/shard_map/ppermute | solution.py:26
  35.2 1.8 %collective-permute-done.10 = bf16[128,256]{1,0:T(8,128)(2,1)S(1)} collective-permute-done((bf16[128,256]{1,0:T(8,128)(2,1)S(1)}, bf16[128,256]{1,0:T(8,128)(2,1)S(1)}, u32[]{:S(2)}, u32[]{:S(2)}) %collective-permute-start.10) | collective-permute-done | bytes 65568 | tf_op jit(solution)/shard_map/ppermute | solution.py:26
  37.0 1.4 %collective-permute-done.11 = bf16[128,256]{1,0:T(8,128)(2,1)S(1)} collective-permute-done((bf16[128,256]{1,0:T(8,128)(2,1)S(1)}, bf16[128,256]{1,0:T(8,128)(2,1)S(1)}, u32[]{:S(2)}, u32[]{:S(2)}) %collective-permute-start.11) | collective-permute-done | bytes 65568 | tf_op jit(solution)/shard_map/ppermute | solution.py:26
  38.4 0.9 %collective-permute-done.12 = bf16[128,256]{1,0:T(8,128)(2,1)S(1)} collective-permute-done((bf16[128,256]{1,0:T(8,128)(2,1)S(1)}, bf16[128,256]{1,0:T(8,128)(2,1)S(1)}, u32[]{:S(2)}, u32[]{:S(2)}) %collective-permute-start.12) | collective-permute-done | bytes 65568 | tf_op jit(solution)/shard_map/ppermute | solution.py:26
  39.4 1.6 %collective-permute-start.13 = (bf16[128,256]{1,0:T(8,128)(2,1)S(1)}, bf16[128,256]{1,0:T(8,128)(2,1)S(1)}, u32[]{:S(2)}, u32[]{:S(2)}) collective-permute-start(bf16[128,256]{1,0:T(8,128)(2,1)S(1)} %add_convert_fusion.refs_3_), channel_id=1, source_target_pairs={{0,6},{2,4},{4,2},{6,0},{8,14},{10,12},{12,10},{14,8},{16,22},{18,... | collective-permute-start | bytes 196616 | tf_op jit(solution)/shard_map/ppermute | solution.py:26
  41.0 0.6 %collective-permute-start.14 = (bf16[128,256]{1,0:T(8,128)(2,1)S(1)}, bf16[128,256]{1,0:T(8,128)(2,1)S(1)}, u32[]{:S(2)}, u32[]{:S(2)}) collective-permute-start(bf16[128,256]{1,0:T(8,128)(2,1)S(1)} %add_convert_fusion.refs_3_), channel_id=1, source_target_pairs={{0,4},{2,6},{4,0},{6,2},{8,12},{10,14},{12,8},{14,10},{16,20},{18,... | collective-permute-start | bytes 196616 | tf_op jit(solution)/shard_map/ppermute | solution.py:26
  41.6 1.3 %collective-permute-start.15 = (bf16[128,256]{1,0:T(8,128)(2,1)S(1)}, bf16[128,256]{1,0:T(8,128)(2,1)S(1)}, u32[]{:S(2)}, u32[]{:S(2)}) collective-permute-start(bf16[128,256]{1,0:T(8,128)(2,1)S(1)} %add_convert_fusion.refs_3_), channel_id=1, source_target_pairs={{0,2},{2,0},{4,6},{6,4},{8,10},{10,8},{12,14},{14,12},{16,18},{18,... | collective-permute-start | bytes 196616 | tf_op jit(solution)/shard_map/ppermute | solution.py:26
  42.9 0.7 %copy.6 = f32[512,128]{1,0:T(8,128)} copy(f32[512,128]{1,0:T(8,128)S(1)} %get-tuple-element.22) | data formatting | bytes 524288
  43.6 1.0 %collective-permute-done.13.refs_0_ = bf16[128,256]{1,0:T(8,128)(2,1)S(1)} collective-permute-done((bf16[128,256]{1,0:T(8,128)(2,1)S(1)}, bf16[128,256]{1,0:T(8,128)(2,1)S(1)}, u32[]{:S(2)}, u32[]{:S(2)}) %collective-permute-start.13) | collective-permute-done | bytes 65568 | tf_op jit(solution)/shard_map/ppermute | solution.py:26
  44.6 0.7 %collective-permute-done.14.refs_1_ = bf16[128,256]{1,0:T(8,128)(2,1)S(1)} collective-permute-done((bf16[128,256]{1,0:T(8,128)(2,1)S(1)}, bf16[128,256]{1,0:T(8,128)(2,1)S(1)}, u32[]{:S(2)}, u32[]{:S(2)}) %collective-permute-start.14) | collective-permute-done | bytes 65568 | tf_op jit(solution)/shard_map/ppermute | solution.py:26
  45.3 0.5 %collective-permute-done.15.refs_2_ = bf16[128,256]{1,0:T(8,128)(2,1)S(1)} collective-permute-done((bf16[128,256]{1,0:T(8,128)(2,1)S(1)}, bf16[128,256]{1,0:T(8,128)(2,1)S(1)}, u32[]{:S(2)}, u32[]{:S(2)}) %collective-permute-start.15) | collective-permute-done | bytes 65568 | tf_op jit(solution)/shard_map/ppermute | solution.py:26
  45.8 0.9 %join.1 = f32[1024,128]{1,0:T(8,128)} custom-call(s32[1]{0:T(128)} %bitcast.8.digit_ref, bf16[128,256]{1,0:T(8,128)(2,1)S(1)} %collective-permute-done.13.refs_0_, bf16[128,256]{1,0:T(8,128)(2,1)S(1)} %collective-permute-done.14.refs_1_, bf16[128,256]{1,0:T(8,128)(2,1)S(1)} %collective-permute-done.15.refs_2_, bf16[128,256]{1,0:T(8,128)(2,1)S(1)} %add_convert_fusion.refs_3_), custom_call_target="tpu_custom_call" | custom-call | tf_op jit(solution)/shard_map/join/pallas_call | solution.py:309
  (13 shorter events, 1.2 us)
Async XLA Ops:
  3.1 8.0 %collective-permute-start.1 = (bf16[528,128]{1,0:T(8,128)(2,1)S(1)}, bf16[528,128]{1,0:T(8,128)(2,1)S(1)}, u32[]{:S(2)}, u32[]{:S(2)}) collective-permute-start(bf16[528,128]{1,0:T(8,128)(2,1)S(1)} %get-tuple-element.12.refs_2_.refs_3_.refs_1_), channel_id=1, source_target_pairs={{0,1},{1,0},{2,3},{3,2},{4,5},{5,4},{6,7},{7,6},{8,9},{9,8},{10,11... | collective-permute-start | bytes 405512 | tf_op jit(solution)/shard_map/ppermute | solution.py:21
  3.6 9.2 %collective-permute-start.4 = (bf16[528,128]{1,0:T(8,128)(2,1)S(1)}, bf16[528,128]{1,0:T(8,128)(2,1)S(1)}, u32[]{:S(2)}, u32[]{:S(2)}) collective-permute-start(bf16[528,128]{1,0:T(8,128)(2,1)S(1)} %get-tuple-element.12.refs_2_.refs_3_.refs_1_), channel_id=1, source_target_pairs={{0,24},{1,25},{2,26},{3,27},{4,28},{5,29},{6,30},{7,31},{8,16},{9,... | collective-permute-start | bytes 405512 | tf_op jit(solution)/shard_map/ppermute | solution.py:36
  8.3 5.5 %collective-permute-start.2 = (bf16[528,128]{1,0:T(8,128)(2,1)S(1)}, bf16[528,128]{1,0:T(8,128)(2,1)S(1)}, u32[]{:S(2)}, u32[]{:S(2)}) collective-permute-start(bf16[528,128]{1,0:T(8,128)(2,1)S(1)} %get-tuple-element.12.refs_2_.refs_3_.refs_1_), channel_id=1, source_target_pairs={{0,3},{1,2},{2,1},{3,0},{4,7},{5,6},{6,5},{7,4},{8,11},{9,10},{10,... | collective-permute-start | bytes 405512 | tf_op jit(solution)/shard_map/ppermute | solution.py:36
  9.6 5.7 %collective-permute-start.3 = (bf16[528,128]{1,0:T(8,128)(2,1)S(1)}, bf16[528,128]{1,0:T(8,128)(2,1)S(1)}, u32[]{:S(2)}, u32[]{:S(2)}) collective-permute-start(bf16[528,128]{1,0:T(8,128)(2,1)S(1)} %get-tuple-element.12.refs_2_.refs_3_.refs_1_), channel_id=1, source_target_pairs={{0,9},{1,8},{2,11},{3,10},{4,13},{5,12},{6,15},{7,14},{8,1},{9,0},... | collective-permute-start | bytes 405512 | tf_op jit(solution)/shard_map/ppermute | solution.py:36
  9.6 10.3 %collective-permute-start = (bf16[528,128]{1,0:T(8,128)(2,1)S(1)}, bf16[528,128]{1,0:T(8,128)(2,1)S(1)}, u32[]{:S(2)}, u32[]{:S(2)}) collective-permute-start(bf16[528,128]{1,0:T(8,128)(2,1)S(1)} %get-tuple-element.12.refs_2_.refs_3_.refs_1_), channel_id=1, source_target_pairs={{0,31},{1,30},{2,5},{3,4},{4,3},{5,2},{6,9},{7,8},{8,7},{9,6},{10,... | collective-permute-start | bytes 405512 | tf_op jit(solution)/shard_map/ppermute | solution.py:36
  20.4 1.6 %collective-permute-start.5 = (f32[512,128]{1,0:T(8,128)S(1)}, f32[512,128]{1,0:T(8,128)S(1)}, u32[]{:S(2)}, u32[]{:S(2)}) collective-permute-start(f32[512,128]{1,0:T(8,128)S(1)} %bitcast.9), channel_id=1, source_target_pairs={{0,1},{1,0},{2,3},{3,2},{4,5},{5,4},{6,7},{7,6},{8,9},{9,8},{10,11... | collective-permute-start | bytes 786440 | tf_op jit(solution)/shard_map/ppermute | solution.py:21
  22.6 1.6 %collective-permute-start.6 = (bf16[128,1024]{1,0:T(8,128)(2,1)S(1)}, bf16[128,1024]{1,0:T(8,128)(2,1)S(1)}, u32[]{:S(2)}, u32[]{:S(2)}) collective-permute-start(bf16[128,1024]{1,0:T(8,128)(2,1)S(1)} %get-tuple-element.17), channel_id=1, source_target_pairs={{0,1},{1,0},{2,3},{3,2},{4,5},{5,4},{6,7},{7,6},{8,9},{9,8},{10,11... | collective-permute-start | bytes 786440 | tf_op jit(solution)/shard_map/ppermute | solution.py:21
  24.3 4.6 %collective-permute-start.7 = (bf16[128,256]{1,0:T(8,128)(2,1)S(1)}, bf16[128,256]{1,0:T(8,128)(2,1)S(1)}, u32[]{:S(2)}, u32[]{:S(2)}) collective-permute-start(bf16[128,256]{1,0:T(8,128)(2,1)S(1)} %get-tuple-element.19), channel_id=1, source_target_pairs={{0,2},{2,0},{4,6},{6,4},{8,10},{10,8},{12,14},{14,12},{16,18},{18,... | collective-permute-start | bytes 196616 | tf_op jit(solution)/shard_map/ppermute | solution.py:26
  24.4 4.5 %collective-permute-start.8 = (bf16[128,256]{1,0:T(8,128)(2,1)S(1)}, bf16[128,256]{1,0:T(8,128)(2,1)S(1)}, u32[]{:S(2)}, u32[]{:S(2)}) collective-permute-start(bf16[128,256]{1,0:T(8,128)(2,1)S(1)} %get-tuple-element.20), channel_id=1, source_target_pairs={{0,4},{2,6},{4,0},{6,2},{8,12},{10,14},{12,8},{14,10},{16,20},{18,... | collective-permute-start | bytes 196616 | tf_op jit(solution)/shard_map/ppermute | solution.py:26
  25.6 5.2 %collective-permute-start.9 = (bf16[128,256]{1,0:T(8,128)(2,1)S(1)}, bf16[128,256]{1,0:T(8,128)(2,1)S(1)}, u32[]{:S(2)}, u32[]{:S(2)}) collective-permute-start(bf16[128,256]{1,0:T(8,128)(2,1)S(1)} %get-tuple-element.21), channel_id=1, source_target_pairs={{0,6},{2,4},{4,2},{6,0},{8,14},{10,12},{12,10},{14,8},{16,22},{18,... | collective-permute-start | bytes 196616 | tf_op jit(solution)/shard_map/ppermute | solution.py:26
  30.8 6.2 %collective-permute-start.10 = (bf16[128,256]{1,0:T(8,128)(2,1)S(1)}, bf16[128,256]{1,0:T(8,128)(2,1)S(1)}, u32[]{:S(2)}, u32[]{:S(2)}) collective-permute-start(bf16[128,256]{1,0:T(8,128)(2,1)S(1)} %add_convert_fusion.1), channel_id=1, source_target_pairs={{0,24},{2,26},{4,28},{6,30},{8,16},{10,18},{12,20},{14,22},{16,8},... | collective-permute-start | bytes 196616 | tf_op jit(solution)/shard_map/ppermute | solution.py:26
  34.2 4.3 %collective-permute-start.11 = (bf16[128,256]{1,0:T(8,128)(2,1)S(1)}, bf16[128,256]{1,0:T(8,128)(2,1)S(1)}, u32[]{:S(2)}, u32[]{:S(2)}) collective-permute-start(bf16[128,256]{1,0:T(8,128)(2,1)S(1)} %add_convert_fusion.1), channel_id=1, source_target_pairs={{0,8},{2,10},{4,12},{6,14},{8,0},{10,2},{12,4},{14,6},{16,24},{18,... | collective-permute-start | bytes 196616 | tf_op jit(solution)/shard_map/ppermute | solution.py:26
  34.2 5.2 %collective-permute-start.12 = (bf16[128,256]{1,0:T(8,128)(2,1)S(1)}, bf16[128,256]{1,0:T(8,128)(2,1)S(1)}, u32[]{:S(2)}, u32[]{:S(2)}) collective-permute-start(bf16[128,256]{1,0:T(8,128)(2,1)S(1)} %add_convert_fusion.1), channel_id=1, source_target_pairs={{0,16},{2,18},{4,20},{6,22},{8,24},{10,26},{12,28},{14,30},{16,0},... | collective-permute-start | bytes 196616 | tf_op jit(solution)/shard_map/ppermute | solution.py:26
  39.4 5.2 %collective-permute-start.13 = (bf16[128,256]{1,0:T(8,128)(2,1)S(1)}, bf16[128,256]{1,0:T(8,128)(2,1)S(1)}, u32[]{:S(2)}, u32[]{:S(2)}) collective-permute-start(bf16[128,256]{1,0:T(8,128)(2,1)S(1)} %add_convert_fusion.refs_3_), channel_id=1, source_target_pairs={{0,6},{2,4},{4,2},{6,0},{8,14},{10,12},{12,10},{14,8},{16,22},{18,... | collective-permute-start | bytes 196616 | tf_op jit(solution)/shard_map/ppermute | solution.py:26
  41.0 4.3 %collective-permute-start.14 = (bf16[128,256]{1,0:T(8,128)(2,1)S(1)}, bf16[128,256]{1,0:T(8,128)(2,1)S(1)}, u32[]{:S(2)}, u32[]{:S(2)}) collective-permute-start(bf16[128,256]{1,0:T(8,128)(2,1)S(1)} %add_convert_fusion.refs_3_), channel_id=1, source_target_pairs={{0,4},{2,6},{4,0},{6,2},{8,12},{10,14},{12,8},{14,10},{16,20},{18,... | collective-permute-start | bytes 196616 | tf_op jit(solution)/shard_map/ppermute | solution.py:26
  41.6 4.3 %collective-permute-start.15 = (bf16[128,256]{1,0:T(8,128)(2,1)S(1)}, bf16[128,256]{1,0:T(8,128)(2,1)S(1)}, u32[]{:S(2)}, u32[]{:S(2)}) collective-permute-start(bf16[128,256]{1,0:T(8,128)(2,1)S(1)} %add_convert_fusion.refs_3_), channel_id=1, source_target_pairs={{0,2},{2,0},{4,6},{6,4},{8,10},{10,8},{12,14},{14,12},{16,18},{18,... | collective-permute-start | bytes 196616 | tf_op jit(solution)/shard_map/ppermute | solution.py:26

commit v7 on v6

--- a/solution.py
+++ b/solution.py
@@ -205,7 +205,7 @@
 def finish_kernel(count, core_ref, acc_ref, projected_ref, features_ref, *refs):
     received, grad_ref, half_ref, sends = refs[:count], refs[count], refs[count + 1], refs[count + 2 :]
     rows = projected_ref.shape[0]
-    chunk = min(256, rows)
+    chunk = min(128, rows)
     for start in range(0, rows, chunk):
         part = pl.ds(start, chunk)
         total = acc_ref[0, part, :]
@@ -342,10 +342,10 @@
     siblings = [swapped(packed, mask) for mask in range(1, dp_count)]
     owns = siblings + [packed]
     acc = couple([base_c], owns, [far_odd])
-    acc = couple([base_a, base_b], owns, [near_even, far_even], (acc,))
-    acc_siblings = couple([base_d], siblings, [near_odd], (acc,))
+    acc = couple([base_d], owns, [near_odd], (acc,))
+    acc_siblings = couple([base_a, base_b], siblings, [near_even, far_even], (acc,))
     returned = [swapped(acc_siblings[mask - 1], mask) for mask in range(1, dp_count)]
-    acc = couple([base_d], [packed], [near_odd], (acc[dp_count - 1 :],))
+    acc = couple([base_a, base_b], [packed], [near_even, far_even], (acc[dp_count - 1 :],))
     grad_embed, half, *sends = finish(core, acc, projected, held, returned, dp_count)
     received = [swapped(send, mask) for mask, send in enumerate(sends, 1)]
     mine = weight_term(half, held, core, dp_count)

time: 46.9 us -> 46.6 us (level)
  waiting for transfers between devices: 17.3 us -> 16.2 us
  starting transfers between devices: 20.1 us -> 20.8 us
    ppermute x4, waiting for transfers between devices: 6.38 us -> 4.9 us  [crossed(): return lax.ppermute(value, ('pair', 'dp'), pairs)]
    ppermute x4, starting transfers between devices: 7.48 us -> 8.31 us  [crossed(): return lax.ppermute(value, ('pair', 'dp'), pairs)]
    ppermute x9, waiting for transfers between devices: 9.17 us -> 9.79 us  [exchanged(): return lax.ppermute(value, 'pair', [(p, p ^ mask) for p in range(count)])]
  transfers between devices with their start and end apart: 16 -> 16, of which waited for: 14 -> 13; matrix products, arithmetic and copies ran while one was open for 2% -> 2% of each run, Pallas kernels for 7% -> 6%
where the time goes in v7:
time: 46.6 us; the launch traced here: 46.5 us
  starting transfers between devices  20.8 us (45%)
  waiting for transfers between devices  16.2 us (35%)
  Pallas kernels  7.9 us (17%)
  local copies, waits for them, and re-layouts  0.72 us (2%)
  between operations  0.71 us (2%)
    ppermute x9, starting transfers between devices, exchanged(): return lax.ppermute(value, 'pair', [(p, p ^ mask) for p in range(count)])  11.6 us
    ppermute x9, waiting for transfers between devices, exchanged(): return lax.ppermute(value, 'pair', [(p, p ^ mask) for p in range(count)])  9.79 us
    ppermute x4, starting transfers between devices, crossed(): return lax.ppermute(value, ('pair', 'dp'), pairs)  8.31 us
    ppermute x4, waiting for transfers between devices, crossed(): return lax.ppermute(value, ('pair', 'dp'), pairs)  4.9 us
    pallas_call x4, Pallas kernels, couple(): pl.pallas_call(functools.partial(couple_kernel, len(owns), len(parts)), i...  3.47 us
    pallas_call x1, Pallas kernels, project(): pl.pallas_call(project_kernel, in_specs=[hbm] * 4, out_specs=[vmem_spec()...  2.48 us
    ppermute x3, waiting for transfers between devices, swapped(): return lax.ppermute(value, 'dp', [(d, d ^ mask) for d in range(count)])  1.56 us
    ppermute x3, starting transfers between devices, swapped(): return lax.ppermute(value, 'dp', [(d, d ^ mask) for d in range(count)])  0.98 us
  transfers between devices with their start and end apart: 16, of which 13 were waited for; matrix products, arithmetic and copies ran while one was open for 2% of the time, Pallas kernels for 6%

profile of v7, /device:TPU:0, one launch (start us, length us, event | category | flops | bytes accessed | tf_op | source)
XLA Modules:
  0.0 46.5 jit_solution(14493445136889169832)
XLA Ops:
  0.6 2.5 %project.1 = (f32[512,128]{1,0:T(8,128)S(1)}, bf16[528,128]{1,0:T(8,128)(2,1)S(1)}, bf16[512,2048]{1,0:T(8,128)(2,1)S(1)}) custom-call(bf16[512,2048]{1,0:T(8,128)(2,1)} %features_ref.1, bf16[2048,128]{1,0:T(8,128)(2,1)} %weight_ref.1, bf16[4,128]{1,0:T(4,128)(2,1)} %bitcast.11, s32[4,128]{1,0:T(4,128)} %bitcast.10), custom_call_target="tpu_custom_call" | custom-call | tf_op jit(solution)/shard_map/project/pallas_call | solution.py:102
  3.1 0.5 %collective-permute-start.2 = (bf16[528,128]{1,0:T(8,128)(2,1)S(1)}, bf16[528,128]{1,0:T(8,128)(2,1)S(1)}, u32[]{:S(2)}, u32[]{:S(2)}) collective-permute-start(bf16[528,128]{1,0:T(8,128)(2,1)S(1)} %get-tuple-element.12.refs_2_), channel_id=1, source_target_pairs={{0,1},{1,0},{2,3},{3,2},{4,5},{5,4},{6,7},{7,6},{8,9},{9,8},{10,11... | collective-permute-start | bytes 405512 | tf_op jit(solution)/shard_map/ppermute | solution.py:21
  3.6 4.7 %collective-permute-start.4 = (bf16[528,128]{1,0:T(8,128)(2,1)S(1)}, bf16[528,128]{1,0:T(8,128)(2,1)S(1)}, u32[]{:S(2)}, u32[]{:S(2)}) collective-permute-start(bf16[528,128]{1,0:T(8,128)(2,1)S(1)} %get-tuple-element.12.refs_2_), channel_id=1, source_target_pairs={{0,24},{1,25},{2,26},{3,27},{4,28},{5,29},{6,30},{7,31},{8,16},{9,... | collective-permute-start | bytes 405512 | tf_op jit(solution)/shard_map/ppermute | solution.py:36
  8.3 1.9 %collective-permute-start.3 = (bf16[528,128]{1,0:T(8,128)(2,1)S(1)}, bf16[528,128]{1,0:T(8,128)(2,1)S(1)}, u32[]{:S(2)}, u32[]{:S(2)}) collective-permute-start(bf16[528,128]{1,0:T(8,128)(2,1)S(1)} %get-tuple-element.12.refs_2_), channel_id=1, source_target_pairs={{0,31},{1,30},{2,5},{3,4},{4,3},{5,2},{6,9},{7,8},{8,7},{9,6},{10,... | collective-permute-start | bytes 405512 | tf_op jit(solution)/shard_map/ppermute | solution.py:36
  10.2 0.8 %collective-permute-start = (bf16[528,128]{1,0:T(8,128)(2,1)S(1)}, bf16[528,128]{1,0:T(8,128)(2,1)S(1)}, u32[]{:S(2)}, u32[]{:S(2)}) collective-permute-start(bf16[528,128]{1,0:T(8,128)(2,1)S(1)} %get-tuple-element.12.refs_2_), channel_id=1, source_target_pairs={{0,3},{1,2},{2,1},{3,0},{4,7},{5,6},{6,5},{7,4},{8,11},{9,10},{10,... | collective-permute-start | bytes 405512 | tf_op jit(solution)/shard_map/ppermute | solution.py:36
  11.0 0.9 %collective-permute-start.1 = (bf16[528,128]{1,0:T(8,128)(2,1)S(1)}, bf16[528,128]{1,0:T(8,128)(2,1)S(1)}, u32[]{:S(2)}, u32[]{:S(2)}) collective-permute-start(bf16[528,128]{1,0:T(8,128)(2,1)S(1)} %get-tuple-element.12.refs_2_), channel_id=1, source_target_pairs={{0,9},{1,8},{2,11},{3,10},{4,13},{5,12},{6,15},{7,14},{8,1},{9,0},... | collective-permute-start | bytes 405512 | tf_op jit(solution)/shard_map/ppermute | solution.py:36
  11.9 0.8 %collective-permute-done.4.refs_3_ = bf16[528,128]{1,0:T(8,128)(2,1)S(1)} collective-permute-done((bf16[528,128]{1,0:T(8,128)(2,1)S(1)}, bf16[528,128]{1,0:T(8,128)(2,1)S(1)}, u32[]{:S(2)}, u32[]{:S(2)}) %collective-permute-start.4) | collective-permute-done | bytes 135200 | tf_op jit(solution)/shard_map/ppermute | solution.py:36
  12.8 1.0 %couple.4.refs_4_ = f32[2,512,128]{2,1,0:T(8,128)S(1)} custom-call(s32[1]{0:T(128)} %bitcast.6.refs_0_, bf16[528,128]{1,0:T(8,128)(2,1)S(1)} %collective-permute-done.2.refs_1_.refs_2_, bf16[528,128]{1,0:T(8,128)(2,1)S(1)} %get-tuple-element.12.refs_2_, bf16[528,128]{1,0:T(8,128)(2,1)S(1)} %collective-permute-done.4.refs_3_), custom_call_target="tpu_custom_call" | custom-call | flops 268435456 | bytes 262144 | tf_op jit(solution)/shard_map/couple/pallas_call | solution.py:194
  13.8 3.8 %collective-permute-done.3.refs_3_ = bf16[528,128]{1,0:T(8,128)(2,1)S(1)} collective-permute-done((bf16[528,128]{1,0:T(8,128)(2,1)S(1)}, bf16[528,128]{1,0:T(8,128)(2,1)S(1)}, u32[]{:S(2)}, u32[]{:S(2)}) %collective-permute-start.3) | collective-permute-done | bytes 135200 | tf_op jit(solution)/shard_map/ppermute | solution.py:36
  17.6 0.8 %couple.5.refs_5_ = f32[2,512,128]{2,1,0:T(8,128)S(1)} custom-call(s32[1]{0:T(128)} %bitcast.5.refs_0_, bf16[528,128]{1,0:T(8,128)(2,1)S(1)} %collective-permute-done.2.refs_1_.refs_2_, bf16[528,128]{1,0:T(8,128)(2,1)S(1)} %get-tuple-element.12.refs_2_, bf16[528,128]{1,0:T(8,128)(2,1)S(1)} %collective-permute-done.3.refs_3_, f32[2,512,128]{2,1,0:T(8,128)S(1)} %couple.4.refs_4_), custom_call_target="tpu_custom_call" | custom-call | flops 268435456 | bytes 262144 | tf_op jit(solution)/shard_map/couple/pallas_call | solution.py:194
  18.7 0.8 %couple.7 = f32[1,512,128]{2,1,0:T(8,128)S(1)} custom-call(s32[1]{0:T(128)} %bitcast.1.refs_0_, s32[1]{0:T(128)} %bitcast.2.refs_1_, bf16[528,128]{1,0:T(8,128)(2,1)S(1)} %collective-permute-done.2.refs_1_.refs_2_, bf16[528,128]{1,0:T(8,128)(2,1)S(1)} %collective-permute-done.refs_3_, bf16[528,128]{1,0:T(8,128)(2,1)S(1)} %collective-permute-done.1.refs_4_, ...), custom_call_target="tpu_custom_call" | custom-call | flops 268435456 | bytes 262144 | tf_op jit(solution)/shard_map/couple/pallas_call | solution.py:194
  19.8 0.8 %couple.6.acc_ref = f32[1,512,128]{2,1,0:T(8,128)S(1)} custom-call(s32[1]{0:T(128)} %bitcast.1.refs_0_, s32[1]{0:T(128)} %bitcast.2.refs_1_, bf16[528,128]{1,0:T(8,128)(2,1)S(1)} %get-tuple-element.12.refs_2_, bf16[528,128]{1,0:T(8,128)(2,1)S(1)} %collective-permute-done.refs_3_, bf16[528,128]{1,0:T(8,128)(2,1)S(1)} %collective-permute-done.1.refs_4_, ...), custom_call_target="tpu_custom_call" | custom-call | flops 268435456 | bytes 262144 | tf_op jit(solution)/shard_map/couple/pallas_call | solution.py:194
  20.6 0.5 %collective-permute-done.5.refs_0_ = f32[512,128]{1,0:T(8,128)S(1)} collective-permute-done((f32[512,128]{1,0:T(8,128)S(1)}, f32[512,128]{1,0:T(8,128)S(1)}, u32[]{:S(2)}, u32[]{:S(2)}) %collective-permute-start.5) | collective-permute-done | bytes 262176 | tf_op jit(solution)/shard_map/ppermute | solution.py:21
  21.1 0.6 %finish.1 = (f32[512,128]{1,0:T(8,128)S(1)}, bf16[128,512]{1,0:T(8,128)(2,1)S(1)}, bf16[128,1024]{1,0:T(8,128)(2,1)S(1)}) custom-call(s32[1]{0:T(128)} %bitcast.core_ref.share_ref, f32[1,512,128]{2,1,0:T(8,128)S(1)} %couple.6.acc_ref, f32[512,128]{1,0:T(8,128)S(1)} %get-tuple-element.13.projected_ref, bf16[512,2048]{1,0:T(8,128)(2,1)S(1)} %get-tuple-element.14.features_ref, ...), custom_call_target="tpu_custom_call" | custom-call | tf_op jit(solution)/shard_map/finish/pallas_call | solution.py:238
  22.3 1.0 %collective-permute-done.6.refs_0_ = bf16[128,1024]{1,0:T(8,128)(2,1)S(1)} collective-permute-done((bf16[128,1024]{1,0:T(8,128)(2,1)S(1)}, bf16[128,1024]{1,0:T(8,128)(2,1)S(1)}, u32[]{:S(2)}, u32[]{:S(2)}) %collective-permute-start.6) | collective-permute-done | bytes 262176 | tf_op jit(solution)/shard_map/ppermute | solution.py:21
  23.4 0.8 %collective-permute-start.7 = (bf16[128,256]{1,0:T(8,128)(2,1)S(1)}, bf16[128,256]{1,0:T(8,128)(2,1)S(1)}, u32[]{:S(2)}, u32[]{:S(2)}) collective-permute-start(bf16[128,256]{1,0:T(8,128)(2,1)S(1)} %get-tuple-element.19), channel_id=1, source_target_pairs={{0,2},{2,0},{4,6},{6,4},{8,10},{10,8},{12,14},{14,12},{16,18},{18,... | collective-permute-start | bytes 196616 | tf_op jit(solution)/shard_map/ppermute | solution.py:26
  24.2 2.3 %collective-permute-start.8 = (bf16[128,256]{1,0:T(8,128)(2,1)S(1)}, bf16[128,256]{1,0:T(8,128)(2,1)S(1)}, u32[]{:S(2)}, u32[]{:S(2)}) collective-permute-start(bf16[128,256]{1,0:T(8,128)(2,1)S(1)} %get-tuple-element.20), channel_id=1, source_target_pairs={{0,4},{2,6},{4,0},{6,2},{8,12},{10,14},{12,8},{14,10},{16,20},{18,... | collective-permute-start | bytes 196616 | tf_op jit(solution)/shard_map/ppermute | solution.py:26
  27.0 0.8 %collective-permute-done.7 = bf16[128,256]{1,0:T(8,128)(2,1)S(1)} collective-permute-done((bf16[128,256]{1,0:T(8,128)(2,1)S(1)}, bf16[128,256]{1,0:T(8,128)(2,1)S(1)}, u32[]{:S(2)}, u32[]{:S(2)}) %collective-permute-start.7) | collective-permute-done | bytes 65568 | tf_op jit(solution)/shard_map/ppermute | solution.py:26
  27.7 1.7 %collective-permute-done.8 = bf16[128,256]{1,0:T(8,128)(2,1)S(1)} collective-permute-done((bf16[128,256]{1,0:T(8,128)(2,1)S(1)}, bf16[128,256]{1,0:T(8,128)(2,1)S(1)}, u32[]{:S(2)}, u32[]{:S(2)}) %collective-permute-start.8) | collective-permute-done | bytes 65568 | tf_op jit(solution)/shard_map/ppermute | solution.py:26
  29.5 2.2 %collective-permute-done.9 = bf16[128,256]{1,0:T(8,128)(2,1)S(1)} collective-permute-done((bf16[128,256]{1,0:T(8,128)(2,1)S(1)}, bf16[128,256]{1,0:T(8,128)(2,1)S(1)}, u32[]{:S(2)}, u32[]{:S(2)}) %collective-permute-start.9) | collective-permute-done | bytes 65568 | tf_op jit(solution)/shard_map/ppermute | solution.py:26
  31.7 1.1 %collective-permute-start.10 = (bf16[128,256]{1,0:T(8,128)(2,1)S(1)}, bf16[128,256]{1,0:T(8,128)(2,1)S(1)}, u32[]{:S(2)}, u32[]{:S(2)}) collective-permute-start(bf16[128,256]{1,0:T(8,128)(2,1)S(1)} %add_convert_fusion.1), channel_id=1, source_target_pairs={{0,24},{2,26},{4,28},{6,30},{8,16},{10,18},{12,20},{14,22},{16,8},... | collective-permute-start | bytes 196616 | tf_op jit(solution)/shard_map/ppermute | solution.py:26
  33.0 3.1 %collective-permute-start.12 = (bf16[128,256]{1,0:T(8,128)(2,1)S(1)}, bf16[128,256]{1,0:T(8,128)(2,1)S(1)}, u32[]{:S(2)}, u32[]{:S(2)}) collective-permute-start(bf16[128,256]{1,0:T(8,128)(2,1)S(1)} %add_convert_fusion.1), channel_id=1, source_target_pairs={{0,16},{2,18},{4,20},{6,22},{8,24},{10,26},{12,28},{14,30},{16,0},... | collective-permute-start | bytes 196616 | tf_op jit(solution)/shard_map/ppermute | solution.py:26
  36.1 1.7 %collective-permute-done.10 = bf16[128,256]{1,0:T(8,128)(2,1)S(1)} collective-permute-done((bf16[128,256]{1,0:T(8,128)(2,1)S(1)}, bf16[128,256]{1,0:T(8,128)(2,1)S(1)}, u32[]{:S(2)}, u32[]{:S(2)}) %collective-permute-start.10) | collective-permute-done | bytes 65568 | tf_op jit(solution)/shard_map/ppermute | solution.py:26
  37.9 0.9 %collective-permute-done.12 = bf16[128,256]{1,0:T(8,128)(2,1)S(1)} collective-permute-done((bf16[128,256]{1,0:T(8,128)(2,1)S(1)}, bf16[128,256]{1,0:T(8,128)(2,1)S(1)}, u32[]{:S(2)}, u32[]{:S(2)}) %collective-permute-start.12) | collective-permute-done | bytes 65568 | tf_op jit(solution)/shard_map/ppermute | solution.py:26
  38.8 1.9 %collective-permute-start.13 = (bf16[128,256]{1,0:T(8,128)(2,1)S(1)}, bf16[128,256]{1,0:T(8,128)(2,1)S(1)}, u32[]{:S(2)}, u32[]{:S(2)}) collective-permute-start(bf16[128,256]{1,0:T(8,128)(2,1)S(1)} %add_convert_fusion.refs_3_), channel_id=1, source_target_pairs={{0,6},{2,4},{4,2},{6,0},{8,14},{10,12},{12,10},{14,8},{16,22},{18,... | collective-permute-start | bytes 196616 | tf_op jit(solution)/shard_map/ppermute | solution.py:26
  40.7 0.5 %collective-permute-start.14 = (bf16[128,256]{1,0:T(8,128)(2,1)S(1)}, bf16[128,256]{1,0:T(8,128)(2,1)S(1)}, u32[]{:S(2)}, u32[]{:S(2)}) collective-permute-start(bf16[128,256]{1,0:T(8,128)(2,1)S(1)} %add_convert_fusion.refs_3_), channel_id=1, source_target_pairs={{0,4},{2,6},{4,0},{6,2},{8,12},{10,14},{12,8},{14,10},{16,20},{18,... | collective-permute-start | bytes 196616 | tf_op jit(solution)/shard_map/ppermute | solution.py:26
  41.3 1.1 %collective-permute-start.15 = (bf16[128,256]{1,0:T(8,128)(2,1)S(1)}, bf16[128,256]{1,0:T(8,128)(2,1)S(1)}, u32[]{:S(2)}, u32[]{:S(2)}) collective-permute-start(bf16[128,256]{1,0:T(8,128)(2,1)S(1)} %add_convert_fusion.refs_3_), channel_id=1, source_target_pairs={{0,2},{2,0},{4,6},{6,4},{8,10},{10,8},{12,14},{14,12},{16,18},{18,... | collective-permute-start | bytes 196616 | tf_op jit(solution)/shard_map/ppermute | solution.py:26
  42.4 0.7 %copy.6 = f32[512,128]{1,0:T(8,128)} copy(f32[512,128]{1,0:T(8,128)S(1)} %get-tuple-element.22) | data formatting | bytes 524288
  43.1 1.0 %collective-permute-done.13.refs_0_ = bf16[128,256]{1,0:T(8,128)(2,1)S(1)} collective-permute-done((bf16[128,256]{1,0:T(8,128)(2,1)S(1)}, bf16[128,256]{1,0:T(8,128)(2,1)S(1)}, u32[]{:S(2)}, u32[]{:S(2)}) %collective-permute-start.13) | collective-permute-done | bytes 65568 | tf_op jit(solution)/shard_map/ppermute | solution.py:26
  44.1 1.0 %collective-permute-done.14.refs_1_ = bf16[128,256]{1,0:T(8,128)(2,1)S(1)} collective-permute-done((bf16[128,256]{1,0:T(8,128)(2,1)S(1)}, bf16[128,256]{1,0:T(8,128)(2,1)S(1)}, u32[]{:S(2)}, u32[]{:S(2)}) %collective-permute-start.14) | collective-permute-done | bytes 65568 | tf_op jit(solution)/shard_map/ppermute | solution.py:26
  45.0 0.5 %collective-permute-done.15.refs_2_ = bf16[128,256]{1,0:T(8,128)(2,1)S(1)} collective-permute-done((bf16[128,256]{1,0:T(8,128)(2,1)S(1)}, bf16[128,256]{1,0:T(8,128)(2,1)S(1)}, u32[]{:S(2)}, u32[]{:S(2)}) %collective-permute-start.15) | collective-permute-done | bytes 65568 | tf_op jit(solution)/shard_map/ppermute | solution.py:26
  45.6 0.9 %join.1 = f32[1024,128]{1,0:T(8,128)} custom-call(s32[1]{0:T(128)} %bitcast.8.digit_ref, bf16[128,256]{1,0:T(8,128)(2,1)S(1)} %collective-permute-done.13.refs_0_, bf16[128,256]{1,0:T(8,128)(2,1)S(1)} %collective-permute-done.14.refs_1_, bf16[128,256]{1,0:T(8,128)(2,1)S(1)} %collective-permute-done.15.refs_2_, bf16[128,256]{1,0:T(8,128)(2,1)S(1)} %add_convert_fusion.refs_3_), custom_call_target="tpu_custom_call" | custom-call | tf_op jit(solution)/shard_map/join/pallas_call | solution.py:309
  (13 shorter events, 1.9 us)
Async XLA Ops:
  3.1 8.8 %collective-permute-start.2 = (bf16[528,128]{1,0:T(8,128)(2,1)S(1)}, bf16[528,128]{1,0:T(8,128)(2,1)S(1)}, u32[]{:S(2)}, u32[]{:S(2)}) collective-permute-start(bf16[528,128]{1,0:T(8,128)(2,1)S(1)} %get-tuple-element.12.refs_2_), channel_id=1, source_target_pairs={{0,1},{1,0},{2,3},{3,2},{4,5},{5,4},{6,7},{7,6},{8,9},{9,8},{10,11... | collective-permute-start | bytes 405512 | tf_op jit(solution)/shard_map/ppermute | solution.py:21
  3.6 9.2 %collective-permute-start.4 = (bf16[528,128]{1,0:T(8,128)(2,1)S(1)}, bf16[528,128]{1,0:T(8,128)(2,1)S(1)}, u32[]{:S(2)}, u32[]{:S(2)}) collective-permute-start(bf16[528,128]{1,0:T(8,128)(2,1)S(1)} %get-tuple-element.12.refs_2_), channel_id=1, source_target_pairs={{0,24},{1,25},{2,26},{3,27},{4,28},{5,29},{6,30},{7,31},{8,16},{9,... | collective-permute-start | bytes 405512 | tf_op jit(solution)/shard_map/ppermute | solution.py:36
  8.3 9.3 %collective-permute-start.3 = (bf16[528,128]{1,0:T(8,128)(2,1)S(1)}, bf16[528,128]{1,0:T(8,128)(2,1)S(1)}, u32[]{:S(2)}, u32[]{:S(2)}) collective-permute-start(bf16[528,128]{1,0:T(8,128)(2,1)S(1)} %get-tuple-element.12.refs_2_), channel_id=1, source_target_pairs={{0,31},{1,30},{2,5},{3,4},{4,3},{5,2},{6,9},{7,8},{8,7},{9,6},{10,... | collective-permute-start | bytes 405512 | tf_op jit(solution)/shard_map/ppermute | solution.py:36
  10.2 8.2 %collective-permute-start = (bf16[528,128]{1,0:T(8,128)(2,1)S(1)}, bf16[528,128]{1,0:T(8,128)(2,1)S(1)}, u32[]{:S(2)}, u32[]{:S(2)}) collective-permute-start(bf16[528,128]{1,0:T(8,128)(2,1)S(1)} %get-tuple-element.12.refs_2_), channel_id=1, source_target_pairs={{0,3},{1,2},{2,1},{3,0},{4,7},{5,6},{6,5},{7,4},{8,11},{9,10},{10,... | collective-permute-start | bytes 405512 | tf_op jit(solution)/shard_map/ppermute | solution.py:36
  11.0 7.7 %collective-permute-start.1 = (bf16[528,128]{1,0:T(8,128)(2,1)S(1)}, bf16[528,128]{1,0:T(8,128)(2,1)S(1)}, u32[]{:S(2)}, u32[]{:S(2)}) collective-permute-start(bf16[528,128]{1,0:T(8,128)(2,1)S(1)} %get-tuple-element.12.refs_2_), channel_id=1, source_target_pairs={{0,9},{1,8},{2,11},{3,10},{4,13},{5,12},{6,15},{7,14},{8,1},{9,0},... | collective-permute-start | bytes 405512 | tf_op jit(solution)/shard_map/ppermute | solution.py:36
  19.5 1.6 %collective-permute-start.5 = (f32[512,128]{1,0:T(8,128)S(1)}, f32[512,128]{1,0:T(8,128)S(1)}, u32[]{:S(2)}, u32[]{:S(2)}) collective-permute-start(f32[512,128]{1,0:T(8,128)S(1)} %bitcast.9), channel_id=1, source_target_pairs={{0,1},{1,0},{2,3},{3,2},{4,5},{5,4},{6,7},{7,6},{8,9},{9,8},{10,11... | collective-permute-start | bytes 786440 | tf_op jit(solution)/shard_map/ppermute | solution.py:21
  21.7 1.6 %collective-permute-start.6 = (bf16[128,1024]{1,0:T(8,128)(2,1)S(1)}, bf16[128,1024]{1,0:T(8,128)(2,1)S(1)}, u32[]{:S(2)}, u32[]{:S(2)}) collective-permute-start(bf16[128,1024]{1,0:T(8,128)(2,1)S(1)} %get-tuple-element.17), channel_id=1, source_target_pairs={{0,1},{1,0},{2,3},{3,2},{4,5},{5,4},{6,7},{7,6},{8,9},{9,8},{10,11... | collective-permute-start | bytes 786440 | tf_op jit(solution)/shard_map/ppermute | solution.py:21
  23.4 4.3 %collective-permute-start.7 = (bf16[128,256]{1,0:T(8,128)(2,1)S(1)}, bf16[128,256]{1,0:T(8,128)(2,1)S(1)}, u32[]{:S(2)}, u32[]{:S(2)}) collective-permute-start(bf16[128,256]{1,0:T(8,128)(2,1)S(1)} %get-tuple-element.19), channel_id=1, source_target_pairs={{0,2},{2,0},{4,6},{6,4},{8,10},{10,8},{12,14},{14,12},{16,18},{18,... | collective-permute-start | bytes 196616 | tf_op jit(solution)/shard_map/ppermute | solution.py:26
  24.2 5.3 %collective-permute-start.8 = (bf16[128,256]{1,0:T(8,128)(2,1)S(1)}, bf16[128,256]{1,0:T(8,128)(2,1)S(1)}, u32[]{:S(2)}, u32[]{:S(2)}) collective-permute-start(bf16[128,256]{1,0:T(8,128)(2,1)S(1)} %get-tuple-element.20), channel_id=1, source_target_pairs={{0,4},{2,6},{4,0},{6,2},{8,12},{10,14},{12,8},{14,10},{16,20},{18,... | collective-permute-start | bytes 196616 | tf_op jit(solution)/shard_map/ppermute | solution.py:26
  26.5 5.2 %collective-permute-start.9 = (bf16[128,256]{1,0:T(8,128)(2,1)S(1)}, bf16[128,256]{1,0:T(8,128)(2,1)S(1)}, u32[]{:S(2)}, u32[]{:S(2)}) collective-permute-start(bf16[128,256]{1,0:T(8,128)(2,1)S(1)} %get-tuple-element.21), channel_id=1, source_target_pairs={{0,6},{2,4},{4,2},{6,0},{8,14},{10,12},{12,10},{14,8},{16,22},{18,... | collective-permute-start | bytes 196616 | tf_op jit(solution)/shard_map/ppermute | solution.py:26
  31.7 6.2 %collective-permute-start.10 = (bf16[128,256]{1,0:T(8,128)(2,1)S(1)}, bf16[128,256]{1,0:T(8,128)(2,1)S(1)}, u32[]{:S(2)}, u32[]{:S(2)}) collective-permute-start(bf16[128,256]{1,0:T(8,128)(2,1)S(1)} %add_convert_fusion.1), channel_id=1, source_target_pairs={{0,24},{2,26},{4,28},{6,30},{8,16},{10,18},{12,20},{14,22},{16,8},... | collective-permute-start | bytes 196616 | tf_op jit(solution)/shard_map/ppermute | solution.py:26
  32.8 5.0 %collective-permute-start.11 = (bf16[128,256]{1,0:T(8,128)(2,1)S(1)}, bf16[128,256]{1,0:T(8,128)(2,1)S(1)}, u32[]{:S(2)}, u32[]{:S(2)}) collective-permute-start(bf16[128,256]{1,0:T(8,128)(2,1)S(1)} %add_convert_fusion.1), channel_id=1, source_target_pairs={{0,8},{2,10},{4,12},{6,14},{8,0},{10,2},{12,4},{14,6},{16,24},{18,... | collective-permute-start | bytes 196616 | tf_op jit(solution)/shard_map/ppermute | solution.py:26
  33.0 5.7 %collective-permute-start.12 = (bf16[128,256]{1,0:T(8,128)(2,1)S(1)}, bf16[128,256]{1,0:T(8,128)(2,1)S(1)}, u32[]{:S(2)}, u32[]{:S(2)}) collective-permute-start(bf16[128,256]{1,0:T(8,128)(2,1)S(1)} %add_convert_fusion.1), channel_id=1, source_target_pairs={{0,16},{2,18},{4,20},{6,22},{8,24},{10,26},{12,28},{14,30},{16,0},... | collective-permute-start | bytes 196616 | tf_op jit(solution)/shard_map/ppermute | solution.py:26
  38.8 5.2 %collective-permute-start.13 = (bf16[128,256]{1,0:T(8,128)(2,1)S(1)}, bf16[128,256]{1,0:T(8,128)(2,1)S(1)}, u32[]{:S(2)}, u32[]{:S(2)}) collective-permute-start(bf16[128,256]{1,0:T(8,128)(2,1)S(1)} %add_convert_fusion.refs_3_), channel_id=1, source_target_pairs={{0,6},{2,4},{4,2},{6,0},{8,14},{10,12},{12,10},{14,8},{16,22},{18,... | collective-permute-start | bytes 196616 | tf_op jit(solution)/shard_map/ppermute | solution.py:26
  40.7 4.3 %collective-permute-start.14 = (bf16[128,256]{1,0:T(8,128)(2,1)S(1)}, bf16[128,256]{1,0:T(8,128)(2,1)S(1)}, u32[]{:S(2)}, u32[]{:S(2)}) collective-permute-start(bf16[128,256]{1,0:T(8,128)(2,1)S(1)} %add_convert_fusion.refs_3_), channel_id=1, source_target_pairs={{0,4},{2,6},{4,0},{6,2},{8,12},{10,14},{12,8},{14,10},{16,20},{18,... | collective-permute-start | bytes 196616 | tf_op jit(solution)/shard_map/ppermute | solution.py:26
  41.3 4.3 %collective-permute-start.15 = (bf16[128,256]{1,0:T(8,128)(2,1)S(1)}, bf16[128,256]{1,0:T(8,128)(2,1)S(1)}, u32[]{:S(2)}, u32[]{:S(2)}) collective-permute-start(bf16[128,256]{1,0:T(8,128)(2,1)S(1)} %add_convert_fusion.refs_3_), channel_id=1, source_target_pairs={{0,2},{2,0},{4,6},{6,4},{8,10},{10,8},{12,14},{14,12},{16,18},{18,... | collective-permute-start | bytes 196616 | tf_op jit(solution)/shard_map/ppermute | solution.py:26

commit v8 on v7

--- a/solution.py
+++ b/solution.py
@@ -343,9 +343,9 @@
     owns = siblings + [packed]
     acc = couple([base_c], owns, [far_odd])
     acc = couple([base_d], owns, [near_odd], (acc,))
-    acc_siblings = couple([base_a, base_b], siblings, [near_even, far_even], (acc,))
+    acc_siblings = couple([base_b, base_a], siblings, [far_even, near_even], (acc,))
     returned = [swapped(acc_siblings[mask - 1], mask) for mask in range(1, dp_count)]
-    acc = couple([base_a, base_b], [packed], [near_even, far_even], (acc[dp_count - 1 :],))
+    acc = couple([base_b, base_a], [packed], [far_even, near_even], (acc[dp_count - 1 :],))
     grad_embed, half, *sends = finish(core, acc, projected, held, returned, dp_count)
     received = [swapped(send, mask) for mask, send in enumerate(sends, 1)]
     mine = weight_term(half, held, core, dp_count)

time: 46.6 us -> 46.6 us (level)
  transfers between devices with their start and end apart: 16 -> 16, of which waited for: 13 -> 14; matrix products, arithmetic and copies ran while one was open for 2% -> 2% of each run, Pallas kernels for 6% -> 6%
where the time goes in v8:
time: 46.6 us; the launch traced here: 46.5 us
  starting transfers between devices  20.9 us (45%)
  waiting for transfers between devices  16.2 us (35%)
  Pallas kernels  7.91 us (17%)
  local copies, waits for them, and re-layouts  0.72 us (2%)
  between operations  0.7 us (2%)
    ppermute x9, starting transfers between devices, exchanged(): return lax.ppermute(value, 'pair', [(p, p ^ mask) for p in range(count)])  11.6 us
    ppermute x9, waiting for transfers between devices, exchanged(): return lax.ppermute(value, 'pair', [(p, p ^ mask) for p in range(count)])  9.77 us
    ppermute x4, starting transfers between devices, crossed(): return lax.ppermute(value, ('pair', 'dp'), pairs)  8.31 us
    ppermute x4, waiting for transfers between devices, crossed(): return lax.ppermute(value, ('pair', 'dp'), pairs)  4.91 us
    pallas_call x4, Pallas kernels, couple(): pl.pallas_call(functools.partial(couple_kernel, len(owns), len(parts)), i...  3.47 us
    pallas_call x1, Pallas kernels, project(): pl.pallas_call(project_kernel, in_specs=[hbm] * 4, out_specs=[vmem_spec()...  2.48 us
    ppermute x3, waiting for transfers between devices, swapped(): return lax.ppermute(value, 'dp', [(d, d ^ mask) for d in range(count)])  1.56 us
    ppermute x3, starting transfers between devices, swapped(): return lax.ppermute(value, 'dp', [(d, d ^ mask) for d in range(count)])  0.98 us
  transfers between devices with their start and end apart: 16, of which 14 were waited for; matrix products, arithmetic and copies ran while one was open for 2% of the time, Pallas kernels for 6%

profile of v8, /device:TPU:0, one launch (start us, length us, event | category | flops | bytes accessed | tf_op | source)
XLA Modules:
  0.0 46.5 jit_solution(16011758663086212584)
XLA Ops:
  0.6 2.5 %project.1 = (f32[512,128]{1,0:T(8,128)S(1)}, bf16[528,128]{1,0:T(8,128)(2,1)S(1)}, bf16[512,2048]{1,0:T(8,128)(2,1)S(1)}) custom-call(bf16[512,2048]{1,0:T(8,128)(2,1)} %features_ref.1, bf16[2048,128]{1,0:T(8,128)(2,1)} %weight_ref.1, bf16[4,128]{1,0:T(4,128)(2,1)} %bitcast.11, s32[4,128]{1,0:T(4,128)} %bitcast.10), custom_call_target="tpu_custom_call" | custom-call | tf_op jit(solution)/shard_map/project/pallas_call | solution.py:102
  3.1 0.5 %collective-permute-start.2 = (bf16[528,128]{1,0:T(8,128)(2,1)S(1)}, bf16[528,128]{1,0:T(8,128)(2,1)S(1)}, u32[]{:S(2)}, u32[]{:S(2)}) collective-permute-start(bf16[528,128]{1,0:T(8,128)(2,1)S(1)} %get-tuple-element.12.refs_2_), channel_id=1, source_target_pairs={{0,1},{1,0},{2,3},{3,2},{4,5},{5,4},{6,7},{7,6},{8,9},{9,8},{10,11... | collective-permute-start | bytes 405512 | tf_op jit(solution)/shard_map/ppermute | solution.py:21
  3.6 4.7 %collective-permute-start.4 = (bf16[528,128]{1,0:T(8,128)(2,1)S(1)}, bf16[528,128]{1,0:T(8,128)(2,1)S(1)}, u32[]{:S(2)}, u32[]{:S(2)}) collective-permute-start(bf16[528,128]{1,0:T(8,128)(2,1)S(1)} %get-tuple-element.12.refs_2_), channel_id=1, source_target_pairs={{0,24},{1,25},{2,26},{3,27},{4,28},{5,29},{6,30},{7,31},{8,16},{9,... | collective-permute-start | bytes 405512 | tf_op jit(solution)/shard_map/ppermute | solution.py:36
  8.3 1.9 %collective-permute-start.3 = (bf16[528,128]{1,0:T(8,128)(2,1)S(1)}, bf16[528,128]{1,0:T(8,128)(2,1)S(1)}, u32[]{:S(2)}, u32[]{:S(2)}) collective-permute-start(bf16[528,128]{1,0:T(8,128)(2,1)S(1)} %get-tuple-element.12.refs_2_), channel_id=1, source_target_pairs={{0,31},{1,30},{2,5},{3,4},{4,3},{5,2},{6,9},{7,8},{8,7},{9,6},{10,... | collective-permute-start | bytes 405512 | tf_op jit(solution)/shard_map/ppermute | solution.py:36
  10.2 1.7 %collective-permute-start = (bf16[528,128]{1,0:T(8,128)(2,1)S(1)}, bf16[528,128]{1,0:T(8,128)(2,1)S(1)}, u32[]{:S(2)}, u32[]{:S(2)}) collective-permute-start(bf16[528,128]{1,0:T(8,128)(2,1)S(1)} %get-tuple-element.12.refs_2_), channel_id=1, source_target_pairs={{0,9},{1,8},{2,11},{3,10},{4,13},{5,12},{6,15},{7,14},{8,1},{9,0},... | collective-permute-start | bytes 405512 | tf_op jit(solution)/shard_map/ppermute | solution.py:36
  11.9 0.8 %collective-permute-done.4.refs_3_ = bf16[528,128]{1,0:T(8,128)(2,1)S(1)} collective-permute-done((bf16[528,128]{1,0:T(8,128)(2,1)S(1)}, bf16[528,128]{1,0:T(8,128)(2,1)S(1)}, u32[]{:S(2)}, u32[]{:S(2)}) %collective-permute-start.4) | collective-permute-done | bytes 135200 | tf_op jit(solution)/shard_map/ppermute | solution.py:36
  12.8 1.0 %couple.4.refs_4_ = f32[2,512,128]{2,1,0:T(8,128)S(1)} custom-call(s32[1]{0:T(128)} %bitcast.6.refs_0_, bf16[528,128]{1,0:T(8,128)(2,1)S(1)} %collective-permute-done.2.refs_1_.refs_2_, bf16[528,128]{1,0:T(8,128)(2,1)S(1)} %get-tuple-element.12.refs_2_, bf16[528,128]{1,0:T(8,128)(2,1)S(1)} %collective-permute-done.4.refs_3_), custom_call_target="tpu_custom_call" | custom-call | flops 268435456 | bytes 262144 | tf_op jit(solution)/shard_map/couple/pallas_call | solution.py:194
  13.8 3.8 %collective-permute-done.3.refs_3_ = bf16[528,128]{1,0:T(8,128)(2,1)S(1)} collective-permute-done((bf16[528,128]{1,0:T(8,128)(2,1)S(1)}, bf16[528,128]{1,0:T(8,128)(2,1)S(1)}, u32[]{:S(2)}, u32[]{:S(2)}) %collective-permute-start.3) | collective-permute-done | bytes 135200 | tf_op jit(solution)/shard_map/ppermute | solution.py:36
  17.6 0.8 %couple.5.refs_5_ = f32[2,512,128]{2,1,0:T(8,128)S(1)} custom-call(s32[1]{0:T(128)} %bitcast.5.refs_0_, bf16[528,128]{1,0:T(8,128)(2,1)S(1)} %collective-permute-done.2.refs_1_.refs_2_, bf16[528,128]{1,0:T(8,128)(2,1)S(1)} %get-tuple-element.12.refs_2_, bf16[528,128]{1,0:T(8,128)(2,1)S(1)} %collective-permute-done.3.refs_3_, f32[2,512,128]{2,1,0:T(8,128)S(1)} %couple.4.refs_4_), custom_call_target="tpu_custom_call" | custom-call | flops 268435456 | bytes 262144 | tf_op jit(solution)/shard_map/couple/pallas_call | solution.py:194
  18.7 0.8 %couple.7 = f32[1,512,128]{2,1,0:T(8,128)S(1)} custom-call(s32[1]{0:T(128)} %bitcast.1.refs_0_, s32[1]{0:T(128)} %bitcast.2.refs_1_, bf16[528,128]{1,0:T(8,128)(2,1)S(1)} %collective-permute-done.2.refs_1_.refs_2_, bf16[528,128]{1,0:T(8,128)(2,1)S(1)} %collective-permute-done.refs_3_, bf16[528,128]{1,0:T(8,128)(2,1)S(1)} %collective-permute-done.1.refs_4_, ...), custom_call_target="tpu_custom_call" | custom-call | flops 268435456 | bytes 262144 | tf_op jit(solution)/shard_map/couple/pallas_call | solution.py:194
  19.8 0.8 %couple.6.acc_ref = f32[1,512,128]{2,1,0:T(8,128)S(1)} custom-call(s32[1]{0:T(128)} %bitcast.1.refs_0_, s32[1]{0:T(128)} %bitcast.2.refs_1_, bf16[528,128]{1,0:T(8,128)(2,1)S(1)} %get-tuple-element.12.refs_2_, bf16[528,128]{1,0:T(8,128)(2,1)S(1)} %collective-permute-done.refs_3_, bf16[528,128]{1,0:T(8,128)(2,1)S(1)} %collective-permute-done.1.refs_4_, ...), custom_call_target="tpu_custom_call" | custom-call | flops 268435456 | bytes 262144 | tf_op jit(solution)/shard_map/couple/pallas_call | solution.py:194
  20.6 0.5 %collective-permute-done.5.refs_0_ = f32[512,128]{1,0:T(8,128)S(1)} collective-permute-done((f32[512,128]{1,0:T(8,128)S(1)}, f32[512,128]{1,0:T(8,128)S(1)}, u32[]{:S(2)}, u32[]{:S(2)}) %collective-permute-start.5) | collective-permute-done | bytes 262176 | tf_op jit(solution)/shard_map/ppermute | solution.py:21
  21.1 0.6 %finish.1 = (f32[512,128]{1,0:T(8,128)S(1)}, bf16[128,512]{1,0:T(8,128)(2,1)S(1)}, bf16[128,1024]{1,0:T(8,128)(2,1)S(1)}) custom-call(s32[1]{0:T(128)} %bitcast.core_ref.share_ref, f32[1,512,128]{2,1,0:T(8,128)S(1)} %couple.6.acc_ref, f32[512,128]{1,0:T(8,128)S(1)} %get-tuple-element.13.projected_ref, bf16[512,2048]{1,0:T(8,128)(2,1)S(1)} %get-tuple-element.14.features_ref, ...), custom_call_target="tpu_custom_call" | custom-call | tf_op jit(solution)/shard_map/finish/pallas_call | solution.py:238
  22.3 1.0 %collective-permute-done.6.refs_0_ = bf16[128,1024]{1,0:T(8,128)(2,1)S(1)} collective-permute-done((bf16[128,1024]{1,0:T(8,128)(2,1)S(1)}, bf16[128,1024]{1,0:T(8,128)(2,1)S(1)}, u32[]{:S(2)}, u32[]{:S(2)}) %collective-permute-start.6) | collective-permute-done | bytes 262176 | tf_op jit(solution)/shard_map/ppermute | solution.py:21
  23.4 1.8 %collective-permute-start.7 = (bf16[128,256]{1,0:T(8,128)(2,1)S(1)}, bf16[128,256]{1,0:T(8,128)(2,1)S(1)}, u32[]{:S(2)}, u32[]{:S(2)}) collective-permute-start(bf16[128,256]{1,0:T(8,128)(2,1)S(1)} %get-tuple-element.19), channel_id=1, source_target_pairs={{0,2},{2,0},{4,6},{6,4},{8,10},{10,8},{12,14},{14,12},{16,18},{18,... | collective-permute-start | bytes 196616 | tf_op jit(solution)/shard_map/ppermute | solution.py:26
  25.2 1.0 %collective-permute-start.8 = (bf16[128,256]{1,0:T(8,128)(2,1)S(1)}, bf16[128,256]{1,0:T(8,128)(2,1)S(1)}, u32[]{:S(2)}, u32[]{:S(2)}) collective-permute-start(bf16[128,256]{1,0:T(8,128)(2,1)S(1)} %get-tuple-element.20), channel_id=1, source_target_pairs={{0,4},{2,6},{4,0},{6,2},{8,12},{10,14},{12,8},{14,10},{16,20},{18,... | collective-permute-start | bytes 196616 | tf_op jit(solution)/shard_map/ppermute | solution.py:26
  26.2 0.8 %collective-permute-start.9 = (bf16[128,256]{1,0:T(8,128)(2,1)S(1)}, bf16[128,256]{1,0:T(8,128)(2,1)S(1)}, u32[]{:S(2)}, u32[]{:S(2)}) collective-permute-start(bf16[128,256]{1,0:T(8,128)(2,1)S(1)} %get-tuple-element.21), channel_id=1, source_target_pairs={{0,6},{2,4},{4,2},{6,0},{8,14},{10,12},{12,10},{14,8},{16,22},{18,... | collective-permute-start | bytes 196616 | tf_op jit(solution)/shard_map/ppermute | solution.py:26
  27.0 0.8 %collective-permute-done.7 = bf16[128,256]{1,0:T(8,128)(2,1)S(1)} collective-permute-done((bf16[128,256]{1,0:T(8,128)(2,1)S(1)}, bf16[128,256]{1,0:T(8,128)(2,1)S(1)}, u32[]{:S(2)}, u32[]{:S(2)}) %collective-permute-start.7) | collective-permute-done | bytes 65568 | tf_op jit(solution)/shard_map/ppermute | solution.py:26
  27.8 2.4 %collective-permute-done.8 = bf16[128,256]{1,0:T(8,128)(2,1)S(1)} collective-permute-done((bf16[128,256]{1,0:T(8,128)(2,1)S(1)}, bf16[128,256]{1,0:T(8,128)(2,1)S(1)}, u32[]{:S(2)}, u32[]{:S(2)}) %collective-permute-start.8) | collective-permute-done | bytes 65568 | tf_op jit(solution)/shard_map/ppermute | solution.py:26
  30.2 1.2 %collective-permute-done.9 = bf16[128,256]{1,0:T(8,128)(2,1)S(1)} collective-permute-done((bf16[128,256]{1,0:T(8,128)(2,1)S(1)}, bf16[128,256]{1,0:T(8,128)(2,1)S(1)}, u32[]{:S(2)}, u32[]{:S(2)}) %collective-permute-start.9) | collective-permute-done | bytes 65568 | tf_op jit(solution)/shard_map/ppermute | solution.py:26
  31.4 1.4 %collective-permute-start.10 = (bf16[128,256]{1,0:T(8,128)(2,1)S(1)}, bf16[128,256]{1,0:T(8,128)(2,1)S(1)}, u32[]{:S(2)}, u32[]{:S(2)}) collective-permute-start(bf16[128,256]{1,0:T(8,128)(2,1)S(1)} %add_convert_fusion.1), channel_id=1, source_target_pairs={{0,24},{2,26},{4,28},{6,30},{8,16},{10,18},{12,20},{14,22},{16,8},... | collective-permute-start | bytes 196616 | tf_op jit(solution)/shard_map/ppermute | solution.py:26
  33.0 2.8 %collective-permute-start.12 = (bf16[128,256]{1,0:T(8,128)(2,1)S(1)}, bf16[128,256]{1,0:T(8,128)(2,1)S(1)}, u32[]{:S(2)}, u32[]{:S(2)}) collective-permute-start(bf16[128,256]{1,0:T(8,128)(2,1)S(1)} %add_convert_fusion.1), channel_id=1, source_target_pairs={{0,16},{2,18},{4,20},{6,22},{8,24},{10,26},{12,28},{14,30},{16,0},... | collective-permute-start | bytes 196616 | tf_op jit(solution)/shard_map/ppermute | solution.py:26
  35.8 1.8 %collective-permute-done.10 = bf16[128,256]{1,0:T(8,128)(2,1)S(1)} collective-permute-done((bf16[128,256]{1,0:T(8,128)(2,1)S(1)}, bf16[128,256]{1,0:T(8,128)(2,1)S(1)}, u32[]{:S(2)}, u32[]{:S(2)}) %collective-permute-start.10) | collective-permute-done | bytes 65568 | tf_op jit(solution)/shard_map/ppermute | solution.py:26
  37.8 1.0 %collective-permute-done.12 = bf16[128,256]{1,0:T(8,128)(2,1)S(1)} collective-permute-done((bf16[128,256]{1,0:T(8,128)(2,1)S(1)}, bf16[128,256]{1,0:T(8,128)(2,1)S(1)}, u32[]{:S(2)}, u32[]{:S(2)}) %collective-permute-start.12) | collective-permute-done | bytes 65568 | tf_op jit(solution)/shard_map/ppermute | solution.py:26
  38.8 2.0 %collective-permute-start.13 = (bf16[128,256]{1,0:T(8,128)(2,1)S(1)}, bf16[128,256]{1,0:T(8,128)(2,1)S(1)}, u32[]{:S(2)}, u32[]{:S(2)}) collective-permute-start(bf16[128,256]{1,0:T(8,128)(2,1)S(1)} %add_convert_fusion.refs_3_), channel_id=1, source_target_pairs={{0,6},{2,4},{4,2},{6,0},{8,14},{10,12},{12,10},{14,8},{16,22},{18,... | collective-permute-start | bytes 196616 | tf_op jit(solution)/shard_map/ppermute | solution.py:26
  40.8 0.4 collective-permute-start.14
  41.3 1.1 %collective-permute-start.15 = (bf16[128,256]{1,0:T(8,128)(2,1)S(1)}, bf16[128,256]{1,0:T(8,128)(2,1)S(1)}, u32[]{:S(2)}, u32[]{:S(2)}) collective-permute-start(bf16[128,256]{1,0:T(8,128)(2,1)S(1)} %add_convert_fusion.refs_3_), channel_id=1, source_target_pairs={{0,2},{2,0},{4,6},{6,4},{8,10},{10,8},{12,14},{14,12},{16,18},{18,... | collective-permute-start | bytes 196616 | tf_op jit(solution)/shard_map/ppermute | solution.py:26
  42.4 0.7 %copy.6 = f32[512,128]{1,0:T(8,128)} copy(f32[512,128]{1,0:T(8,128)S(1)} %get-tuple-element.22) | data formatting | bytes 524288
  43.1 1.0 %collective-permute-done.13.refs_0_ = bf16[128,256]{1,0:T(8,128)(2,1)S(1)} collective-permute-done((bf16[128,256]{1,0:T(8,128)(2,1)S(1)}, bf16[128,256]{1,0:T(8,128)(2,1)S(1)}, u32[]{:S(2)}, u32[]{:S(2)}) %collective-permute-start.13) | collective-permute-done | bytes 65568 | tf_op jit(solution)/shard_map/ppermute | solution.py:26
  44.1 1.0 %collective-permute-done.14.refs_1_ = bf16[128,256]{1,0:T(8,128)(2,1)S(1)} collective-permute-done((bf16[128,256]{1,0:T(8,128)(2,1)S(1)}, bf16[128,256]{1,0:T(8,128)(2,1)S(1)}, u32[]{:S(2)}, u32[]{:S(2)}) %collective-permute-start.14) | collective-permute-done | bytes 65568 | tf_op jit(solution)/shard_map/ppermute | solution.py:26
  45.1 0.4 collective-permute-done.15.refs_2_
  45.5 0.9 %join.1 = f32[1024,128]{1,0:T(8,128)} custom-call(s32[1]{0:T(128)} %bitcast.8.digit_ref, bf16[128,256]{1,0:T(8,128)(2,1)S(1)} %collective-permute-done.13.refs_0_, bf16[128,256]{1,0:T(8,128)(2,1)S(1)} %collective-permute-done.14.refs_1_, bf16[128,256]{1,0:T(8,128)(2,1)S(1)} %collective-permute-done.15.refs_2_, bf16[128,256]{1,0:T(8,128)(2,1)S(1)} %add_convert_fusion.refs_3_), custom_call_target="tpu_custom_call" | custom-call | tf_op jit(solution)/shard_map/join/pallas_call | solution.py:309
  (13 shorter events, 1.6 us)
Async XLA Ops:
  3.1 8.8 %collective-permute-start.2 = (bf16[528,128]{1,0:T(8,128)(2,1)S(1)}, bf16[528,128]{1,0:T(8,128)(2,1)S(1)}, u32[]{:S(2)}, u32[]{:S(2)}) collective-permute-start(bf16[528,128]{1,0:T(8,128)(2,1)S(1)} %get-tuple-element.12.refs_2_), channel_id=1, source_target_pairs={{0,1},{1,0},{2,3},{3,2},{4,5},{5,4},{6,7},{7,6},{8,9},{9,8},{10,11... | collective-permute-start | bytes 405512 | tf_op jit(solution)/shard_map/ppermute | solution.py:21
  3.6 9.2 %collective-permute-start.4 = (bf16[528,128]{1,0:T(8,128)(2,1)S(1)}, bf16[528,128]{1,0:T(8,128)(2,1)S(1)}, u32[]{:S(2)}, u32[]{:S(2)}) collective-permute-start(bf16[528,128]{1,0:T(8,128)(2,1)S(1)} %get-tuple-element.12.refs_2_), channel_id=1, source_target_pairs={{0,24},{1,25},{2,26},{3,27},{4,28},{5,29},{6,30},{7,31},{8,16},{9,... | collective-permute-start | bytes 405512 | tf_op jit(solution)/shard_map/ppermute | solution.py:36
  8.3 9.3 %collective-permute-start.3 = (bf16[528,128]{1,0:T(8,128)(2,1)S(1)}, bf16[528,128]{1,0:T(8,128)(2,1)S(1)}, u32[]{:S(2)}, u32[]{:S(2)}) collective-permute-start(bf16[528,128]{1,0:T(8,128)(2,1)S(1)} %get-tuple-element.12.refs_2_), channel_id=1, source_target_pairs={{0,31},{1,30},{2,5},{3,4},{4,3},{5,2},{6,9},{7,8},{8,7},{9,6},{10,... | collective-permute-start | bytes 405512 | tf_op jit(solution)/shard_map/ppermute | solution.py:36
  10.2 8.4 %collective-permute-start = (bf16[528,128]{1,0:T(8,128)(2,1)S(1)}, bf16[528,128]{1,0:T(8,128)(2,1)S(1)}, u32[]{:S(2)}, u32[]{:S(2)}) collective-permute-start(bf16[528,128]{1,0:T(8,128)(2,1)S(1)} %get-tuple-element.12.refs_2_), channel_id=1, source_target_pairs={{0,9},{1,8},{2,11},{3,10},{4,13},{5,12},{6,15},{7,14},{8,1},{9,0},... | collective-permute-start | bytes 405512 | tf_op jit(solution)/shard_map/ppermute | solution.py:36
  11.9 6.7 %collective-permute-start.1 = (bf16[528,128]{1,0:T(8,128)(2,1)S(1)}, bf16[528,128]{1,0:T(8,128)(2,1)S(1)}, u32[]{:S(2)}, u32[]{:S(2)}) collective-permute-start(bf16[528,128]{1,0:T(8,128)(2,1)S(1)} %get-tuple-element.12.refs_2_), channel_id=1, source_target_pairs={{0,3},{1,2},{2,1},{3,0},{4,7},{5,6},{6,5},{7,4},{8,11},{9,10},{10,... | collective-permute-start | bytes 405512 | tf_op jit(solution)/shard_map/ppermute | solution.py:36
  19.5 1.6 %collective-permute-start.5 = (f32[512,128]{1,0:T(8,128)S(1)}, f32[512,128]{1,0:T(8,128)S(1)}, u32[]{:S(2)}, u32[]{:S(2)}) collective-permute-start(f32[512,128]{1,0:T(8,128)S(1)} %bitcast.9), channel_id=1, source_target_pairs={{0,1},{1,0},{2,3},{3,2},{4,5},{5,4},{6,7},{7,6},{8,9},{9,8},{10,11... | collective-permute-start | bytes 786440 | tf_op jit(solution)/shard_map/ppermute | solution.py:21
  21.7 1.6 %collective-permute-start.6 = (bf16[128,1024]{1,0:T(8,128)(2,1)S(1)}, bf16[128,1024]{1,0:T(8,128)(2,1)S(1)}, u32[]{:S(2)}, u32[]{:S(2)}) collective-permute-start(bf16[128,1024]{1,0:T(8,128)(2,1)S(1)} %get-tuple-element.17), channel_id=1, source_target_pairs={{0,1},{1,0},{2,3},{3,2},{4,5},{5,4},{6,7},{7,6},{8,9},{9,8},{10,11... | collective-permute-start | bytes 786440 | tf_op jit(solution)/shard_map/ppermute | solution.py:21
  23.4 4.3 %collective-permute-start.7 = (bf16[128,256]{1,0:T(8,128)(2,1)S(1)}, bf16[128,256]{1,0:T(8,128)(2,1)S(1)}, u32[]{:S(2)}, u32[]{:S(2)}) collective-permute-start(bf16[128,256]{1,0:T(8,128)(2,1)S(1)} %get-tuple-element.19), channel_id=1, source_target_pairs={{0,2},{2,0},{4,6},{6,4},{8,10},{10,8},{12,14},{14,12},{16,18},{18,... | collective-permute-start | bytes 196616 | tf_op jit(solution)/shard_map/ppermute | solution.py:26
  25.2 5.0 %collective-permute-start.8 = (bf16[128,256]{1,0:T(8,128)(2,1)S(1)}, bf16[128,256]{1,0:T(8,128)(2,1)S(1)}, u32[]{:S(2)}, u32[]{:S(2)}) collective-permute-start(bf16[128,256]{1,0:T(8,128)(2,1)S(1)} %get-tuple-element.20), channel_id=1, source_target_pairs={{0,4},{2,6},{4,0},{6,2},{8,12},{10,14},{12,8},{14,10},{16,20},{18,... | collective-permute-start | bytes 196616 | tf_op jit(solution)/shard_map/ppermute | solution.py:26
  26.2 5.2 %collective-permute-start.9 = (bf16[128,256]{1,0:T(8,128)(2,1)S(1)}, bf16[128,256]{1,0:T(8,128)(2,1)S(1)}, u32[]{:S(2)}, u32[]{:S(2)}) collective-permute-start(bf16[128,256]{1,0:T(8,128)(2,1)S(1)} %get-tuple-element.21), channel_id=1, source_target_pairs={{0,6},{2,4},{4,2},{6,0},{8,14},{10,12},{12,10},{14,8},{16,22},{18,... | collective-permute-start | bytes 196616 | tf_op jit(solution)/shard_map/ppermute | solution.py:26
  31.4 6.2 %collective-permute-start.10 = (bf16[128,256]{1,0:T(8,128)(2,1)S(1)}, bf16[128,256]{1,0:T(8,128)(2,1)S(1)}, u32[]{:S(2)}, u32[]{:S(2)}) collective-permute-start(bf16[128,256]{1,0:T(8,128)(2,1)S(1)} %add_convert_fusion.1), channel_id=1, source_target_pairs={{0,24},{2,26},{4,28},{6,30},{8,16},{10,18},{12,20},{14,22},{16,8},... | collective-permute-start | bytes 196616 | tf_op jit(solution)/shard_map/ppermute | solution.py:26
  32.8 5.0 %collective-permute-start.11 = (bf16[128,256]{1,0:T(8,128)(2,1)S(1)}, bf16[128,256]{1,0:T(8,128)(2,1)S(1)}, u32[]{:S(2)}, u32[]{:S(2)}) collective-permute-start(bf16[128,256]{1,0:T(8,128)(2,1)S(1)} %add_convert_fusion.1), channel_id=1, source_target_pairs={{0,8},{2,10},{4,12},{6,14},{8,0},{10,2},{12,4},{14,6},{16,24},{18,... | collective-permute-start | bytes 196616 | tf_op jit(solution)/shard_map/ppermute | solution.py:26
  33.0 5.7 %collective-permute-start.12 = (bf16[128,256]{1,0:T(8,128)(2,1)S(1)}, bf16[128,256]{1,0:T(8,128)(2,1)S(1)}, u32[]{:S(2)}, u32[]{:S(2)}) collective-permute-start(bf16[128,256]{1,0:T(8,128)(2,1)S(1)} %add_convert_fusion.1), channel_id=1, source_target_pairs={{0,16},{2,18},{4,20},{6,22},{8,24},{10,26},{12,28},{14,30},{16,0},... | collective-permute-start | bytes 196616 | tf_op jit(solution)/shard_map/ppermute | solution.py:26
  38.8 5.2 %collective-permute-start.13 = (bf16[128,256]{1,0:T(8,128)(2,1)S(1)}, bf16[128,256]{1,0:T(8,128)(2,1)S(1)}, u32[]{:S(2)}, u32[]{:S(2)}) collective-permute-start(bf16[128,256]{1,0:T(8,128)(2,1)S(1)} %add_convert_fusion.refs_3_), channel_id=1, source_target_pairs={{0,6},{2,4},{4,2},{6,0},{8,14},{10,12},{12,10},{14,8},{16,22},{18,... | collective-permute-start | bytes 196616 | tf_op jit(solution)/shard_map/ppermute | solution.py:26
  40.8 4.3 %collective-permute-start.14 = (bf16[128,256]{1,0:T(8,128)(2,1)S(1)}, bf16[128,256]{1,0:T(8,128)(2,1)S(1)}, u32[]{:S(2)}, u32[]{:S(2)}) collective-permute-start(bf16[128,256]{1,0:T(8,128)(2,1)S(1)} %add_convert_fusion.refs_3_), channel_id=1, source_target_pairs={{0,4},{2,6},{4,0},{6,2},{8,12},{10,14},{12,8},{14,10},{16,20},{18,... | collective-permute-start | bytes 196616 | tf_op jit(solution)/shard_map/ppermute | solution.py:26
  41.3 4.3 %collective-permute-start.15 = (bf16[128,256]{1,0:T(8,128)(2,1)S(1)}, bf16[128,256]{1,0:T(8,128)(2,1)S(1)}, u32[]{:S(2)}, u32[]{:S(2)}) collective-permute-start(bf16[128,256]{1,0:T(8,128)(2,1)S(1)} %add_convert_fusion.refs_3_), channel_id=1, source_target_pairs={{0,2},{2,0},{4,6},{6,4},{8,10},{10,8},{12,14},{14,12},{16,18},{18,... | collective-permute-start | bytes 196616 | tf_op jit(solution)/shard_map/ppermute | solution.py:26
